TPU v7x, 128 devices: a whole 4x4x4 slice. The times are simulated.
128 devices in a mesh: rep: 8 (over z, core), pipe: 8 (over y_lo, x), tp: 2 (over y_hi).
Axes of the slice: x: 4, y: 4 (y_hi: 2, y_lo: 2; y = y_hi * 2 + y_lo), z: 4, core: 2. Of those that a mesh axis runs over, the one named last changes fastest.
Arguments:
- fwd_in: bfloat16 [8, 8, 256, 3072], P('rep', 'pipe', None, 'tp'), may hold values from -6 to 6
- bwd_in: bfloat16 [8, 8, 256, 3072], P('rep', 'pipe', None, 'tp'), may hold values from -6 to 6
- bwd_grad: bfloat16 [8, 8, 256, 3072], P('rep', 'pipe', None, 'tp'), may hold values from -18 to 18
- seg_fwd: int32 [8, 8, 256], P('rep', 'pipe'), may hold values from 0 to 3, never falling along the last dimension, each value on 1 to 128 neighbouring positions
- seg_bwd: int32 [8, 8, 256], P('rep', 'pipe'), may hold values from 0 to 3, never falling along the last dimension, each value on 1 to 128 neighbouring positions
- w_query: bfloat16 [8, 8, 3072, 3072], P('rep', 'pipe', None, 'tp'), may hold values from -6 to 6
- w_key: bfloat16 [8, 8, 3072, 128], P('rep', 'pipe'), may hold values from -60 to 60
- gain: bfloat16 [8, 8, 3072], P('rep', 'pipe', 'tp'), may hold values from 0.5 to 1.5
- gossip_exp: int32 [8], P('pipe'), may hold values from 0 to 2
Outputs:
- next_input: bfloat16 [8, 8, 256, 3072], P('rep', 'pipe', None, 'tp')
- prev_grad: bfloat16 [8, 8, 256, 3072], P('rep', 'pipe', None, 'tp')
- w_query_out: bfloat16 [8, 8, 3072, 3072], P('rep', 'pipe', None, 'tp')
- w_key_out: bfloat16 [8, 8, 3072, 128], P('rep', 'pipe')
- gain_out: bfloat16 [8, 8, 3072], P('rep', 'pipe', 'tp')
Inputs may be any that keep to these rules, and one draw needn't show every extreme that they name: The partner of replica r at section p is r XOR 2^k with k = gossip_exp[p]. `seg_fwd`: along each section's rows the caption ids never fall; each caption has 1 to 128 tokens. `seg_bwd`: along each section's rows the caption ids never fall; each caption has 1 to 128 tokens.
All inputs are finite; a program needn't handle non-finite values.
Results may differ from a plain program's by a relative error of at most 0.015.
The roundings to bfloat16 on the way count: a program that leaves them out, or rounds other values in their place, can miss the bound.
Values may be sent and summed in bfloat16 or wider, within the bound.
A program may use at most 192 MiB of HBM per device.

v0:
```python
import jax
import jax.numpy as jnp
from jax import lax
from jax.experimental import pallas as pl
from jax.experimental.pallas import tpu as pltpu
from jax.sharding import PartitionSpec as P


HEAD = 128


LN_EPS = 1e-05
STEP_EPS = 1e-06
LEARN_RATE = 0.2
MASK_FILL = -1e30
CHUNK_SHARES = (2, 3, 1)
BLOCK = 256
STRIP = 512


def from_behind(shard, axis, by):
    length = lax.axis_size(axis)
    return lax.ppermute(shard, axis, [(i, (i + by) % length) for i in range(length)])


def flipped(block, axis, bit):
    return lax.ppermute(block, axis, [(i, i ^ 1 << bit) for i in range(lax.axis_size(axis))])


def in_order(own, other, low, axis):
    return jnp.where(
        low, jnp.concatenate([own, other], axis), jnp.concatenate([other, own], axis)
    )


def of_everyone(shard, axis):
    copies = jnp.broadcast_to(shard, (lax.axis_size(axis), *shard.shape))
    return jnp.sum(lax.all_to_all(copies, axis, split_axis=0, concat_axis=0, tiled=True), axis=0)


def chunk_cuts(rows):
    whole, edges = sum(CHUNK_SHARES), [0]
    for share in CHUNK_SHARES:
        edges.append(edges[-1] + rows * share // whole)
    return list(zip(edges[:-1], edges[1:]))


def relay_kernel(case_ref, up, down, above_in, below_in, above, below, held, sem):
    def carry(source, target):
        for one, other in ((source, held), (held, target)):
            copy = pltpu.make_async_copy(one, other, sem)
            copy.start()
            copy.wait()

    @pl.when(case_ref[0] == 1)
    def _():
        carry(down, above)

    @pl.when(case_ref[0] == 2)
    def _():
        carry(up, below)


def relayed(case, up, down, above, below):
    anywhere = pl.BlockSpec(memory_space=pl.ANY)
    return pl.pallas_call(
        relay_kernel,
        in_specs=[pl.BlockSpec(memory_space=pltpu.SMEM)] + [anywhere] * 4,
        out_specs=[anywhere] * 2,
        out_shape=[jax.ShapeDtypeStruct(up.shape, up.dtype)] * 2,
        input_output_aliases={3: 0, 4: 1},
        scratch_shapes=[pltpu.VMEM(up.shape, up.dtype), pltpu.SemaphoreType.DMA],
        cost_estimate=pl.CostEstimate(flops=0, bytes_accessed=up.size, transcendentals=0),
        compiler_params=pltpu.CompilerParams(vmem_limit_bytes=8 << 20),
    )(case.reshape(1), up, down, above, below)


class Gossip:
    def __init__(self, exponent):
        self.exponent = exponent
        odd = (lax.axis_index("rep") // 2) % 2
        self.case = jnp.where(exponent == 2, 3, jnp.where(exponent == 1, 1 + odd, 0))

    def first(self, up, down):
        return up, down, from_behind(up, "rep", 2), from_behind(down, "rep", -2)

    def second(self, state):
        above, below = relayed(self.case, *state)
        return above, below, from_behind(above, "rep", 2), from_behind(below, "rep", -2)

    def small(self, block):
        half = block.shape[0] // 2
        up, down, block = lax.optimization_barrier((block[:half], block[half:], block))
        state = self.first(up, down)
        above, below, from_up, from_down = self.second(state)
        near = flipped(block, "rep", 0)
        case = self.case

        def pick(a, b, c, d):
            return jnp.where(case == 0, a, jnp.where(case == 1, b, jnp.where(case == 2, c, d)))

        return jnp.concatenate(
            [
                pick(near[:half], from_down, above, from_up),
                pick(near[half:], below, from_up, from_down),
            ],
            axis=0,
        )

    def tiny(self, block):
        results = [flipped(block, "rep", bit) for bit in range(3)]
        return jnp.where(
            self.exponent == 0, results[0], jnp.where(self.exponent == 1, results[1], results[2])
        )


def normalize(rows, gain_full):
    values = rows.astype(jnp.float32)
    centred = values - jnp.mean(values, axis=-1, keepdims=True)
    inv_std = lax.rsqrt(jnp.mean(centred * centred, axis=-1, keepdims=True) + LN_EPS)
    scaled = centred * inv_std
    normed = (scaled * gain_full.astype(jnp.float32)).astype(jnp.bfloat16)
    return (values, scaled, inv_std, normed)


def projected(normed, weight):
    in_scale = normed.shape[1] ** (-0.5)
    product = jnp.dot(normed, weight, preferred_element_type=jnp.float32)
    return (product * in_scale).astype(jnp.bfloat16)


def dot(a, b, over):
    return lax.dot_general(a, b, (over, ((), ())), preferred_element_type=jnp.float32)


ROWS_COLS, LAST_LAST, FIRST_FIRST = ((1,), (0,)), ((1,), (1,)), ((0,), (0,))


def head_probs(queries, keys, tall, wide):
    scores = dot(queries, keys, LAST_LAST) * HEAD ** (-0.5)
    scores = jnp.where(tall == wide, scores, MASK_FILL)
    peak = jnp.max(scores, axis=-1, keepdims=True)
    expo = jnp.exp(scores - peak)
    return (expo / jnp.sum(expo, axis=-1, keepdims=True)).astype(jnp.bfloat16)


def onward_kernel(queries, keys, values, rows, tall, wide, out):
    probs = head_probs(queries[...], keys[...], tall[...], wide[...])
    mixed = dot(probs, values[...], ROWS_COLS)
    out[...] = (rows[...].astype(jnp.float32) + mixed).astype(jnp.bfloat16)


def back_kernel(queries, keys, values, grads, tall, wide, query_grad, value_grad, key_part, total):
    head = pl.program_id(0)

    @pl.when(head == 0)
    def _():
        total[...] = jnp.zeros_like(total)

    query, key, grad = queries[...], keys[...], grads[...]
    probs = head_probs(query, key, tall[...], wide[...])
    prob_f = probs.astype(jnp.float32)
    value_grad[...] = dot(probs, grad, FIRST_FIRST)
    prob_grad = dot(grad, values[...], LAST_LAST)
    inner = jnp.sum(prob_grad * prob_f, axis=-1, keepdims=True)
    score_grad = (prob_f * (prob_grad - inner) * HEAD ** (-0.5)).astype(jnp.bfloat16)
    query_grad[...] = dot(score_grad, key, ROWS_COLS).astype(jnp.bfloat16)
    total[...] += dot(score_grad, query, FIRST_FIRST)

    @pl.when(head == pl.num_programs(0) - 1)
    def _():
        key_part[...] = total[...].astype(jnp.bfloat16)


def per_head(kernel, caption, queries, keys, extras, outs, products):
    count, width = queries.shape
    heads = width // HEAD
    by_head = pl.BlockSpec((count, HEAD), lambda h: (0, h))
    fixed = pl.BlockSpec((count, HEAD), lambda h: (0, 0))
    specs = [by_head, fixed] + [by_head] * len(extras)
    specs += [pl.BlockSpec((count, 1), lambda h: (0, 0)), pl.BlockSpec((1, count), lambda h: (0, 0))]
    backward = len(outs) > 1
    return pl.pallas_call(
        kernel,
        grid=(heads,),
        in_specs=specs,
        out_specs=[by_head if shape[1] == width else fixed for shape, kind in outs],
        out_shape=[jax.ShapeDtypeStruct(shape, kind) for shape, kind in outs],
        scratch_shapes=[pltpu.VMEM((count, HEAD), jnp.float32)] if backward else [],
        cost_estimate=pl.CostEstimate(
            flops=2 * products * heads * count * count * HEAD,
            bytes_accessed=2 * (len(extras) + 1 + len(outs)) * count * width,
            transcendentals=heads * count * count,
        ),
        compiler_params=pltpu.CompilerParams(vmem_limit_bytes=24 << 20),
    )(queries, keys, *extras, caption[:, None], caption[None, :])


def updated(weight, step):
    return (weight.astype(jnp.float32) - step.astype(jnp.float32)).astype(jnp.bfloat16)


def halves(mine, theirs):
    return ((mine.astype(jnp.float32) + theirs.astype(jnp.float32)) * 0.5).astype(jnp.bfloat16)


def average_kernel(
    case_ref, scales, weights, slope, slope_other, grad, grad_other, near, above, below, from_up,
    from_down, *rest,
):
    out_ref = rest[-1]
    columns = weights.shape[1]
    in_scale = (2 * columns) ** (-0.5)
    flipped_own, flipped_other = slope[...].T, slope_other[...].T
    chosen = source_of(pl.program_id(0), case_ref[0])

    def strip(number, carry):
        cols = pl.ds(pl.multiple_of(number * STRIP, STRIP), STRIP)

        def step(rows, grads, scale):
            gradient = dot(rows, grads[:, cols], ROWS_COLS)
            return (gradient * (LEARN_RATE * in_scale * scale)).astype(jnp.bfloat16)

        mine = weights[:, cols] - step(flipped_own, grad, scales[0])
        theirs = step(flipped_other, grad_other, scales[1])
        partner = near[:, cols]
        for source, weight in enumerate((above, below, from_up, from_down), 1):
            partner = jnp.where(chosen == source, weight[:, cols], partner)
        out_ref[:, cols] = (mine + (partner - theirs)) * 0.5
        return carry

    lax.fori_loop(0, columns // STRIP, strip, 0)


def squares_kernel(slope, grad, key_grad, out, total):
    step = pl.program_id(0)

    @pl.when(step == 0)
    def _():
        total[...] = jnp.zeros_like(total)

    rows = slope[...].T
    columns = grad.shape[1]

    def added(grads):
        gradient = dot(rows, grads, ROWS_COLS)
        return jnp.sum((gradient * gradient).reshape(-1, 8, gradient.shape[1]), axis=0)

    def strip(number, carry):
        cols = pl.ds(pl.multiple_of(number * STRIP, STRIP), STRIP)
        total[...] += added(grad[:, cols])
        return carry

    lax.fori_loop(0, columns // STRIP, strip, 0)
    total[:, :HEAD] += added(key_grad[...]) * 0.5

    @pl.when(step == pl.num_programs(0) - 1)
    def _():
        out[...] = jnp.sum(total[...], keepdims=True)


def gradient_squares(slope, grad, key_grad):
    depth, rows = slope.shape
    in_scale = rows ** (-0.5)
    size = rows * (grad.shape[1] + HEAD) * depth
    block = rows // 3
    squares = pl.pallas_call(
        squares_kernel,
        grid=(rows // block,),
        in_specs=[
            pl.BlockSpec((depth, block), lambda i: (0, i)),
            pl.BlockSpec(grad.shape, lambda i: (0, 0)),
            pl.BlockSpec(key_grad.shape, lambda i: (0, 0)),
        ],
        out_specs=pl.BlockSpec((1, 1), lambda i: (0, 0)),
        out_shape=jax.ShapeDtypeStruct((1, 1), jnp.float32),
        scratch_shapes=[pltpu.VMEM((8, STRIP), jnp.float32)],
        cost_estimate=pl.CostEstimate(
            flops=2 * size, bytes_accessed=2 * slope.size + 2 * grad.size, transcendentals=0
        ),
        compiler_params=pltpu.CompilerParams(vmem_limit_bytes=16 << 20),
    )(slope, grad, key_grad)
    return squares[0, 0] * (in_scale * in_scale)


def source_of(half, case):
    up = jnp.where(case == 1, 4, jnp.where(case == 2, 1, 3))
    down = jnp.where(case == 1, 2, jnp.where(case == 2, 3, 4))
    return jnp.where(case == 0, 0, jnp.where(half == 0, up, down))


def averaged_chunk(case, scales, weights, slopes, grads, near, chunk, cut, out):
    rows, columns = weights.shape
    first, blocks = cut[0] // BLOCK, (cut[1] - cut[0]) // BLOCK
    stride = rows // (2 * BLOCK)

    def whole(half, i, case_ref):
        return (half * stride + first + i, 0)

    def near_map(half, i, case_ref):
        used = source_of(half, case_ref[0]) == 0
        return (jnp.where(used, half * stride + first + i, 0), 0)

    def part_map(number):
        def index(half, i, case_ref):
            return (jnp.where(source_of(half, case_ref[0]) == number, i, 0), 0)

        return index

    block = (BLOCK, columns)
    depth = slopes[0].shape[0]
    in_specs = [pl.BlockSpec(memory_space=pltpu.SMEM), pl.BlockSpec(block, whole)]
    across = pl.BlockSpec((depth, BLOCK), lambda *at: whole(*at)[::-1])
    in_specs += [across] * 2
    in_specs += [pl.BlockSpec((depth, columns), lambda half, i, case_ref: (0, 0))] * 2
    in_specs += [pl.BlockSpec(block, near_map)]
    in_specs += [pl.BlockSpec(block, part_map(number)) for number in range(1, 5)]
    operands = [case.reshape(1), scales, weights, *slopes, *grads, near, *chunk]
    aliases = {}
    if out is not None:
        in_specs.append(pl.BlockSpec(memory_space=pl.ANY))
        aliases = {len(operands): 0}
        operands.append(out)
    size = 2 * blocks * BLOCK * columns
    return pl.pallas_call(
        average_kernel,
        grid_spec=pltpu.PrefetchScalarGridSpec(
            num_scalar_prefetch=1,
            grid=(2, blocks),
            in_specs=in_specs,
            out_specs=pl.BlockSpec(block, whole),
        ),
        out_shape=jax.ShapeDtypeStruct(weights.shape, weights.dtype),
        input_output_aliases=aliases,
        cost_estimate=pl.CostEstimate(
            flops=4 * size * depth, bytes_accessed=6 * size, transcendentals=0
        ),
        compiler_params=pltpu.CompilerParams(vmem_limit_bytes=40 << 20),
    )(*operands)


def settled_kernel(a_ref, b_ref, c_ref, d_ref):
    c_ref[...] = a_ref[...]
    d_ref[...] = b_ref[...]


def settled(a, b):
    block = pl.BlockSpec((64, a.shape[1]), lambda i: (i, 0))
    return pl.pallas_call(
        settled_kernel,
        grid=(a.shape[0] // 64,),
        in_specs=[block, block],
        out_specs=[block, block],
        out_shape=[jax.ShapeDtypeStruct(x.shape, x.dtype) for x in (a, b)],
        cost_estimate=pl.CostEstimate(flops=0, bytes_accessed=8 * a.size, transcendentals=0),
        compiler_params=pltpu.CompilerParams(vmem_limit_bytes=8 << 20),
    )(a, b)


def section(fwd_in, bwd_in, bwd_grad, seg_fwd, seg_bwd, w_query, w_key, gain, gossip_exp):
    query_weight = w_query[0, 0]
    key_weight = w_key[0, 0]
    gain_local = gain[0, 0]
    fwd_rows = fwd_in[0, 0]
    bwd_rows = bwd_in[0, 0]
    grad_rows = bwd_grad[0, 0]
    count, local_width = fwd_rows.shape
    pipe_count = lax.axis_size("pipe")
    tp_index = lax.axis_index("tp")
    low = tp_index == 0
    offset = tp_index * local_width
    gossip = Gossip(gossip_exp[0])

    width = query_weight.shape[0]
    in_scale = width ** (-0.5)
    cuts = chunk_cuts(width // 2)
    parts = [
        [query_weight[base + a : base + b] for a, b in cuts] for base in (0, width // 2)
    ]
    sent = []
    for up, down in zip(*parts):
        sent.append(gossip.first(up, down))
    query_near = flipped(query_weight, "rep", 0)

    beside = jnp.broadcast_to(gain_local[None], (16, local_width))
    other = flipped(jnp.concatenate([bwd_rows, beside], axis=0), "tp", 0)
    bwd_full = in_order(bwd_rows, other[:count], low, 1)
    gain_full = in_order(gain_local, other[count], low, 0)

    _, scaled_b, inv_b, normed_b = normalize(bwd_full, gain_full)
    own_values_b = lax.dynamic_slice_in_dim(normed_b, offset, local_width, 1)
    key_rows = lax.dynamic_slice_in_dim(key_weight, offset, local_width, 0)
    early = gossip.small(
        jnp.concatenate([own_values_b, key_rows.reshape(HEAD, local_width)], axis=0)
    )
    early_other = flipped(early, "tp", 0)
    normed_partner = in_order(early[:count], early_other[:count], low, 1)
    key_partner = in_order(
        early[count:].reshape(local_width, HEAD),
        early_other[count:].reshape(local_width, HEAD),
        low,
        0,
    )

    queries = projected(normed_b, query_weight)
    keys = projected(normed_b, key_weight)
    query_grad, value_grad, key_part = per_head(
        back_kernel,
        seg_bwd[0, 0],
        queries,
        keys,
        (own_values_b, grad_rows),
        (
            ((count, local_width), jnp.bfloat16),
            ((count, local_width), jnp.float32),
            ((count, HEAD), jnp.bfloat16),
        ),
        5,
    )

    def tp_sum(part):
        other = flipped(part, "tp", 0)
        return (part.astype(jnp.float32) + other.astype(jnp.float32)).astype(jnp.bfloat16)

    late = gossip.small(jnp.concatenate([query_grad, key_part], axis=1))
    query_grad_partner = late[:, :local_width]
    key_grad = tp_sum(key_part)
    key_grad_partner = tp_sum(late[:, local_width:])

    contract_last = (((1,), (1,)), ((), ()))
    partial_grad = (
        lax.dot_general(query_grad, query_weight, contract_last, preferred_element_type=jnp.float32)
        * in_scale
    )
    own_part = (lax.dynamic_slice_in_dim(partial_grad, offset, local_width, 1) + value_grad).astype(
        jnp.bfloat16
    )
    other_part = lax.dynamic_slice_in_dim(
        partial_grad, local_width - offset, local_width, 1
    ).astype(jnp.bfloat16)
    from_other = flipped(other_part, "tp", 0)
    full_grad = (
        own_part.astype(jnp.float32)
        + from_other.astype(jnp.float32)
        + lax.dot_general(key_grad, key_rows, contract_last, preferred_element_type=jnp.float32)
        * in_scale
    )
    own_scaled = lax.dynamic_slice_in_dim(scaled_b, offset, local_width, 1)
    weighted = full_grad * gain_local.astype(jnp.float32)
    sums = jnp.stack([jnp.sum(weighted, axis=-1), jnp.sum(weighted * own_scaled, axis=-1)])
    means = (sums + flipped(sums, "tp", 0)) / width
    input_grad = inv_b * (weighted - means[0][:, None] - own_scaled * means[1][:, None])
    grad_gain = jnp.sum(full_grad * own_scaled, axis=0)
    back_rows = (grad_rows.astype(jnp.float32) + input_grad).astype(jnp.bfloat16)
    prev_rows = from_behind(back_rows, "pipe", -1)

    contract_first = (((0,), (0,)), ((), ()))

    def weight_grad(rows, grad):
        return (
            lax.dot_general(rows, grad, contract_first, preferred_element_type=jnp.float32)
            * in_scale
        )

    query_squares = gradient_squares(normed_b, query_grad, key_grad)
    grad_key = weight_grad(normed_b, key_grad)
    local_squares = query_squares + jnp.sum(grad_gain * grad_gain)
    fwd_other = flipped(fwd_rows, "tp", 0)
    fwd_other, local_squares = lax.optimization_barrier((fwd_other, local_squares))
    fwd_full = in_order(fwd_rows, fwd_other, low, 1)
    _, _, _, normed = normalize(fwd_full, gain_full)
    own_values = lax.dynamic_slice_in_dim(normed, offset, local_width, 1)
    queries_f = projected(normed, query_weight)
    keys_f = projected(normed, key_weight)
    (section_out,) = per_head(
        onward_kernel,
        seg_fwd[0, 0],
        queries_f,
        keys_f,
        (own_values, fwd_rows),
        (((count, local_width), jnp.bfloat16),),
        2,
    )
    next_rows = from_behind(section_out, "pipe", 1)

    total_squares = of_everyone(local_squares, ("pipe", "tp"))
    total = pipe_count * (width * width + width * HEAD + width)
    inverse = lax.rsqrt(total_squares / total + STEP_EPS)

    def step_of(gradient, scale):
        return (LEARN_RATE * gradient * scale).astype(jnp.bfloat16)

    gain_new = updated(gain_local, step_of(grad_gain, inverse))
    both = gossip.tiny(
        jnp.concatenate([gain_new.astype(jnp.float32), jnp.broadcast_to(inverse, (HEAD,))])
    )
    gain_partner = both[:local_width].astype(jnp.bfloat16)
    inverse_partner = both[local_width]
    gain_out = halves(gain_new, gain_partner)

    key_out = halves(
        updated(key_weight, step_of(grad_key, inverse)),
        updated(
            key_partner,
            step_of(weight_grad(normed_partner, key_grad_partner), inverse_partner),
        ),
    )
    later = []
    for state in sent:
        later.append(gossip.second(state))
    next_rows, prev_rows = settled(next_rows, prev_rows)
    slopes = (normed_b, normed_partner)
    query_out = None
    for i, cut in enumerate(cuts):
        query_out = averaged_chunk(
            gossip.case,
            jnp.stack([inverse, inverse_partner]),
            query_weight,
            slopes,
            (query_grad, query_grad_partner),
            query_near,
            later[i],
            cut,
            query_out,
        )
    return (
        next_rows[None, None],
        prev_rows[None, None],
        query_out[None, None],
        key_out[None, None],
        gain_out[None, None],
    )


def solution(mesh):
    return jax.shard_map(
        section,
        mesh=mesh,
        in_specs=(
            P("rep", "pipe", None, "tp"),
            P("rep", "pipe", None, "tp"),
            P("rep", "pipe", None, "tp"),
            P("rep", "pipe", None),
            P("rep", "pipe", None),
            P("rep", "pipe", None, "tp"),
            P("rep", "pipe", None, None),
            P("rep", "pipe", "tp"),
            P("pipe"),
        ),
        out_specs=(
            P("rep", "pipe", None, "tp"),
            P("rep", "pipe", None, "tp"),
            P("rep", "pipe", None, "tp"),
            P("rep", "pipe", None, None),
            P("rep", "pipe", "tp"),
        ),
        check_vma=False,
    )
```

profile of v0, /device:TPU:0, one launch (start us, length us, event | category | flops | bytes accessed | tf_op | source)
XLA Modules:
  0.0 403.0 jit_solution(11020497777986260874)
XLA Ops:
  2.6 3.4 collective-permute-start.1
  6.0 3.8 slice_bitcast_fusion.2
  11.2 5.2 %slice_bitcast_fusion = (bf16[768,1536]{1,0:T(8,128)(2,1)}, bf16[768,1536]{1,0:T(8,128)(2,1)}) fusion(bf16[1,1,3072,1536]{3,2,1,0:T(8,128)(2,1)} %param.14), kind=kLoop, calls=%fused_computation.35 | loop fusion | bytes 9437184 | tf_op jit(solution)/shard_map/slice | solution.py:378
  16.4 8.1 %collective-permute-done.1 = bf16[272,1536]{1,0:T(8,128)(2,1)S(1)} collective-permute-done((bf16[272,1536]{1,0:T(8,128)(2,1)S(1)}, bf16[272,1536]{1,0:T(8,128)(2,1)S(1)}, u32[]{:S(2)}, u32[]{:S(2)}) %collective-permute-start.1) | collective-permute-done | bytes 835616 | tf_op jit(solution)/shard_map/ppermute | solution.py:27
  25.7 2.6 multiply_convert_fusion
  29.8 2.6 fusion.22.queries
  32.5 12.7 %shard_map.128 = (bf16[256,1536]{1,0:T(8,128)(2,1)S(1)}, f32[256,1536]{1,0:T(8,128)S(1)}, bf16[256,128]{1,0:T(8,128)(2,1)S(1)}) custom-call(bf16[256,1536]{1,0:T(8,128)(2,1)S(1)} %fusion.22.queries, bf16[256,128]{1,0:T(8,128)(2,1)S(1)} %fusion.24.keys, bf16[256,1536]{1,0:T(8,128)(2,1)S(1)} %constant_dynamic-slice_fusion.3.values, ...), custom_call_target="tpu_custom_call" | custom-call | flops 1006632960 | bytes 4718592 | tf_op jit(solution)/shard_map/pallas_call | solution.py:183
  46.4 2.7 convolution_multiply_fusion
  50.3 3.2 collective-permute-start.2
  54.5 1.9 collective-permute-start.17
  57.3 1.9 collective-permute-start.11
  62.5 6.7 %collective-permute-done.17.above_in = bf16[128,1664]{1,0:T(8,128)(2,1)S(1)} collective-permute-done((bf16[128,1664]{1,0:T(8,128)(2,1)S(1)}, bf16[128,1664]{1,0:T(8,128)(2,1)S(1)}, u32[]{:S(2)}, u32[]{:S(2)}) %collective-permute-start.17) | collective-permute-done | bytes 426016 | tf_op jit(solution)/shard_map/ppermute | solution.py:23
  72.4 9.6 %collective-permute-done.18.below_in = bf16[128,1664]{1,0:T(8,128)(2,1)} collective-permute-done((bf16[128,1664]{1,0:T(8,128)(2,1)}, bf16[128,1664]{1,0:T(8,128)(2,1)}, u32[]{:S(2)}, u32[]{:S(2)}) %collective-permute-start.18) | collective-permute-done | bytes 426016 | tf_op jit(solution)/shard_map/ppermute | solution.py:23
  82.6 6.4 %shard_map.129 = f32[1,1]{1,0:T(1,128)} custom-call(bf16[256,3072]{1,0:T(8,128)(2,1)S(1)} %get-tuple-element.54.slope, bf16[256,1536]{1,0:T(8,128)(2,1)S(1)} %get-tuple-element.28.grad, bf16[256,128]{1,0:T(8,128)(2,1)S(1)} %add_convert_fusion.3.key_grad), custom_call_target="tpu_custom_call" | custom-call | flops 2617245696 | bytes 2359296 | tf_op jit(solution)/shard_map/pallas_call | solution.py:267
  90.5 2.5 collective-permute-start.23
  93.1 3.3 collective-permute-start.31
  96.4 3.1 multiply_reduce_fusion
  100.7 3.5 collective-permute-done
  104.8 6.1 %all-to-all-start = ((f32[16,1,1]{2,1,0:T(1,128)}), f32[16,1,1]{2,1,0:T(1,128)S(1)}, u32[]{:S(2)}, u32[]{:S(2)}) async-start(f32[16,1,1]{2,1,0:T(1,128)} %broadcast_in_dim.37), calls=%async_computation | async-start | bytes 16384 | tf_op jit(solution)/shard_map/all_to_all | solution.py:38
  110.9 1.8 convert_reduce_fusion
  112.7 2.0 fusion.18
  114.8 3.7 all-to-all-done
  121.0 1.8 collective-permute-start.9
  122.9 2.2 fusion.20
  125.1 16.4 %collective-permute-done.31.below_in = bf16[512,1536]{1,0:T(8,128)(2,1)} collective-permute-done((bf16[512,1536]{1,0:T(8,128)(2,1)}, bf16[512,1536]{1,0:T(8,128)(2,1)}, u32[]{:S(2)}, u32[]{:S(2)}) %collective-permute-start.31) | collective-permute-done | bytes 1572896 | tf_op jit(solution)/shard_map/ppermute | solution.py:23
  141.5 3.4 collective-permute-done.30.above_in
  145.2 1.7 collective-permute-start.8
  146.9 6.3 %fusion.23.queries = bf16[256,1536]{1,0:T(8,128)(2,1)S(1)} fusion(bf16[256,3072]{1,0:T(8,128)(2,1)S(1)} %fusion.20, bf16[1,1,3072,1536]{3,2,1,0:T(8,128)(2,1)} %param.14), kind=kOutput, calls=%fused_computation.34 | convolution fusion | flops 2416705536 | bytes 11796480 | tf_op jit(solution)/shard_map/dot_general | solution.py:128
  155.6 2.5 collective-permute-start.13
  158.8 7.4 %shard_map.130 = bf16[256,1536]{1,0:T(8,128)(2,1)S(1)} custom-call(bf16[256,1536]{1,0:T(8,128)(2,1)S(1)} %fusion.23.queries, bf16[256,128]{1,0:T(8,128)(2,1)S(1)} %fusion.25.keys, bf16[256,1536]{1,0:T(8,128)(2,1)S(1)} %constant_dynamic-slice_fusion.1.values, bf16[256,1536]{1,0:T(8,128)(2,1)S(1)} %bitcast.68, s32[256,1]{1,0:T(8,128)S(1)} %copy.31.tall, ...), custom_call_target="tpu_custom_call" | custom-call | flops 402653184 | bytes 3145728 | tf_op jit(solution)/shard_map/pallas_call | solution.py:183
  166.3 53.2 %collective-permute-done.13 = bf16[192,1536]{1,0:T(8,128)(2,1)S(1)} collective-permute-done((bf16[192,1536]{1,0:T(8,128)(2,1)}, bf16[192,1536]{1,0:T(8,128)(2,1)S(1)}, u32[]{:S(2)}, u32[]{:S(2)}) %collective-permute-start.13) | collective-permute-done | bytes 589856 | tf_op jit(solution)/shard_map/ppermute | solution.py:23
  219.6 2.0 collective-permute-start.20
  222.9 11.3 %collective-permute-done.20 = bf16[128,1664]{1,0:T(8,128)(2,1)S(1)} collective-permute-done((bf16[128,1664]{1,0:T(8,128)(2,1)S(1)}, bf16[128,1664]{1,0:T(8,128)(2,1)S(1)}, u32[]{:S(2)}, u32[]{:S(2)}) %collective-permute-start.20) | collective-permute-done | bytes 426016 | tf_op jit(solution)/shard_map/ppermute | solution.py:23
  235.8 2.7 collective-permute-start.15
  239.9 2.1 collective-permute-start.6
  242.2 2.1 collective-permute-start.34
  244.3 38.1 %collective-permute-done.34 = bf16[256,128]{1,0:T(8,128)(2,1)S(1)} collective-permute-done((bf16[256,128]{1,0:T(8,128)(2,1)S(1)}, bf16[256,128]{1,0:T(8,128)(2,1)S(1)}, u32[]{:S(2)}, u32[]{:S(2)}) %collective-permute-start.34) | collective-permute-done | bytes 65568 | tf_op jit(solution)/shard_map/ppermute | solution.py:27
  282.5 3.2 collective-permute-start.29
  287.3 3.2 collective-permute-start.33
  290.5 2.9 fusion.16
  297.2 2.2 fusion.27
  299.4 1.7 shard_map.131
  305.1 64.6 %collective-permute-done.32.from_up = bf16[512,1536]{1,0:T(8,128)(2,1)} collective-permute-done((bf16[512,1536]{1,0:T(8,128)(2,1)}, bf16[512,1536]{1,0:T(8,128)(2,1)}, u32[]{:S(2)}, u32[]{:S(2)}) %collective-permute-start.32) | collective-permute-done | bytes 1572896 | tf_op jit(solution)/shard_map/ppermute | solution.py:23
  369.7 3.2 collective-permute-start.25
  373.0 4.8 %fusion.17 = bf16[1,1,3072,128]{3,2,1,0:T(8,128)(2,1)} fusion(f32[3072,128]{1,0:T(8,128)S(1)} %copy-done.40, bf16[1536,128]{1,0:T(8,128)(2,1)S(1)} %copy-done.43, bf16[1536,128]{1,0:T(8,128)(2,1)S(1)} %copy-done.42, f32[]{:T(128)} %bitcast.29, pred[]{:T(512)S(6)} %eq.42, bf16[256,128]{1,0:T(8,128)(2,1)S(1)} %copy-done.47, ...), kind=kOutput, calls=%fused_computation.24 | convolution fusion | flops 216006656 | bytes 4849669 | tf_op jit(solution)/shard_map/dot_general | solution.py:461
  377.7 8.6 %shard_map.137.rest_0_ = bf16[3072,1536]{1,0:T(8,128)(2,1)} custom-call(s32[1]{0:T(128)} %bitcast.19.case_ref, f32[2]{0:T(128)S(1)} %pad_maximum_fusion.5.scales, bf16[3072,1536]{1,0:T(8,128)(2,1)} %bitcast.75, bf16[256,3072]{1,0:T(8,128)(2,1)S(1)} %get-tuple-element.54.slope, bf16[256,3072]{1,0:T(8,128)(2,1)S(1)} %maximum_select_fusion.2.slope_other, ...), custom_call_target="tpu_custom_call" | custom-call | flops 1610612736 | bytes 9437184 | tf_op jit(solution)/shard_map/pallas_call | solution.py:325
  386.4 11.5 %shard_map.138.rest_0_ = bf16[3072,1536]{1,0:T(8,128)(2,1)} custom-call(s32[1]{0:T(128)} %bitcast.19.case_ref, f32[2]{0:T(128)S(1)} %pad_maximum_fusion.5.scales, bf16[3072,1536]{1,0:T(8,128)(2,1)} %bitcast.76, bf16[256,3072]{1,0:T(8,128)(2,1)S(1)} %get-tuple-element.54.slope, ...), custom_call_target="tpu_custom_call", output_to_operand_aliasing={{}: (12, {})} | custom-call | flops 2415919104 | bytes 14155776 | tf_op jit(solution)/shard_map/pallas_call | solution.py:325
  397.9 5.1 %shard_map.139 = bf16[3072,1536]{1,0:T(8,128)(2,1)} custom-call(s32[1]{0:T(128)} %bitcast.19.case_ref, f32[2]{0:T(128)S(1)} %pad_maximum_fusion.5.scales, bf16[3072,1536]{1,0:T(8,128)(2,1)} %bitcast.77, bf16[256,3072]{1,0:T(8,128)(2,1)S(1)} %get-tuple-element.54.slope, ...), custom_call_target="tpu_custom_call", output_to_operand_aliasing={{}: (12, {})} | custom-call | flops 805306368 | bytes 4718592 | tf_op jit(solution)/shard_map/pallas_call | solution.py:325
  (207 shorter events, 37.3 us)
Async XLA Ops:
  2.6 22.0 %collective-permute-start.1 = (bf16[272,1536]{1,0:T(8,128)(2,1)S(1)}, bf16[272,1536]{1,0:T(8,128)(2,1)S(1)}, u32[]{:S(2)}, u32[]{:S(2)}) collective-permute-start(bf16[272,1536]{1,0:T(8,128)(2,1)S(1)} %pad_maximum_fusion.2), channel_id=1, source_target_pairs={{0,1},{1,0},{2,3},{3,2},{4,5},{5,4},{6,7},{7,6},{8,9},{9,8},{10,11... | collective-permute-start | bytes 2506760 | tf_op jit(solution)/shard_map/ppermute | solution.py:27
  5.9 371.8 %collective-permute-start.21 = (bf16[3072,1536]{1,0:T(8,128)(2,1)}, bf16[3072,1536]{1,0:T(8,128)(2,1)}, u32[]{:S(2)}, u32[]{:S(2)}) collective-permute-start(bf16[3072,1536]{1,0:T(8,128)(2,1)} %bitcast.74), channel_id=1, source_target_pairs={{0,16},{16,0},{32,48},{48,32},{64,80},{80,64},{96,112},{112,96},{1... | collective-permute-start | bytes 28311560 | tf_op jit(solution)/shard_map/ppermute | solution.py:27
  11.2 18.6 %slice-start = ((s8[9437184]{0:T(1024)(128)(4,1)}), s8[4194304]{0:T(1024)(128)(4,1)S(1)}, s32[]{:S(2)}) async-start(s8[9437184]{0:T(1024)(128)(4,1)} %bitcast.78), calls=%async_computation.1 | async-start | bytes 8388608
  11.2 18.6 %slice-start.1 = ((s8[9437184]{0:T(1024)(128)(4,1)}), s8[4194304]{0:T(1024)(128)(4,1)S(1)}, s32[]{:S(2)}) async-start(s8[9437184]{0:T(1024)(128)(4,1)} %bitcast.78), calls=%async_computation.2 | async-start | bytes 8388608
  50.3 11.2 %collective-permute-start.2 = (bf16[256,128]{1,0:T(8,128)(2,1)S(1)}, bf16[256,128]{1,0:T(8,128)(2,1)S(1)}, u32[]{:S(2)}, u32[]{:S(2)}) collective-permute-start(bf16[256,128]{1,0:T(8,128)(2,1)S(1)} %get-tuple-element.29), channel_id=1, source_target_pairs={{0,1},{1,0},{2,3},{3,2},{4,5},{5,4},{6,7},{7,6},{8,9},{9,8},{10,11... | collective-permute-start | bytes 196616 | tf_op jit(solution)/shard_map/ppermute | solution.py:27
  54.5 14.7 %collective-permute-start.17 = (bf16[128,1664]{1,0:T(8,128)(2,1)S(1)}, bf16[128,1664]{1,0:T(8,128)(2,1)S(1)}, u32[]{:S(2)}, u32[]{:S(2)}) collective-permute-start(bf16[128,1664]{1,0:T(8,128)(2,1)S(1)} %get-tuple-element.41.up), channel_id=1, source_target_pairs={{0,32},{16,48},{32,64},{48,80},{64,96},{80,112},{96,0},{112,16},{1... | collective-permute-start | bytes 1277960 | tf_op jit(solution)/shard_map/ppermute | solution.py:23
  57.3 33.2 %collective-permute-start.11 = (bf16[192,1536]{1,0:T(8,128)(2,1)}, bf16[192,1536]{1,0:T(8,128)(2,1)}, u32[]{:S(2)}, u32[]{:S(2)}) collective-permute-start(bf16[192,1536]{1,0:T(8,128)(2,1)} %constant_dynamic-slice_fusion.up), channel_id=1, source_target_pairs={{0,32},{16,48},{32,64},{48,80},{64,96},{80,112},{96,0},{112,16},{1... | collective-permute-start | bytes 1769480 | tf_op jit(solution)/shard_map/ppermute | solution.py:23
  59.2 33.9 %collective-permute-start.12 = (bf16[192,1536]{1,0:T(8,128)(2,1)}, bf16[192,1536]{1,0:T(8,128)(2,1)}, u32[]{:S(2)}, u32[]{:S(2)}) collective-permute-start(bf16[192,1536]{1,0:T(8,128)(2,1)} %fusion.30.down), channel_id=1, source_target_pairs={{0,96},{16,112},{32,0},{48,16},{64,32},{80,48},{96,64},{112,80},{1... | collective-permute-start | bytes 1769480 | tf_op jit(solution)/shard_map/ppermute | solution.py:23
  61.5 20.5 %copy-start = (bf16[1,1,256,1536]{3,2,1,0:T(8,128)(2,1)S(1)}, bf16[1,1,256,1536]{3,2,1,0:T(8,128)(2,1)}, u32[]{:S(2)}) copy-start(bf16[1,1,256,1536]{3,2,1,0:T(8,128)(2,1)} %param.9) | copy-start | bytes 2359300
  61.5 20.5 %collective-permute-start.18 = (bf16[128,1664]{1,0:T(8,128)(2,1)}, bf16[128,1664]{1,0:T(8,128)(2,1)}, u32[]{:S(2)}, u32[]{:S(2)}) collective-permute-start(bf16[128,1664]{1,0:T(8,128)(2,1)} %get-tuple-element.42.down), channel_id=1, source_target_pairs={{0,96},{16,112},{32,0},{48,16},{64,32},{80,48},{96,64},{112,80},{1... | collective-permute-start | bytes 1277960 | tf_op jit(solution)/shard_map/ppermute | solution.py:23
  70.0 23.1 %collective-permute-start.3 = (bf16[256,1536]{1,0:T(8,128)(2,1)}, bf16[256,1536]{1,0:T(8,128)(2,1)}, u32[]{:S(2)}, u32[]{:S(2)}) collective-permute-start(bf16[256,1536]{1,0:T(8,128)(2,1)} %dynamic-slice_convert_fusion), channel_id=1, source_target_pairs={{0,1},{1,0},{2,3},{3,2},{4,5},{5,4},{6,7},{7,6},{8,9},{9,8},{10,11... | collective-permute-start | bytes 2359304 | tf_op jit(solution)/shard_map/ppermute | solution.py:27
  82.0 22.2 %collective-permute-start = (bf16[256,1536]{1,0:T(8,128)(2,1)S(1)}, bf16[256,1536]{1,0:T(8,128)(2,1)}, u32[]{:S(2)}, u32[]{:S(2)}) collective-permute-start(bf16[256,1536]{1,0:T(8,128)(2,1)S(1)} %bitcast.64), channel_id=1, source_target_pairs={{0,1},{1,0},{2,3},{3,2},{4,5},{5,4},{6,7},{7,6},{8,9},{9,8},{10,11... | collective-permute-start | bytes 2359304 | tf_op jit(solution)/shard_map/ppermute | solution.py:27
  90.5 29.3 %collective-permute-start.23 = (bf16[256,1536]{1,0:T(8,128)(2,1)}, bf16[256,1536]{1,0:T(8,128)(2,1)}, u32[]{:S(2)}, u32[]{:S(2)}) collective-permute-start(bf16[256,1536]{1,0:T(8,128)(2,1)} %get-tuple-element.60.down), channel_id=1, source_target_pairs={{0,96},{16,112},{32,0},{48,16},{64,32},{80,48},{96,64},{112,80},{1... | collective-permute-start | bytes 2359304 | tf_op jit(solution)/shard_map/ppermute | solution.py:23
  93.0 28.0 %collective-permute-start.22 = (bf16[256,1536]{1,0:T(8,128)(2,1)}, bf16[256,1536]{1,0:T(8,128)(2,1)}, u32[]{:S(2)}, u32[]{:S(2)}) collective-permute-start(bf16[256,1536]{1,0:T(8,128)(2,1)} %get-tuple-element.61.up), channel_id=1, source_target_pairs={{0,32},{16,48},{32,64},{48,80},{64,96},{80,112},{96,0},{112,16},{1... | collective-permute-start | bytes 2359304 | tf_op jit(solution)/shard_map/ppermute | solution.py:23
  93.1 48.4 %collective-permute-start.31 = (bf16[512,1536]{1,0:T(8,128)(2,1)}, bf16[512,1536]{1,0:T(8,128)(2,1)}, u32[]{:S(2)}, u32[]{:S(2)}) collective-permute-start(bf16[512,1536]{1,0:T(8,128)(2,1)} %get-tuple-element.56.down), channel_id=1, source_target_pairs={{0,96},{16,112},{32,0},{48,16},{64,32},{80,48},{96,64},{112,80},{1... | collective-permute-start | bytes 4718600 | tf_op jit(solution)/shard_map/ppermute | solution.py:23
  104.2 40.6 %collective-permute-start.30 = (bf16[512,1536]{1,0:T(8,128)(2,1)}, bf16[512,1536]{1,0:T(8,128)(2,1)}, u32[]{:S(2)}, u32[]{:S(2)}) collective-permute-start(bf16[512,1536]{1,0:T(8,128)(2,1)} %get-tuple-element.57.up), channel_id=1, source_target_pairs={{0,32},{16,48},{32,64},{48,80},{64,96},{80,112},{96,0},{112,16},{1... | collective-permute-start | bytes 4718600 | tf_op jit(solution)/shard_map/ppermute | solution.py:23
  104.8 13.6 %all-to-all-start = ((f32[16,1,1]{2,1,0:T(1,128)}), f32[16,1,1]{2,1,0:T(1,128)S(1)}, u32[]{:S(2)}, u32[]{:S(2)}) async-start(f32[16,1,1]{2,1,0:T(1,128)} %broadcast_in_dim.37), calls=%async_computation | async-start | bytes 16384 | tf_op jit(solution)/shard_map/all_to_all | solution.py:38
  119.8 21.7 %copy-start.41 = (bf16[384,1536]{1,0:T(8,128)(2,1)S(1)}, bf16[384,1536]{1,0:T(8,128)(2,1)}, u32[]{:S(2)}) copy-start(bf16[384,1536]{1,0:T(8,128)(2,1)} %pad_maximum_fusion) | copy-start | bytes 3538948
  119.8 25.4 %collective-permute-start.5 = (f32[2,256]{1,0:T(2,128)S(1)}, f32[2,256]{1,0:T(2,128)S(1)}, u32[]{:S(2)}, u32[]{:S(2)}) collective-permute-start(f32[2,256]{1,0:T(2,128)S(1)} %pad_maximum_fusion.4), channel_id=1, source_target_pairs={{0,1},{1,0},{2,3},{3,2},{4,5},{5,4},{6,7},{7,6},{8,9},{9,8},{10,11... | collective-permute-start | bytes 6152 | tf_op jit(solution)/shard_map/ppermute | solution.py:27
  121.0 25.9 %collective-permute-start.9 = (f32[1664]{0:T(1024)S(1)}, f32[1664]{0:T(1024)S(1)}, u32[]{:S(2)}, u32[]{:S(2)}) collective-permute-start(f32[1664]{0:T(1024)S(1)} %concatenate.66), channel_id=1, source_target_pairs={{0,64},{16,80},{32,96},{48,112},{64,0},{80,16},{96,32},{112,48},{1... | collective-permute-start | bytes 19976 | tf_op jit(solution)/shard_map/ppermute | solution.py:27
  141.5 24.7 %collective-permute-start.10 = (bf16[384,1536]{1,0:T(8,128)(2,1)S(1)}, bf16[384,1536]{1,0:T(8,128)(2,1)S(1)}, u32[]{:S(2)}, u32[]{:S(2)}) collective-permute-start(bf16[384,1536]{1,0:T(8,128)(2,1)S(1)} %copy-done.41), channel_id=1, source_target_pairs={{0,16},{16,0},{32,48},{48,32},{64,80},{80,64},{96,112},{112,96},{1... | collective-permute-start | bytes 3538952 | tf_op jit(solution)/shard_map/ppermute | solution.py:27
  144.8 13.8 %collective-permute-start.19 = (bf16[128,1664]{1,0:T(8,128)(2,1)}, bf16[128,1664]{1,0:T(8,128)(2,1)S(1)}, u32[]{:S(2)}, u32[]{:S(2)}) collective-permute-start(bf16[128,1664]{1,0:T(8,128)(2,1)} %get-tuple-element.43), channel_id=1, source_target_pairs={{0,96},{16,112},{32,0},{48,16},{64,32},{80,48},{96,64},{112,80},{1... | collective-permute-start | bytes 1277960 | tf_op jit(solution)/shard_map/ppermute | solution.py:23
  145.2 8.9 %collective-permute-start.8 = (f32[1664]{0:T(1024)S(1)}, f32[1664]{0:T(1024)S(1)}, u32[]{:S(2)}, u32[]{:S(2)}) collective-permute-start(f32[1664]{0:T(1024)S(1)} %concatenate.66), channel_id=1, source_target_pairs={{0,32},{16,48},{32,0},{48,16},{64,96},{80,112},{96,64},{112,80},{1... | collective-permute-start | bytes 19976 | tf_op jit(solution)/shard_map/ppermute | solution.py:27
  146.9 8.7 %collective-permute-start.7 = (f32[1664]{0:T(1024)S(1)}, f32[1664]{0:T(1024)S(1)}, u32[]{:S(2)}, u32[]{:S(2)}) collective-permute-start(f32[1664]{0:T(1024)S(1)} %concatenate.66), channel_id=1, source_target_pairs={{0,16},{16,0},{32,48},{48,32},{64,80},{80,64},{96,112},{112,96},{1... | collective-permute-start | bytes 19976 | tf_op jit(solution)/shard_map/ppermute | solution.py:27
  154.1 85.8 %collective-permute-start.27 = (bf16[768,1536]{1,0:T(8,128)(2,1)S(1)}, bf16[768,1536]{1,0:T(8,128)(2,1)}, u32[]{:S(2)}, u32[]{:S(2)}) collective-permute-start(bf16[768,1536]{1,0:T(8,128)(2,1)S(1)} %copy-done.1), channel_id=1, source_target_pairs={{0,96},{16,112},{32,0},{48,16},{64,32},{80,48},{96,64},{112,80},{1... | collective-permute-start | bytes 7077896 | tf_op jit(solution)/shard_map/ppermute | solution.py:23
  155.6 64.0 %collective-permute-start.13 = (bf16[192,1536]{1,0:T(8,128)(2,1)}, bf16[192,1536]{1,0:T(8,128)(2,1)S(1)}, u32[]{:S(2)}, u32[]{:S(2)}) collective-permute-start(bf16[192,1536]{1,0:T(8,128)(2,1)} %get-tuple-element.38), channel_id=1, source_target_pairs={{0,96},{16,112},{32,0},{48,16},{64,32},{80,48},{96,64},{112,80},{1... | collective-permute-start | bytes 1769480 | tf_op jit(solution)/shard_map/ppermute | solution.py:23
  158.6 61.0 %collective-permute-start.14 = (bf16[192,1536]{1,0:T(8,128)(2,1)}, bf16[192,1536]{1,0:T(8,128)(2,1)S(1)}, u32[]{:S(2)}, u32[]{:S(2)}) collective-permute-start(bf16[192,1536]{1,0:T(8,128)(2,1)} %get-tuple-element.39), channel_id=1, source_target_pairs={{0,32},{16,48},{32,64},{48,80},{64,96},{80,112},{96,0},{112,16},{1... | collective-permute-start | bytes 1769480 | tf_op jit(solution)/shard_map/ppermute | solution.py:23
  158.7 60.9 %copy-start.36 = (bf16[256,1664]{1,0:T(8,128)(2,1)S(1)}, bf16[256,1664]{1,0:T(8,128)(2,1)}, u32[]{:S(2)}) copy-start(bf16[256,1664]{1,0:T(8,128)(2,1)} %copy-done.35) | copy-start | bytes 2555908
  158.8 60.8 %copy-start.7 = (bf16[128,1664]{1,0:T(8,128)(2,1)S(1)}, bf16[128,1664]{1,0:T(8,128)(2,1)}, u32[]{:S(2)}) copy-start(bf16[128,1664]{1,0:T(8,128)(2,1)} %copy-done.6) | copy-start | bytes 1277956
  166.2 76.0 %collective-permute-start.26 = (bf16[768,1536]{1,0:T(8,128)(2,1)S(1)}, bf16[768,1536]{1,0:T(8,128)(2,1)}, u32[]{:S(2)}, u32[]{:S(2)}) collective-permute-start(bf16[768,1536]{1,0:T(8,128)(2,1)S(1)} %copy-done.2), channel_id=1, source_target_pairs={{0,32},{16,48},{32,64},{48,80},{64,96},{80,112},{96,0},{112,16},{1... | collective-permute-start | bytes 7077896 | tf_op jit(solution)/shard_map/ppermute | solution.py:23
  219.5 16.2 %collective-permute-start.16 = (bf16[256,1664]{1,0:T(8,128)(2,1)S(1)}, bf16[256,1664]{1,0:T(8,128)(2,1)S(1)}, u32[]{:S(2)}, u32[]{:S(2)}) collective-permute-start(bf16[256,1664]{1,0:T(8,128)(2,1)S(1)} %copy-done.36), channel_id=1, source_target_pairs={{0,16},{16,0},{32,48},{48,32},{64,80},{80,64},{96,112},{112,96},{1... | collective-permute-start | bytes 2555912 | tf_op jit(solution)/shard_map/ppermute | solution.py:27
  219.6 14.7 %collective-permute-start.20 = (bf16[128,1664]{1,0:T(8,128)(2,1)S(1)}, bf16[128,1664]{1,0:T(8,128)(2,1)S(1)}, u32[]{:S(2)}, u32[]{:S(2)}) collective-permute-start(bf16[128,1664]{1,0:T(8,128)(2,1)S(1)} %copy-done.7), channel_id=1, source_target_pairs={{0,32},{16,48},{32,64},{48,80},{64,96},{80,112},{96,0},{112,16},{1... | collective-permute-start | bytes 1277960 | tf_op jit(solution)/shard_map/ppermute | solution.py:23
  221.8 18.1 %copy-start.26 = (bf16[192,1536]{1,0:T(8,128)(2,1)}, bf16[192,1536]{1,0:T(8,128)(2,1)S(1)}, u32[]{:S(2)}) copy-start(bf16[192,1536]{1,0:T(8,128)(2,1)S(1)} %get-tuple-element.63) | copy-start | bytes 1769476
  234.3 48.2 %collective-permute-start.4 = (bf16[256,1536]{1,0:T(8,128)(2,1)S(1)}, bf16[256,1536]{1,0:T(8,128)(2,1)S(1)}, u32[]{:S(2)}, u32[]{:S(2)}) collective-permute-start(bf16[256,1536]{1,0:T(8,128)(2,1)S(1)} %shard_map.130), channel_id=1, source_target_pairs={{0,2},{2,4},{4,6},{6,8},{8,10},{10,12},{12,14},{14,0},{1,3},{3,5},... | collective-permute-start | bytes 2359304 | tf_op jit(solution)/shard_map/ppermute | solution.py:23
  235.8 51.5 %collective-permute-start.15 = (bf16[384,1536]{1,0:T(8,128)(2,1)}, bf16[384,1536]{1,0:T(8,128)(2,1)}, u32[]{:S(2)}, u32[]{:S(2)}) collective-permute-start(bf16[384,1536]{1,0:T(8,128)(2,1)} %pad_maximum_fusion.1), channel_id=1, source_target_pairs={{0,1},{1,0},{2,3},{3,2},{4,5},{5,4},{6,7},{7,6},{8,9},{9,8},{10,11... | collective-permute-start | bytes 3538952 | tf_op jit(solution)/shard_map/ppermute | solution.py:27
  239.9 47.3 %collective-permute-start.6 = (bf16[256,1536]{1,0:T(8,128)(2,1)}, bf16[256,1536]{1,0:T(8,128)(2,1)S(1)}, u32[]{:S(2)}, u32[]{:S(2)}) collective-permute-start(bf16[256,1536]{1,0:T(8,128)(2,1)} %add_convert_fusion), channel_id=1, source_target_pairs={{0,14},{2,0},{4,2},{6,4},{8,6},{10,8},{12,10},{14,12},{1,15},{3,1}... | collective-permute-start | bytes 2359304 | tf_op jit(solution)/shard_map/ppermute | solution.py:23
  242.2 40.3 %collective-permute-start.34 = (bf16[256,128]{1,0:T(8,128)(2,1)S(1)}, bf16[256,128]{1,0:T(8,128)(2,1)S(1)}, u32[]{:S(2)}, u32[]{:S(2)}) collective-permute-start(bf16[256,128]{1,0:T(8,128)(2,1)S(1)} %pad_maximum_fusion.3), channel_id=1, source_target_pairs={{0,1},{1,0},{2,3},{3,2},{4,5},{5,4},{6,7},{7,6},{8,9},{9,8},{10,11... | collective-permute-start | bytes 196616 | tf_op jit(solution)/shard_map/ppermute | solution.py:27
  282.5 103.9 %collective-permute-start.28 = (bf16[768,1536]{1,0:T(8,128)(2,1)}, bf16[768,1536]{1,0:T(8,128)(2,1)}, u32[]{:S(2)}, u32[]{:S(2)}) collective-permute-start(bf16[768,1536]{1,0:T(8,128)(2,1)} %get-tuple-element.47.above), channel_id=1, source_target_pairs={{0,32},{16,48},{32,64},{48,80},{64,96},{80,112},{96,0},{112,16},{1... | collective-permute-start | bytes 7077896 | tf_op jit(solution)/shard_map/ppermute | solution.py:23
  282.5 103.9 %collective-permute-start.29 = (bf16[768,1536]{1,0:T(8,128)(2,1)}, bf16[768,1536]{1,0:T(8,128)(2,1)}, u32[]{:S(2)}, u32[]{:S(2)}) collective-permute-start(bf16[768,1536]{1,0:T(8,128)(2,1)} %get-tuple-element.48.below), channel_id=1, source_target_pairs={{0,96},{16,112},{32,0},{48,16},{64,32},{80,48},{96,64},{112,80},{1... | collective-permute-start | bytes 7077896 | tf_op jit(solution)/shard_map/ppermute | solution.py:23
  287.2 82.5 %collective-permute-start.32 = (bf16[512,1536]{1,0:T(8,128)(2,1)}, bf16[512,1536]{1,0:T(8,128)(2,1)}, u32[]{:S(2)}, u32[]{:S(2)}) collective-permute-start(bf16[512,1536]{1,0:T(8,128)(2,1)} %get-tuple-element.49.above), channel_id=1, source_target_pairs={{0,32},{16,48},{32,64},{48,80},{64,96},{80,112},{96,0},{112,16},{1... | collective-permute-start | bytes 4718600 | tf_op jit(solution)/shard_map/ppermute | solution.py:23
  287.3 82.4 %collective-permute-start.33 = (bf16[512,1536]{1,0:T(8,128)(2,1)}, bf16[512,1536]{1,0:T(8,128)(2,1)}, u32[]{:S(2)}, u32[]{:S(2)}) collective-permute-start(bf16[512,1536]{1,0:T(8,128)(2,1)} %get-tuple-element.50.below), channel_id=1, source_target_pairs={{0,96},{16,112},{32,0},{48,16},{64,32},{80,48},{96,64},{112,80},{1... | collective-permute-start | bytes 4718600 | tf_op jit(solution)/shard_map/ppermute | solution.py:23
  304.7 68.2 %copy-start.40 = (f32[3072,128]{1,0:T(8,128)S(1)}, f32[3072,128]{1,0:T(8,128)}, u32[]{:S(2)}) copy-start(f32[3072,128]{1,0:T(8,128)} %fusion.16) | copy-start | bytes 4718596
  304.7 68.2 %copy-start.42 = (bf16[1536,128]{1,0:T(8,128)(2,1)S(1)}, bf16[1536,128]{1,0:T(8,128)(2,1)}, u32[]{:S(2)}) copy-start(bf16[1536,128]{1,0:T(8,128)(2,1)} %reshape.115) | copy-start | bytes 1179652
  304.7 68.2 %copy-start.43 = (bf16[1536,128]{1,0:T(8,128)(2,1)S(1)}, bf16[1536,128]{1,0:T(8,128)(2,1)}, u32[]{:S(2)}) copy-start(bf16[1536,128]{1,0:T(8,128)(2,1)} %reshape.116) | copy-start | bytes 1179652
  304.7 68.2 %copy-start.45 = (bf16[256,128]{1,0:T(8,128)(2,1)S(1)}, bf16[256,128]{1,0:T(8,128)(2,1)}, u32[]{:S(2)}) copy-start(bf16[256,128]{1,0:T(8,128)(2,1)} %copy-done.44) | copy-start | bytes 196612
  304.7 68.2 %copy-start.47 = (bf16[256,128]{1,0:T(8,128)(2,1)S(1)}, bf16[256,128]{1,0:T(8,128)(2,1)}, u32[]{:S(2)}) copy-start(bf16[256,128]{1,0:T(8,128)(2,1)} %copy-done.46) | copy-start | bytes 196612
  369.7 28.2 %collective-permute-start.24 = (bf16[256,1536]{1,0:T(8,128)(2,1)}, bf16[256,1536]{1,0:T(8,128)(2,1)S(1)}, u32[]{:S(2)}, u32[]{:S(2)}) collective-permute-start(bf16[256,1536]{1,0:T(8,128)(2,1)} %get-tuple-element.45.above), channel_id=1, source_target_pairs={{0,32},{16,48},{32,64},{48,80},{64,96},{80,112},{96,0},{112,16},{1... | collective-permute-start | bytes 2359304 | tf_op jit(solution)/shard_map/ppermute | solution.py:23
  369.7 28.2 %collective-permute-start.25 = (bf16[256,1536]{1,0:T(8,128)(2,1)}, bf16[256,1536]{1,0:T(8,128)(2,1)S(1)}, u32[]{:S(2)}, u32[]{:S(2)}) collective-permute-start(bf16[256,1536]{1,0:T(8,128)(2,1)} %get-tuple-element.46.below), channel_id=1, source_target_pairs={{0,96},{16,112},{32,0},{48,16},{64,32},{80,48},{96,64},{112,80},{1... | collective-permute-start | bytes 2359304 | tf_op jit(solution)/shard_map/ppermute | solution.py:23
  (39 other events, 258.9 us)
where the time goes:
time: 404 us; the launch traced here: 403 us
  waiting for transfers between devices  219 us (54%)
  starting transfers between devices  55.1 us (14%)
  Pallas kernels  53.4 us (13%)
  local copies, waits for them, and re-layouts  25.7 us (6%)
  matrix products  23.5 us (6%)
  other arithmetic  21.1 us (5%)
  between operations  4.75 us (1%)
    ppermute x22, waiting for transfers between devices, from_behind(): lax.ppermute(shard, axis, [(i, (i + by) % length) for i in range(length)])  165 us
    ppermute x13, waiting for transfers between devices, flipped(): lax.ppermute(block, axis, [(i, i ^ 1 << bit) for i in range(lax.axis_size...  50.7 us
    ppermute x22, starting transfers between devices, from_behind(): lax.ppermute(shard, axis, [(i, (i + by) % length) for i in range(length)])  32 us
    pallas_call x3, Pallas kernels, averaged_chunk(): pl.pallas_call(average_kernel, grid_spec=pltpu.PrefetchScalarGridSpec(num...  25.3 us
    pallas_call x2, Pallas kernels, per_head(): pl.pallas_call(kernel, grid=(heads,), in_specs=specs, out_specs=[by_head...  20 us
    ppermute x13, starting transfers between devices, flipped(): lax.ppermute(block, axis, [(i, i ^ 1 << bit) for i in range(lax.axis_size...  17.1 us
    slice x3, local copies, waits for them, and re-layouts, section(): query_weight[base + a:base + b]  10.4 us
    dot_general x4, matrix products, projected(): product = jnp.dot(normed, weight, preferred_element_type=jnp.float32)  10 us
  transfers between devices with their start and end apart: 36, of which 12 were waited for; matrix products, arithmetic and copies ran while one was open for 16% of the time, Pallas kernels for 12%

commit v1 on v0

--- a/solution.py
+++ b/solution.py
@@ -1,3 +1,5 @@
+from functools import partial
+
 import jax
 import jax.numpy as jnp
 from jax import lax
@@ -13,7 +15,6 @@
 STEP_EPS = 1e-06
 LEARN_RATE = 0.2
 MASK_FILL = -1e30
-CHUNK_SHARES = (2, 3, 1)
 BLOCK = 256
 STRIP = 512
 
@@ -36,13 +37,6 @@
 def of_everyone(shard, axis):
     copies = jnp.broadcast_to(shard, (lax.axis_size(axis), *shard.shape))
     return jnp.sum(lax.all_to_all(copies, axis, split_axis=0, concat_axis=0, tiled=True), axis=0)
-
-
-def chunk_cuts(rows):
-    whole, edges = sum(CHUNK_SHARES), [0]
-    for share in CHUNK_SHARES:
-        edges.append(edges[-1] + rows * share // whole)
-    return list(zip(edges[:-1], edges[1:]))
 
 
 def relay_kernel(case_ref, up, down, above_in, below_in, above, below, held, sem):
@@ -204,32 +198,207 @@
     return ((mine.astype(jnp.float32) + theirs.astype(jnp.float32)) * 0.5).astype(jnp.bfloat16)
 
 
-def average_kernel(
-    case_ref, scales, weights, slope, slope_other, grad, grad_other, near, above, below, from_up,
-    from_down, *rest,
-):
-    out_ref = rest[-1]
-    columns = weights.shape[1]
-    in_scale = (2 * columns) ** (-0.5)
-    flipped_own, flipped_other = slope[...].T, slope_other[...].T
-    chosen = source_of(pl.program_id(0), case_ref[0])
-
-    def strip(number, carry):
-        cols = pl.ds(pl.multiple_of(number * STRIP, STRIP), STRIP)
-
-        def step(rows, grads, scale):
-            gradient = dot(rows, grads[:, cols], ROWS_COLS)
-            return (gradient * (LEARN_RATE * in_scale * scale)).astype(jnp.bfloat16)
-
-        mine = weights[:, cols] - step(flipped_own, grad, scales[0])
-        theirs = step(flipped_other, grad_other, scales[1])
-        partner = near[:, cols]
-        for source, weight in enumerate((above, below, from_up, from_down), 1):
-            partner = jnp.where(chosen == source, weight[:, cols], partner)
-        out_ref[:, cols] = (mine + (partner - theirs)) * 0.5
+def strips(columns, body):
+    def at(number, carry):
+        body(pl.ds(pl.multiple_of(number * STRIP, STRIP), STRIP))
         return carry
 
-    lax.fori_loop(0, columns // STRIP, strip, 0)
+    lax.fori_loop(0, columns // STRIP, at, 0)
+
+
+def stepped(rows, grads, scale):
+    in_scale = (2 * grads.shape[1]) ** (-0.5)
+
+    def at(cols):
+        gradient = dot(rows, grads[:, cols], ROWS_COLS)
+        return (gradient * (LEARN_RATE * in_scale * scale)).astype(jnp.bfloat16)
+
+    return at
+
+
+def source_of(half, case):
+    up = jnp.where(case == 1, 4, jnp.where(case == 2, 1, 3))
+    down = jnp.where(case == 1, 2, jnp.where(case == 2, 3, 4))
+    return jnp.where(case == 0, 0, jnp.where(half == 0, up, down))
+
+
+def partner_at(half, case, near_up, near_down, *parts):
+    chosen = source_of(half, case)
+
+    def at(cols):
+        partner = jnp.where(half == 0, near_up[:, cols], near_down[:, cols])
+        for source, part in enumerate(parts, 1):
+            partner = jnp.where(chosen == source, part[:, cols], partner)
+        return partner
+
+    return at
+
+
+def renew_kernel(scale, up, down, slope_up, slope_down, grad, out_up, out_down):
+    step_up = stepped(slope_up[...].T, grad, scale[0])
+    step_down = stepped(slope_down[...].T, grad, scale[0])
+
+    def body(cols):
+        out_up[:, cols] = up[:, cols] - step_up(cols)
+        out_down[:, cols] = down[:, cols] - step_down(cols)
+
+    strips(grad.shape[1], body)
+
+
+def renewed(scale, weights, slope, grad, begin, end):
+    rows, columns = weights.shape
+    depth, base = slope.shape[0], rows // (2 * BLOCK)
+    first, blocks = begin // BLOCK, (end - begin) // BLOCK
+    block = (BLOCK, columns)
+    shape = jax.ShapeDtypeStruct((end - begin, columns), weights.dtype)
+    size = (end - begin) * columns
+    return pl.pallas_call(
+        renew_kernel,
+        grid=(blocks,),
+        in_specs=[
+            pl.BlockSpec(memory_space=pltpu.SMEM),
+            pl.BlockSpec(block, lambda i: (first + i, 0)),
+            pl.BlockSpec(block, lambda i: (base + first + i, 0)),
+            pl.BlockSpec((depth, BLOCK), lambda i: (0, first + i)),
+            pl.BlockSpec((depth, BLOCK), lambda i: (0, base + first + i)),
+            pl.BlockSpec((depth, columns), lambda i: (0, 0)),
+        ],
+        out_specs=[pl.BlockSpec(block, lambda i: (i, 0))] * 2,
+        out_shape=[shape] * 2,
+        cost_estimate=pl.CostEstimate(
+            flops=4 * size * depth, bytes_accessed=8 * size, transcendentals=0
+        ),
+        compiler_params=pltpu.CompilerParams(vmem_limit_bytes=24 << 20),
+    )(scale, weights, weights, slope, slope, grad)
+
+
+def average_kernel(case_ref, scales, weights, slope, slope_other, grad, grad_other, *rest):
+    sources, out = rest[:6], rest[-1]
+    mine = stepped(slope[...].T, grad, scales[0])
+    theirs = stepped(slope_other[...].T, grad_other, scales[1])
+    partner = partner_at(pl.program_id(0), case_ref[0], *sources)
+
+    def body(cols):
+        own = weights[:, cols] - mine(cols)
+        out[:, cols] = (own + (partner(cols) - theirs(cols))) * 0.5
+
+    strips(weights.shape[1], body)
+
+
+def plain_kernel(begin, case_ref, *refs):
+    new, near, (above, below, from_up, from_down) = refs[:2], refs[2:4], refs[4:8]
+    out, own, part, sems = refs[-4:]
+    rows, base = own.shape[1], out.shape[0] // 2
+    kinds = (near, (from_down, below), (above, from_up), (from_up, from_down))
+
+    def average(partner):
+        loads = []
+        for half in range(2):
+            loads.append(pltpu.make_async_copy(new[half], own.at[half], sems.at[0, half]))
+            loads.append(pltpu.make_async_copy(partner[half], part.at[half], sems.at[1, half]))
+        for load in loads:
+            load.start()
+        stores = []
+        for half in range(2):
+            loads[2 * half].wait()
+            loads[2 * half + 1].wait()
+
+            def body(number, carry, half=half):
+                at = pl.ds(pl.multiple_of(number * 64, 64), 64)
+                own[half, at] = (own[half, at] + part[half, at]) * 0.5
+                return carry
+
+            lax.fori_loop(0, rows // 64, body, 0)
+            place = out.at[pl.ds(half * base + begin, rows)]
+            stores.append(pltpu.make_async_copy(own.at[half], place, sems.at[2, half]))
+            stores[half].start()
+        for store in stores:
+            store.wait()
+
+    for kind, partner in enumerate(kinds):
+
+        @pl.when(case_ref[0] == kind)
+        def _(partner=partner):
+            average(partner)
+
+
+def averaged(kernel, case, own, own_specs, sources, begin, end, shape, out):
+    rows, columns = shape
+    first, blocks = begin // BLOCK, (end - begin) // BLOCK
+    base = rows // (2 * BLOCK)
+    block = (BLOCK, columns)
+
+    def near_map(wanted):
+        def index(half, i, case_ref):
+            used = (half == wanted) & (case_ref[0] == 0)
+            return (jnp.where(used, i, 0), 0)
+
+        return index
+
+    def part_map(number):
+        def index(half, i, case_ref):
+            return (jnp.where(source_of(half, case_ref[0]) == number, i, 0), 0)
+
+        return index
+
+    in_specs = own_specs + [pl.BlockSpec(block, near_map(wanted)) for wanted in range(2)]
+    in_specs += [pl.BlockSpec(block, part_map(number)) for number in range(1, 5)]
+    operands = [case.reshape(1), *own, *sources]
+    aliases = {}
+    if out is not None:
+        in_specs.append(pl.BlockSpec(memory_space=pl.ANY))
+        aliases = {len(operands): 0}
+        operands.append(out)
+    size = 2 * blocks * BLOCK * columns
+    return pl.pallas_call(
+        kernel,
+        grid_spec=pltpu.PrefetchScalarGridSpec(
+            num_scalar_prefetch=1,
+            grid=(2, blocks),
+            in_specs=in_specs,
+            out_specs=pl.BlockSpec(block, lambda half, i, case_ref: (half * base + first + i, 0)),
+        ),
+        out_shape=jax.ShapeDtypeStruct(shape, jnp.bfloat16),
+        input_output_aliases=aliases,
+        cost_estimate=pl.CostEstimate(flops=4 * size, bytes_accessed=6 * size, transcendentals=0),
+        compiler_params=pltpu.CompilerParams(vmem_limit_bytes=40 << 20),
+    )(*operands)
+
+
+def averaged_weights(case, scales, weights, slopes, grads, sources, end, out):
+    rows, columns = weights.shape
+    depth, base, short = slopes[0].shape[0], rows // (2 * BLOCK), end // BLOCK
+    fixed = pl.BlockSpec((depth, columns), lambda half, i, case_ref: (0, 0))
+    own_specs = [
+        pl.BlockSpec(memory_space=pltpu.SMEM),
+        pl.BlockSpec((BLOCK, columns), lambda half, i, case_ref: (half * base + i, 0)),
+        pl.BlockSpec((depth, BLOCK), lambda half, i, case_ref: (0, half * base + i)),
+        pl.BlockSpec((depth, BLOCK), lambda half, i, case_ref: (0, half * short + i)),
+        fixed,
+        fixed,
+    ]
+    own = (scales, weights, *slopes, *grads)
+    return averaged(average_kernel, case, own, own_specs, sources, 0, end, weights.shape, out)
+
+
+def averaged_updates(case, own, sources, begin, end, shape, out):
+    block = (2, end - begin, shape[1])
+    anywhere = pl.BlockSpec(memory_space=pl.ANY)
+    size = (end - begin) * shape[1]
+    return pl.pallas_call(
+        partial(plain_kernel, begin),
+        in_specs=[pl.BlockSpec(memory_space=pltpu.SMEM)] + [anywhere] * 9,
+        out_specs=anywhere,
+        out_shape=jax.ShapeDtypeStruct(shape, jnp.bfloat16),
+        input_output_aliases={9: 0},
+        scratch_shapes=[
+            pltpu.VMEM(block, jnp.bfloat16),
+            pltpu.VMEM(block, jnp.bfloat16),
+            pltpu.SemaphoreType.DMA((3, 2)),
+        ],
+        cost_estimate=pl.CostEstimate(flops=4 * size, bytes_accessed=12 * size, transcendentals=0),
+        compiler_params=pltpu.CompilerParams(vmem_limit_bytes=24 << 20),
+    )(case.reshape(1), *own, *sources, out)
 
 
 def squares_kernel(slope, grad, key_grad, out, total):
@@ -289,56 +458,6 @@
     return jnp.where(case == 0, 0, jnp.where(half == 0, up, down))
 
 
-def averaged_chunk(case, scales, weights, slopes, grads, near, chunk, cut, out):
-    rows, columns = weights.shape
-    first, blocks = cut[0] // BLOCK, (cut[1] - cut[0]) // BLOCK
-    stride = rows // (2 * BLOCK)
-
-    def whole(half, i, case_ref):
-        return (half * stride + first + i, 0)
-
-    def near_map(half, i, case_ref):
-        used = source_of(half, case_ref[0]) == 0
-        return (jnp.where(used, half * stride + first + i, 0), 0)
-
-    def part_map(number):
-        def index(half, i, case_ref):
-            return (jnp.where(source_of(half, case_ref[0]) == number, i, 0), 0)
-
-        return index
-
-    block = (BLOCK, columns)
-    depth = slopes[0].shape[0]
-    in_specs = [pl.BlockSpec(memory_space=pltpu.SMEM), pl.BlockSpec(block, whole)]
-    across = pl.BlockSpec((depth, BLOCK), lambda *at: whole(*at)[::-1])
-    in_specs += [across] * 2
-    in_specs += [pl.BlockSpec((depth, columns), lambda half, i, case_ref: (0, 0))] * 2
-    in_specs += [pl.BlockSpec(block, near_map)]
-    in_specs += [pl.BlockSpec(block, part_map(number)) for number in range(1, 5)]
-    operands = [case.reshape(1), scales, weights, *slopes, *grads, near, *chunk]
-    aliases = {}
-    if out is not None:
-        in_specs.append(pl.BlockSpec(memory_space=pl.ANY))
-        aliases = {len(operands): 0}
-        operands.append(out)
-    size = 2 * blocks * BLOCK * columns
-    return pl.pallas_call(
-        average_kernel,
-        grid_spec=pltpu.PrefetchScalarGridSpec(
-            num_scalar_prefetch=1,
-            grid=(2, blocks),
-            in_specs=in_specs,
-            out_specs=pl.BlockSpec(block, whole),
-        ),
-        out_shape=jax.ShapeDtypeStruct(weights.shape, weights.dtype),
-        input_output_aliases=aliases,
-        cost_estimate=pl.CostEstimate(
-            flops=4 * size * depth, bytes_accessed=6 * size, transcendentals=0
-        ),
-        compiler_params=pltpu.CompilerParams(vmem_limit_bytes=40 << 20),
-    )(*operands)
-
-
 def settled_kernel(a_ref, b_ref, c_ref, d_ref):
     c_ref[...] = a_ref[...]
     d_ref[...] = b_ref[...]
@@ -373,14 +492,11 @@
 
     width = query_weight.shape[0]
     in_scale = width ** (-0.5)
-    cuts = chunk_cuts(width // 2)
-    parts = [
-        [query_weight[base + a : base + b] for a, b in cuts] for base in (0, width // 2)
-    ]
-    sent = []
-    for up, down in zip(*parts):
-        sent.append(gossip.first(up, down))
-    query_near = flipped(query_weight, "rep", 0)
+    half, early_rows = width // 2, width // 4
+    cuts = ((early_rows, half - BLOCK), (half - BLOCK, half))
+    parts = query_weight[:early_rows], query_weight[half : half + early_rows]
+    sent = gossip.first(*parts)
+    near = [flipped(part, "rep", 0) for part in parts]
 
     beside = jnp.broadcast_to(gain_local[None], (16, local_width))
     other = flipped(jnp.concatenate([bwd_rows, beside], axis=0), "tp", 0)
@@ -390,17 +506,9 @@
     _, scaled_b, inv_b, normed_b = normalize(bwd_full, gain_full)
     own_values_b = lax.dynamic_slice_in_dim(normed_b, offset, local_width, 1)
     key_rows = lax.dynamic_slice_in_dim(key_weight, offset, local_width, 0)
-    early = gossip.small(
-        jnp.concatenate([own_values_b, key_rows.reshape(HEAD, local_width)], axis=0)
-    )
+    early = gossip.small(own_values_b[:, :early_rows])
     early_other = flipped(early, "tp", 0)
-    normed_partner = in_order(early[:count], early_other[:count], low, 1)
-    key_partner = in_order(
-        early[count:].reshape(local_width, HEAD),
-        early_other[count:].reshape(local_width, HEAD),
-        low,
-        0,
-    )
+    normed_partner = in_order(early, early_other, low, 1)
 
     queries = projected(normed_b, query_weight)
     keys = projected(normed_b, key_weight)
@@ -418,14 +526,9 @@
         5,
     )
 
-    def tp_sum(part):
-        other = flipped(part, "tp", 0)
-        return (part.astype(jnp.float32) + other.astype(jnp.float32)).astype(jnp.bfloat16)
-
-    late = gossip.small(jnp.concatenate([query_grad, key_part], axis=1))
-    query_grad_partner = late[:, :local_width]
-    key_grad = tp_sum(key_part)
-    key_grad_partner = tp_sum(late[:, local_width:])
+    query_grad_partner = gossip.small(query_grad)
+    key_other = flipped(key_part, "tp", 0)
+    key_grad = (key_part.astype(jnp.float32) + key_other.astype(jnp.float32)).astype(jnp.bfloat16)
 
     contract_last = (((1,), (1,)), ((), ()))
     partial_grad = (
@@ -463,7 +566,7 @@
         )
 
     query_squares = gradient_squares(normed_b, query_grad, key_grad)
-    grad_key = weight_grad(normed_b, key_grad)
+    grad_key = weight_grad(own_values_b, key_grad)
     local_squares = query_squares + jnp.sum(grad_gain * grad_gain)
     fwd_other = flipped(fwd_rows, "tp", 0)
     fwd_other, local_squares = lax.optimization_barrier((fwd_other, local_squares))
@@ -498,30 +601,33 @@
     inverse_partner = both[local_width]
     gain_out = halves(gain_new, gain_partner)
 
-    key_out = halves(
-        updated(key_weight, step_of(grad_key, inverse)),
-        updated(
-            key_partner,
-            step_of(weight_grad(normed_partner, key_grad_partner), inverse_partner),
-        ),
-    )
-    later = []
-    for state in sent:
-        later.append(gossip.second(state))
+    key_new = updated(key_rows, step_of(grad_key, inverse))
+    key_half = halves(key_new, gossip.small(key_new))
+    key_out = in_order(key_half, flipped(key_half, "tp", 0), low, 0)
+
+    news = []
+    for begin, end in cuts:
+        new = renewed(inverse.reshape(1), query_weight, normed_b, query_grad, begin, end)
+        state = gossip.first(*new)
+        new_near = [flipped(part, "rep", 0) for part in new]
+        later = gossip.second(state)
+        news.append((new, (*new_near, *later)))
+
+    sources = (*near, *gossip.second(sent))
     next_rows, prev_rows = settled(next_rows, prev_rows)
-    slopes = (normed_b, normed_partner)
-    query_out = None
-    for i, cut in enumerate(cuts):
-        query_out = averaged_chunk(
-            gossip.case,
-            jnp.stack([inverse, inverse_partner]),
-            query_weight,
-            slopes,
-            (query_grad, query_grad_partner),
-            query_near,
-            later[i],
-            cut,
-            query_out,
+    query_out = averaged_weights(
+        gossip.case,
+        jnp.stack([inverse, inverse_partner]),
+        query_weight,
+        (normed_b, normed_partner),
+        (query_grad, query_grad_partner),
+        sources,
+        early_rows,
+        None,
+    )
+    for number, (begin, end) in enumerate(cuts):
+        query_out = averaged_updates(
+            gossip.case, *news[number], begin, end, query_weight.shape, query_out
         )
     return (
         next_rows[None, None],

time: 404 us -> 386 us (0.955)
  waiting for transfers between devices: 219 us -> 205 us
  starting transfers between devices: 55.1 us -> 65.6 us
  local copies, waits for them, and re-layouts: 25.7 us -> 16.9 us
  matrix products: 23.5 us -> 17.9 us
    ppermute x13 -> x19, waiting for transfers between devices: 50.7 us -> 21.6 us  [flipped(): lax.ppermute(block, axis, [(i, i ^ 1 << bit) for i in range(lax.axis_size...]
    ppermute x22 -> x26, waiting for transfers between devices: 165 us -> 184 us  [from_behind(): lax.ppermute(shard, axis, [(i, (i + by) % length) for i in range(length)])]
    slice x7 -> x2, local copies, waits for them, and re-layouts: 13.5 us -> 5.28 us  [the longest x1 5.24 us: section(): parts = (query_weight[:early_rows], query_weight[half:half + early_rows])]
    ppermute x22 -> x26, starting transfers between devices: 32 us -> 39.7 us  [from_behind(): lax.ppermute(shard, axis, [(i, (i + by) % length) for i in range(length)])]
    dot_general x2 -> x1, matrix products: 7.66 us -> 1.43 us  [weight_grad(): lax.dot_general(rows, grad, contract_first, preferred_element_type=jnp.fl...]
    unnamed x103 -> x110, local copies, waits for them, and re-layouts: 4.39 us -> 8.53 us
    pallas_call x3 -> x5, Pallas kernels: 25.3 us -> 21.7 us  [the longest x1 11.2 us: averaged(): pl.pallas_call(kernel, grid_spec=pltpu.PrefetchScalarGridSpec(num_scalar_...]
    ppermute x13 -> x19, starting transfers between devices: 17.1 us -> 19.6 us  [flipped(): lax.ppermute(block, axis, [(i, i ^ 1 << bit) for i in range(lax.axis_size...]
  transfers between devices with their start and end apart: 36 -> 46, of which waited for: 12 -> 13; matrix products, arithmetic and copies ran while one was open for 16% -> 10% of each run, Pallas kernels for 12% -> 9%
where the time goes in v1:
time: 386 us; the launch traced here: 385 us
  waiting for transfers between devices  205 us (53%)
  starting transfers between devices  65.6 us (17%)
  Pallas kernels  51.8 us (13%)
  other arithmetic  23.1 us (6%)
  matrix products  17.9 us (5%)
  local copies, waits for them, and re-layouts  16.9 us (4%)
  between operations  4.37 us (1%)
    ppermute x26, waiting for transfers between devices, from_behind(): lax.ppermute(shard, axis, [(i, (i + by) % length) for i in range(length)])  184 us
    ppermute x26, starting transfers between devices, from_behind(): lax.ppermute(shard, axis, [(i, (i + by) % length) for i in range(length)])  39.7 us
    pallas_call x2, Pallas kernels, per_head(): pl.pallas_call(kernel, grid=(heads,), in_specs=specs, out_specs=[by_head...  22 us
    ppermute x19, waiting for transfers between devices, flipped(): lax.ppermute(block, axis, [(i, i ^ 1 << bit) for i in range(lax.axis_size...  21.6 us
    ppermute x19, starting transfers between devices, flipped(): lax.ppermute(block, axis, [(i, i ^ 1 << bit) for i in range(lax.axis_size...  19.6 us
    pallas_call x1, Pallas kernels, averaged(): pl.pallas_call(kernel, grid_spec=pltpu.PrefetchScalarGridSpec(num_scalar_...  11.2 us
    dot_general x4, matrix products, projected(): product = jnp.dot(normed, weight, preferred_element_type=jnp.float32)  10 us
    unnamed x110, local copies, waits for them, and re-layouts  8.53 us
  transfers between devices with their start and end apart: 46, of which 13 were waited for; matrix products, arithmetic and copies ran while one was open for 10% of the time, Pallas kernels for 9%

profile of v1, /device:TPU:0, one launch (start us, length us, event | category | flops | bytes accessed | tf_op | source)
XLA Modules:
  0.0 384.8 jit_solution(18110818304047106763)
XLA Ops:
  2.6 3.4 collective-permute-start.1
  8.2 5.2 %slice_bitcast_fusion = (bf16[768,1536]{1,0:T(8,128)(2,1)}, bf16[768,1536]{1,0:T(8,128)(2,1)}) fusion(bf16[1,1,3072,1536]{3,2,1,0:T(8,128)(2,1)} %param.14), kind=kLoop, calls=%fused_computation.24 | loop fusion | bytes 9437184 | tf_op jit(solution)/shard_map/slice | solution.py:497
  13.5 11.1 %collective-permute-done.1 = bf16[272,1536]{1,0:T(8,128)(2,1)S(1)} collective-permute-done((bf16[272,1536]{1,0:T(8,128)(2,1)S(1)}, bf16[272,1536]{1,0:T(8,128)(2,1)S(1)}, u32[]{:S(2)}, u32[]{:S(2)}) %collective-permute-start.1) | collective-permute-done | bytes 835616 | tf_op jit(solution)/shard_map/ppermute | solution.py:28
  26.7 2.6 fusion.8.queries
  31.7 12.7 %shard_map.128 = (bf16[256,1536]{1,0:T(8,128)(2,1)S(1)}, f32[256,1536]{1,0:T(8,128)S(1)}, bf16[256,128]{1,0:T(8,128)(2,1)S(1)}) custom-call(bf16[256,1536]{1,0:T(8,128)(2,1)S(1)} %fusion.8.queries, bf16[256,128]{1,0:T(8,128)(2,1)S(1)} %fusion.14.keys, bf16[256,1536]{1,0:T(8,128)(2,1)S(1)} %constant_dynamic-slice_fusion.3.values, ...), custom_call_target="tpu_custom_call" | custom-call | flops 1006632960 | bytes 4718592 | tf_op jit(solution)/shard_map/pallas_call | solution.py:177
  44.4 4.4 %convolution_multiply_fusion = f32[256,3072]{1,0:T(8,128)} fusion(bf16[256,1536]{1,0:T(8,128)(2,1)S(1)} %get-tuple-element.57.grad, bf16[1,1,3072,1536]{3,2,1,0:T(8,128)(2,1)S(1)} %bitcast.54), kind=kOutput, calls=%fused_computation | convolution fusion | flops 2416705536 | bytes 13369344 | tf_op jit(solution)/shard_map/dot_general | solution.py:535
  48.8 3.3 collective-permute-start.2
  52.2 1.9 collective-permute-start.29
  54.1 2.0 collective-permute-start.23
  58.9 9.5 %collective-permute-done.23.above_in = bf16[128,768]{1,0:T(8,128)(2,1)S(1)} collective-permute-done((bf16[128,768]{1,0:T(8,128)(2,1)S(1)}, bf16[128,768]{1,0:T(8,128)(2,1)S(1)}, u32[]{:S(2)}, u32[]{:S(2)}) %collective-permute-start.23) | collective-permute-done | bytes 196640 | tf_op jit(solution)/shard_map/ppermute | solution.py:24
  69.8 3.6 collective-permute-start.25
  73.3 6.4 %shard_map.129 = f32[1,1]{1,0:T(1,128)} custom-call(bf16[256,3072]{1,0:T(8,128)(2,1)S(1)} %get-tuple-element.72.slope.slope_up.slope_down, bf16[256,1536]{1,0:T(8,128)(2,1)S(1)} %get-tuple-element.57.grad, bf16[256,128]{1,0:T(8,128)(2,1)S(1)} %add_convert_fusion.2.key_grad), custom_call_target="tpu_custom_call" | custom-call | flops 2617245696 | bytes 2359296 | tf_op jit(solution)/shard_map/pallas_call | solution.py:436
  80.4 2.3 collective-permute-start
  82.8 3.3 collective-permute-start.31
  88.4 2.0 multiply_reduce_fusion
  92.3 10.4 %collective-permute-done = bf16[256,1536]{1,0:T(8,128)(2,1)} collective-permute-done((bf16[256,1536]{1,0:T(8,128)(2,1)}, bf16[256,1536]{1,0:T(8,128)(2,1)}, u32[]{:S(2)}, u32[]{:S(2)}) %collective-permute-start) | collective-permute-done | bytes 786464 | tf_op jit(solution)/shard_map/ppermute | solution.py:28
  103.3 6.2 %all-to-all-start = ((f32[16,1,1]{2,1,0:T(1,128)}), f32[16,1,1]{2,1,0:T(1,128)S(1)}, u32[]{:S(2)}, u32[]{:S(2)}) async-start(f32[16,1,1]{2,1,0:T(1,128)} %broadcast_in_dim.35), calls=%async_computation | async-start | bytes 16384 | tf_op jit(solution)/shard_map/all_to_all | solution.py:39
  110.1 3.4 collective-permute-start.5
  113.5 2.3 convert_reduce_fusion
  115.9 3.1 fusion.4
  124.3 3.6 collective-permute-start.21
  128.7 3.3 collective-permute-start.36
  132.2 4.7 %collective-permute-done.40.above_in = bf16[768,128]{1,0:T(8,128)(2,1)S(1)} collective-permute-done((bf16[768,128]{1,0:T(8,128)(2,1)S(1)}, bf16[768,128]{1,0:T(8,128)(2,1)S(1)}, u32[]{:S(2)}, u32[]{:S(2)}) %collective-permute-start.40) | collective-permute-done | bytes 196640 | tf_op jit(solution)/shard_map/ppermute | solution.py:24
  136.9 2.9 fusion.6
  139.8 47.7 %collective-permute-done.41.below_in = bf16[768,128]{1,0:T(8,128)(2,1)S(1)} collective-permute-done((bf16[768,128]{1,0:T(8,128)(2,1)S(1)}, bf16[768,128]{1,0:T(8,128)(2,1)S(1)}, u32[]{:S(2)}, u32[]{:S(2)}) %collective-permute-start.41) | collective-permute-done | bytes 196640 | tf_op jit(solution)/shard_map/ppermute | solution.py:24
  187.6 6.3 %fusion.9.queries = bf16[256,1536]{1,0:T(8,128)(2,1)S(1)} fusion(bf16[256,3072]{1,0:T(8,128)(2,1)S(1)} %fusion.6, bf16[1,1,3072,1536]{3,2,1,0:T(8,128)(2,1)} %param.14), kind=kOutput, calls=%fused_computation.18 | convolution fusion | flops 2416705536 | bytes 11796480 | tf_op jit(solution)/shard_map/dot_general | solution.py:122
  193.9 4.0 %collective-permute-start.42 = (bf16[768,128]{1,0:T(8,128)(2,1)S(1)}, bf16[768,128]{1,0:T(8,128)(2,1)S(1)}, u32[]{:S(2)}, u32[]{:S(2)}) collective-permute-start(bf16[768,128]{1,0:T(8,128)(2,1)S(1)} %get-tuple-element.67), channel_id=1, source_target_pairs={{0,96},{16,112},{32,0},{48,16},{64,32},{80,48},{96,64},{112,80},{1... | collective-permute-start | bytes 589832 | tf_op jit(solution)/shard_map/ppermute | solution.py:24
  198.4 4.3 %collective-permute-done.42 = bf16[768,128]{1,0:T(8,128)(2,1)S(1)} collective-permute-done((bf16[768,128]{1,0:T(8,128)(2,1)S(1)}, bf16[768,128]{1,0:T(8,128)(2,1)S(1)}, u32[]{:S(2)}, u32[]{:S(2)}) %collective-permute-start.42) | collective-permute-done | bytes 196640 | tf_op jit(solution)/shard_map/ppermute | solution.py:24
  203.7 9.3 %shard_map.130 = bf16[256,1536]{1,0:T(8,128)(2,1)S(1)} custom-call(bf16[256,1536]{1,0:T(8,128)(2,1)S(1)} %fusion.9.queries, bf16[256,128]{1,0:T(8,128)(2,1)S(1)} %fusion.15.keys, bf16[256,1536]{1,0:T(8,128)(2,1)S(1)} %constant_dynamic-slice_fusion.2.values, bf16[256,1536]{1,0:T(8,128)(2,1)} %bitcast.rows, s32[256,1]{1,0:T(8,128)S(1)} %copy-done.20, ...), custom_call_target="tpu_custom_call" | custom-call | flops 402653184 | bytes 3145728 | tf_op jit(solution)/shard_map/pallas_call | solution.py:177
  213.0 1.9 shard_map.132
  215.0 2.2 shard_map.134
  217.2 1.8 collective-permute-start.15
  221.2 1.7 collective-permute-start.10
  223.0 1.7 collective-permute-start.16
  225.3 15.1 %collective-permute-done.4.a_ref = bf16[256,1536]{1,0:T(8,128)(2,1)S(1)} collective-permute-done((bf16[256,1536]{1,0:T(8,128)(2,1)S(1)}, bf16[256,1536]{1,0:T(8,128)(2,1)S(1)}, u32[]{:S(2)}, u32[]{:S(2)}) %collective-permute-start.4) | collective-permute-done | bytes 786464 | tf_op jit(solution)/shard_map/ppermute | solution.py:24
  240.4 2.0 collective-permute-done.10.below_in
  245.4 25.8 %collective-permute-done.9.above_in = bf16[256,1536]{1,0:T(8,128)(2,1)} collective-permute-done((bf16[256,1536]{1,0:T(8,128)(2,1)S(1)}, bf16[256,1536]{1,0:T(8,128)(2,1)}, u32[]{:S(2)}, u32[]{:S(2)}) %collective-permute-start.9) | collective-permute-done | bytes 786464 | tf_op jit(solution)/shard_map/ppermute | solution.py:24
  271.6 2.9 collective-permute-start.38
  274.5 2.7 collective-permute-start.6
  277.2 15.0 %collective-permute-done.6.b_ref = bf16[256,1536]{1,0:T(8,128)(2,1)S(1)} collective-permute-done((bf16[256,1536]{1,0:T(8,128)(2,1)S(1)}, bf16[256,1536]{1,0:T(8,128)(2,1)S(1)}, u32[]{:S(2)}, u32[]{:S(2)}) %collective-permute-start.6) | collective-permute-done | bytes 786464 | tf_op jit(solution)/shard_map/ppermute | solution.py:24
  292.3 3.2 collective-permute-start.18
  300.7 25.9 %collective-permute-done.37.rest_4_ = bf16[768,1536]{1,0:T(8,128)(2,1)S(1)} collective-permute-done((bf16[768,1536]{1,0:T(8,128)(2,1)S(1)}, bf16[768,1536]{1,0:T(8,128)(2,1)S(1)}, u32[]{:S(2)}, u32[]{:S(2)}) %collective-permute-start.37) | collective-permute-done | bytes 2359328 | tf_op jit(solution)/shard_map/ppermute | solution.py:24
  326.6 1.7 collective-permute-start.11
  328.3 32.0 %collective-permute-done.17.refs_6_ = bf16[512,1536]{1,0:T(8,128)(2,1)S(1)} collective-permute-done((bf16[512,1536]{1,0:T(8,128)(2,1)S(1)}, bf16[512,1536]{1,0:T(8,128)(2,1)S(1)}, u32[]{:S(2)}, u32[]{:S(2)}) %collective-permute-start.17) | collective-permute-done | bytes 1572896 | tf_op jit(solution)/shard_map/ppermute | solution.py:24
  363.8 1.7 shard_map.131
  365.5 11.2 %shard_map.139.refs_8_ = bf16[3072,1536]{1,0:T(8,128)(2,1)} custom-call(s32[1]{0:T(128)} %bitcast.19.case_ref, f32[2]{0:T(128)S(1)} %pad_maximum_fusion.4.scales, bf16[3072,1536]{1,0:T(8,128)(2,1)} %bitcast.52, bf16[256,3072]{1,0:T(8,128)(2,1)S(1)} %get-tuple-element.72.slope.slope_up.slope_down, bf16[256,1536]{1,0:T(8,128)(2,1)S(1)} %maximum_select_fusion.2.slope_other, ...), custom_call_target="tpu_custom_call" | custom-call | flops 9437184 | bytes 14155776 | tf_op jit(solution)/shard_map/pallas_call | solution.py:353
  378.1 3.7 shard_map.140.refs_8_
  381.8 2.7 shard_map.141
  (228 shorter events, 40.1 us)
Async XLA Ops:
  2.6 22.0 %collective-permute-start.1 = (bf16[272,1536]{1,0:T(8,128)(2,1)S(1)}, bf16[272,1536]{1,0:T(8,128)(2,1)S(1)}, u32[]{:S(2)}, u32[]{:S(2)}) collective-permute-start(bf16[272,1536]{1,0:T(8,128)(2,1)S(1)} %pad_maximum_fusion), channel_id=1, source_target_pairs={{0,1},{1,0},{2,3},{3,2},{4,5},{5,4},{6,7},{7,6},{8,9},{9,8},{10,11... | collective-permute-start | bytes 2506760 | tf_op jit(solution)/shard_map/ppermute | solution.py:28
  48.8 9.2 %collective-permute-start.2 = (bf16[256,128]{1,0:T(8,128)(2,1)S(1)}, bf16[256,128]{1,0:T(8,128)(2,1)S(1)}, u32[]{:S(2)}, u32[]{:S(2)}) collective-permute-start(bf16[256,128]{1,0:T(8,128)(2,1)S(1)} %get-tuple-element.38), channel_id=1, source_target_pairs={{0,1},{1,0},{2,3},{3,2},{4,5},{5,4},{6,7},{7,6},{8,9},{9,8},{10,11... | collective-permute-start | bytes 196616 | tf_op jit(solution)/shard_map/ppermute | solution.py:28
  52.2 21.2 %collective-permute-start.29 = (bf16[128,1536]{1,0:T(8,128)(2,1)S(1)}, bf16[128,1536]{1,0:T(8,128)(2,1)S(1)}, u32[]{:S(2)}, u32[]{:S(2)}) collective-permute-start(bf16[128,1536]{1,0:T(8,128)(2,1)S(1)} %get-tuple-element.58.up), channel_id=1, source_target_pairs={{0,32},{16,48},{32,64},{48,80},{64,96},{80,112},{96,0},{112,16},{1... | collective-permute-start | bytes 1179656 | tf_op jit(solution)/shard_map/ppermute | solution.py:24
  54.1 14.3 %collective-permute-start.23 = (bf16[128,768]{1,0:T(8,128)(2,1)S(1)}, bf16[128,768]{1,0:T(8,128)(2,1)S(1)}, u32[]{:S(2)}, u32[]{:S(2)}) collective-permute-start(bf16[128,768]{1,0:T(8,128)(2,1)S(1)} %get-tuple-element.53.up), channel_id=1, source_target_pairs={{0,32},{16,48},{32,64},{48,80},{64,96},{80,112},{96,0},{112,16},{1... | collective-permute-start | bytes 589832 | tf_op jit(solution)/shard_map/ppermute | solution.py:24
  56.2 30.9 %collective-permute-start.3 = (bf16[256,1536]{1,0:T(8,128)(2,1)S(1)}, bf16[256,1536]{1,0:T(8,128)(2,1)S(1)}, u32[]{:S(2)}, u32[]{:S(2)}) collective-permute-start(bf16[256,1536]{1,0:T(8,128)(2,1)S(1)} %dynamic-slice_convert_fusion), channel_id=1, source_target_pairs={{0,1},{1,0},{2,3},{3,2},{4,5},{5,4},{6,7},{7,6},{8,9},{9,8},{10,11... | collective-permute-start | bytes 2359304 | tf_op jit(solution)/shard_map/ppermute | solution.py:28
  56.6 23.7 %collective-permute-start.30 = (bf16[128,1536]{1,0:T(8,128)(2,1)S(1)}, bf16[128,1536]{1,0:T(8,128)(2,1)S(1)}, u32[]{:S(2)}, u32[]{:S(2)}) collective-permute-start(bf16[128,1536]{1,0:T(8,128)(2,1)S(1)} %get-tuple-element.59.down), channel_id=1, source_target_pairs={{0,96},{16,112},{32,0},{48,16},{64,32},{80,48},{96,64},{112,80},{1... | collective-permute-start | bytes 1179656 | tf_op jit(solution)/shard_map/ppermute | solution.py:24
  58.1 11.6 %collective-permute-start.24 = (bf16[128,768]{1,0:T(8,128)(2,1)S(1)}, bf16[128,768]{1,0:T(8,128)(2,1)S(1)}, u32[]{:S(2)}, u32[]{:S(2)}) collective-permute-start(bf16[128,768]{1,0:T(8,128)(2,1)S(1)} %get-tuple-element.54.down), channel_id=1, source_target_pairs={{0,96},{16,112},{32,0},{48,16},{64,32},{80,48},{96,64},{112,80},{1... | collective-permute-start | bytes 589832 | tf_op jit(solution)/shard_map/ppermute | solution.py:24
  68.4 17.7 %collective-permute-start.22 = (bf16[256,768]{1,0:T(8,128)(2,1)S(1)}, bf16[256,768]{1,0:T(8,128)(2,1)S(1)}, u32[]{:S(2)}, u32[]{:S(2)}) collective-permute-start(bf16[256,768]{1,0:T(8,128)(2,1)S(1)} %constant_dynamic-slice_fusion), channel_id=1, source_target_pairs={{0,16},{16,0},{32,48},{48,32},{64,80},{80,64},{96,112},{112,96},{1... | collective-permute-start | bytes 1179656 | tf_op jit(solution)/shard_map/ppermute | solution.py:28
  69.8 12.9 %collective-permute-start.25 = (bf16[128,768]{1,0:T(8,128)(2,1)S(1)}, bf16[128,768]{1,0:T(8,128)(2,1)S(1)}, u32[]{:S(2)}, u32[]{:S(2)}) collective-permute-start(bf16[128,768]{1,0:T(8,128)(2,1)S(1)} %get-tuple-element.55), channel_id=1, source_target_pairs={{0,96},{16,112},{32,0},{48,16},{64,32},{80,48},{96,64},{112,80},{1... | collective-permute-start | bytes 589832 | tf_op jit(solution)/shard_map/ppermute | solution.py:24
  73.3 9.5 %collective-permute-start.26 = (bf16[128,768]{1,0:T(8,128)(2,1)S(1)}, bf16[128,768]{1,0:T(8,128)(2,1)S(1)}, u32[]{:S(2)}, u32[]{:S(2)}) collective-permute-start(bf16[128,768]{1,0:T(8,128)(2,1)S(1)} %get-tuple-element.56), channel_id=1, source_target_pairs={{0,32},{16,48},{32,64},{48,80},{64,96},{80,112},{96,0},{112,16},{1... | collective-permute-start | bytes 589832 | tf_op jit(solution)/shard_map/ppermute | solution.py:24
  80.4 22.3 %collective-permute-start = (bf16[256,1536]{1,0:T(8,128)(2,1)}, bf16[256,1536]{1,0:T(8,128)(2,1)}, u32[]{:S(2)}, u32[]{:S(2)}) collective-permute-start(bf16[256,1536]{1,0:T(8,128)(2,1)} %bitcast.rows), channel_id=1, source_target_pairs={{0,1},{1,0},{2,3},{3,2},{4,5},{5,4},{6,7},{7,6},{8,9},{9,8},{10,11... | collective-permute-start | bytes 2359304 | tf_op jit(solution)/shard_map/ppermute | solution.py:28
  82.7 41.6 %collective-permute-start.28 = (bf16[256,1536]{1,0:T(8,128)(2,1)S(1)}, bf16[256,1536]{1,0:T(8,128)(2,1)}, u32[]{:S(2)}, u32[]{:S(2)}) collective-permute-start(bf16[256,1536]{1,0:T(8,128)(2,1)S(1)} %get-tuple-element.57.grad), channel_id=1, source_target_pairs={{0,16},{16,0},{32,48},{48,32},{64,80},{80,64},{96,112},{112,96},{1... | collective-permute-start | bytes 2359304 | tf_op jit(solution)/shard_map/ppermute | solution.py:28
  82.8 40.5 %collective-permute-start.31 = (bf16[128,1536]{1,0:T(8,128)(2,1)S(1)}, bf16[128,1536]{1,0:T(8,128)(2,1)}, u32[]{:S(2)}, u32[]{:S(2)}) collective-permute-start(bf16[128,1536]{1,0:T(8,128)(2,1)S(1)} %get-tuple-element.60), channel_id=1, source_target_pairs={{0,96},{16,112},{32,0},{48,16},{64,32},{80,48},{96,64},{112,80},{1... | collective-permute-start | bytes 1179656 | tf_op jit(solution)/shard_map/ppermute | solution.py:24
  86.1 37.3 %collective-permute-start.32 = (bf16[128,1536]{1,0:T(8,128)(2,1)S(1)}, bf16[128,1536]{1,0:T(8,128)(2,1)}, u32[]{:S(2)}, u32[]{:S(2)}) collective-permute-start(bf16[128,1536]{1,0:T(8,128)(2,1)S(1)} %get-tuple-element.61), channel_id=1, source_target_pairs={{0,32},{16,48},{32,64},{48,80},{64,96},{80,112},{96,0},{112,16},{1... | collective-permute-start | bytes 1179656 | tf_op jit(solution)/shard_map/ppermute | solution.py:24
  87.1 40.9 %collective-permute-start.27 = (bf16[256,768]{1,0:T(8,128)(2,1)}, bf16[256,768]{1,0:T(8,128)(2,1)}, u32[]{:S(2)}, u32[]{:S(2)}) collective-permute-start(bf16[256,768]{1,0:T(8,128)(2,1)} %pad_maximum_fusion.2), channel_id=1, source_target_pairs={{0,1},{1,0},{2,3},{3,2},{4,5},{5,4},{6,7},{7,6},{8,9},{9,8},{10,11... | collective-permute-start | bytes 1179656 | tf_op jit(solution)/shard_map/ppermute | solution.py:28
  103.3 15.7 %all-to-all-start = ((f32[16,1,1]{2,1,0:T(1,128)}), f32[16,1,1]{2,1,0:T(1,128)S(1)}, u32[]{:S(2)}, u32[]{:S(2)}) async-start(f32[16,1,1]{2,1,0:T(1,128)} %broadcast_in_dim.35), calls=%async_computation | async-start | bytes 16384 | tf_op jit(solution)/shard_map/all_to_all | solution.py:39
  110.1 18.5 %collective-permute-start.5 = (f32[2,256]{1,0:T(2,128)}, f32[2,256]{1,0:T(2,128)}, u32[]{:S(2)}, u32[]{:S(2)}) collective-permute-start(f32[2,256]{1,0:T(2,128)} %pad_maximum_fusion.3), channel_id=1, source_target_pairs={{0,1},{1,0},{2,3},{3,2},{4,5},{5,4},{6,7},{7,6},{8,9},{9,8},{10,11... | collective-permute-start | bytes 6152 | tf_op jit(solution)/shard_map/ppermute | solution.py:28
  123.3 5.4 %collective-permute-start.19 = (f32[1664]{0:T(1024)S(1)}, f32[1664]{0:T(1024)S(1)}, u32[]{:S(2)}, u32[]{:S(2)}) collective-permute-start(f32[1664]{0:T(1024)S(1)} %concatenate.81), channel_id=1, source_target_pairs={{0,16},{16,0},{32,48},{48,32},{64,80},{80,64},{96,112},{112,96},{1... | collective-permute-start | bytes 19976 | tf_op jit(solution)/shard_map/ppermute | solution.py:28
  123.4 5.3 %collective-permute-start.20 = (f32[1664]{0:T(1024)S(1)}, f32[1664]{0:T(1024)S(1)}, u32[]{:S(2)}, u32[]{:S(2)}) collective-permute-start(f32[1664]{0:T(1024)S(1)} %concatenate.81), channel_id=1, source_target_pairs={{0,32},{16,48},{32,0},{48,16},{64,96},{80,112},{96,64},{112,80},{1... | collective-permute-start | bytes 19976 | tf_op jit(solution)/shard_map/ppermute | solution.py:28
  124.3 7.7 %collective-permute-start.21 = (f32[1664]{0:T(1024)S(1)}, f32[1664]{0:T(1024)S(1)}, u32[]{:S(2)}, u32[]{:S(2)}) collective-permute-start(f32[1664]{0:T(1024)S(1)} %concatenate.81), channel_id=1, source_target_pairs={{0,64},{16,80},{32,96},{48,112},{64,0},{80,16},{96,32},{112,48},{1... | collective-permute-start | bytes 19976 | tf_op jit(solution)/shard_map/ppermute | solution.py:28
  127.9 9.0 %collective-permute-start.40 = (bf16[768,128]{1,0:T(8,128)(2,1)S(1)}, bf16[768,128]{1,0:T(8,128)(2,1)S(1)}, u32[]{:S(2)}, u32[]{:S(2)}) collective-permute-start(bf16[768,128]{1,0:T(8,128)(2,1)S(1)} %get-tuple-element.65.up), channel_id=1, source_target_pairs={{0,32},{16,48},{32,64},{48,80},{64,96},{80,112},{96,0},{112,16},{1... | collective-permute-start | bytes 589832 | tf_op jit(solution)/shard_map/ppermute | solution.py:24
  128.6 91.1 %collective-permute-start.35 = (bf16[768,1536]{1,0:T(8,128)(2,1)}, bf16[768,1536]{1,0:T(8,128)(2,1)S(1)}, u32[]{:S(2)}, u32[]{:S(2)}) collective-permute-start(bf16[768,1536]{1,0:T(8,128)(2,1)} %get-tuple-element.75.up), channel_id=1, source_target_pairs={{0,32},{16,48},{32,64},{48,80},{64,96},{80,112},{96,0},{112,16},{1... | collective-permute-start | bytes 7077896 | tf_op jit(solution)/shard_map/ppermute | solution.py:24
  128.7 94.4 %collective-permute-start.33 = (bf16[768,1536]{1,0:T(8,128)(2,1)}, bf16[768,1536]{1,0:T(8,128)(2,1)S(1)}, u32[]{:S(2)}, u32[]{:S(2)}) collective-permute-start(bf16[768,1536]{1,0:T(8,128)(2,1)} %get-tuple-element.75.up), channel_id=1, source_target_pairs={{0,16},{16,0},{32,48},{48,32},{64,80},{80,64},{96,112},{112,96},{1... | collective-permute-start | bytes 7077896 | tf_op jit(solution)/shard_map/ppermute | solution.py:28
  128.7 92.5 %collective-permute-start.36 = (bf16[768,1536]{1,0:T(8,128)(2,1)}, bf16[768,1536]{1,0:T(8,128)(2,1)S(1)}, u32[]{:S(2)}, u32[]{:S(2)}) collective-permute-start(bf16[768,1536]{1,0:T(8,128)(2,1)} %get-tuple-element.74.down), channel_id=1, source_target_pairs={{0,96},{16,112},{32,0},{48,16},{64,32},{80,48},{96,64},{112,80},{1... | collective-permute-start | bytes 7077896 | tf_op jit(solution)/shard_map/ppermute | solution.py:24
  132.0 92.6 %collective-permute-start.34 = (bf16[768,1536]{1,0:T(8,128)(2,1)}, bf16[768,1536]{1,0:T(8,128)(2,1)S(1)}, u32[]{:S(2)}, u32[]{:S(2)}) collective-permute-start(bf16[768,1536]{1,0:T(8,128)(2,1)} %get-tuple-element.74.down), channel_id=1, source_target_pairs={{0,16},{16,0},{32,48},{48,32},{64,80},{80,64},{96,112},{112,96},{1... | collective-permute-start | bytes 7077896 | tf_op jit(solution)/shard_map/ppermute | solution.py:28
  136.9 50.6 %collective-permute-start.41 = (bf16[768,128]{1,0:T(8,128)(2,1)S(1)}, bf16[768,128]{1,0:T(8,128)(2,1)S(1)}, u32[]{:S(2)}, u32[]{:S(2)}) collective-permute-start(bf16[768,128]{1,0:T(8,128)(2,1)S(1)} %get-tuple-element.66.down), channel_id=1, source_target_pairs={{0,96},{16,112},{32,0},{48,16},{64,32},{80,48},{96,64},{112,80},{1... | collective-permute-start | bytes 589832 | tf_op jit(solution)/shard_map/ppermute | solution.py:24
  136.9 76.1 %slice-start.3 = ((s8[9437184]{0:T(1024)(128)(4,1)}), s8[4194304]{0:T(1024)(128)(4,1)S(1)}, s32[]{:S(2)}) async-start(s8[9437184]{0:T(1024)(128)(4,1)} %bitcast.55), calls=%async_computation.4 | async-start | bytes 8388608
  139.8 73.2 %slice-start.4 = ((s8[9437184]{0:T(1024)(128)(4,1)}), s8[4194304]{0:T(1024)(128)(4,1)S(1)}, s32[]{:S(2)}) async-start(s8[9437184]{0:T(1024)(128)(4,1)} %bitcast.55), calls=%async_computation.5 | async-start | bytes 8388608
  187.6 6.3 %collective-permute-start.39 = (bf16[1536,128]{1,0:T(8,128)(2,1)S(1)}, bf16[1536,128]{1,0:T(8,128)(2,1)S(1)}, u32[]{:S(2)}, u32[]{:S(2)}) collective-permute-start(bf16[1536,128]{1,0:T(8,128)(2,1)S(1)} %copy-done.30), channel_id=1, source_target_pairs={{0,16},{16,0},{32,48},{48,32},{64,80},{80,64},{96,112},{112,96},{1... | collective-permute-start | bytes 1179656 | tf_op jit(solution)/shard_map/ppermute | solution.py:28
  193.9 8.8 %collective-permute-start.42 = (bf16[768,128]{1,0:T(8,128)(2,1)S(1)}, bf16[768,128]{1,0:T(8,128)(2,1)S(1)}, u32[]{:S(2)}, u32[]{:S(2)}) collective-permute-start(bf16[768,128]{1,0:T(8,128)(2,1)S(1)} %get-tuple-element.67), channel_id=1, source_target_pairs={{0,96},{16,112},{32,0},{48,16},{64,32},{80,48},{96,64},{112,80},{1... | collective-permute-start | bytes 589832 | tf_op jit(solution)/shard_map/ppermute | solution.py:24
  202.7 14.5 %collective-permute-start.43 = (bf16[768,128]{1,0:T(8,128)(2,1)S(1)}, bf16[768,128]{1,0:T(8,128)(2,1)S(1)}, u32[]{:S(2)}, u32[]{:S(2)}) collective-permute-start(bf16[768,128]{1,0:T(8,128)(2,1)S(1)} %get-tuple-element.68), channel_id=1, source_target_pairs={{0,32},{16,48},{32,64},{48,80},{64,96},{80,112},{96,0},{112,16},{1... | collective-permute-start | bytes 589832 | tf_op jit(solution)/shard_map/ppermute | solution.py:24
  217.2 57.3 %collective-permute-start.15 = (bf16[512,1536]{1,0:T(8,128)(2,1)S(1)}, bf16[512,1536]{1,0:T(8,128)(2,1)S(1)}, u32[]{:S(2)}, u32[]{:S(2)}) collective-permute-start(bf16[512,1536]{1,0:T(8,128)(2,1)S(1)} %get-tuple-element.48.up.refs_0_), channel_id=1, source_target_pairs={{0,32},{16,48},{32,64},{48,80},{64,96},{80,112},{96,0},{112,16},{1... | collective-permute-start | bytes 4718600 | tf_op jit(solution)/shard_map/ppermute | solution.py:24
  219.7 20.7 %collective-permute-start.4 = (bf16[256,1536]{1,0:T(8,128)(2,1)S(1)}, bf16[256,1536]{1,0:T(8,128)(2,1)S(1)}, u32[]{:S(2)}, u32[]{:S(2)}) collective-permute-start(bf16[256,1536]{1,0:T(8,128)(2,1)S(1)} %shard_map.130), channel_id=1, source_target_pairs={{0,2},{2,4},{4,6},{6,8},{8,10},{10,12},{12,14},{14,0},{1,3},{3,5},... | collective-permute-start | bytes 2359304 | tf_op jit(solution)/shard_map/ppermute | solution.py:24
  221.2 21.2 %collective-permute-start.10 = (bf16[256,1536]{1,0:T(8,128)(2,1)}, bf16[256,1536]{1,0:T(8,128)(2,1)}, u32[]{:S(2)}, u32[]{:S(2)}) collective-permute-start(bf16[256,1536]{1,0:T(8,128)(2,1)} %get-tuple-element.45.down.refs_1_), channel_id=1, source_target_pairs={{0,96},{16,112},{32,0},{48,16},{64,32},{80,48},{96,64},{112,80},{1... | collective-permute-start | bytes 2359304 | tf_op jit(solution)/shard_map/ppermute | solution.py:24
  223.0 54.2 %collective-permute-start.16 = (bf16[512,1536]{1,0:T(8,128)(2,1)S(1)}, bf16[512,1536]{1,0:T(8,128)(2,1)S(1)}, u32[]{:S(2)}, u32[]{:S(2)}) collective-permute-start(bf16[512,1536]{1,0:T(8,128)(2,1)S(1)} %get-tuple-element.49.down.refs_1_), channel_id=1, source_target_pairs={{0,96},{16,112},{32,0},{48,16},{64,32},{80,48},{96,64},{112,80},{1... | collective-permute-start | bytes 4718600 | tf_op jit(solution)/shard_map/ppermute | solution.py:24
  224.7 46.6 %collective-permute-start.9 = (bf16[256,1536]{1,0:T(8,128)(2,1)S(1)}, bf16[256,1536]{1,0:T(8,128)(2,1)}, u32[]{:S(2)}, u32[]{:S(2)}) collective-permute-start(bf16[256,1536]{1,0:T(8,128)(2,1)S(1)} %get-tuple-element.44.up.refs_0_), channel_id=1, source_target_pairs={{0,32},{16,48},{32,64},{48,80},{64,96},{80,112},{96,0},{112,16},{1... | collective-permute-start | bytes 2359304 | tf_op jit(solution)/shard_map/ppermute | solution.py:24
  240.4 51.9 %collective-permute-start.13 = (bf16[512,1536]{1,0:T(8,128)(2,1)S(1)}, bf16[512,1536]{1,0:T(8,128)(2,1)S(1)}, u32[]{:S(2)}, u32[]{:S(2)}) collective-permute-start(bf16[512,1536]{1,0:T(8,128)(2,1)S(1)} %get-tuple-element.48.up.refs_0_), channel_id=1, source_target_pairs={{0,16},{16,0},{32,48},{48,32},{64,80},{80,64},{96,112},{112,96},{1... | collective-permute-start | bytes 4718600 | tf_op jit(solution)/shard_map/ppermute | solution.py:28
  242.5 29.2 %collective-permute-start.44 = (bf16[1536,128]{1,0:T(8,128)(2,1)S(1)}, bf16[1536,128]{1,0:T(8,128)(2,1)S(1)}, u32[]{:S(2)}, u32[]{:S(2)}) collective-permute-start(bf16[1536,128]{1,0:T(8,128)(2,1)S(1)} %multiply_convert_fusion.1), channel_id=1, source_target_pairs={{0,1},{1,0},{2,3},{3,2},{4,5},{5,4},{6,7},{7,6},{8,9},{9,8},{10,11... | collective-permute-start | bytes 1179656 | tf_op jit(solution)/shard_map/ppermute | solution.py:28
  271.3 55.3 %collective-permute-start.37 = (bf16[768,1536]{1,0:T(8,128)(2,1)S(1)}, bf16[768,1536]{1,0:T(8,128)(2,1)S(1)}, u32[]{:S(2)}, u32[]{:S(2)}) collective-permute-start(bf16[768,1536]{1,0:T(8,128)(2,1)S(1)} %get-tuple-element.62.rest_2_), channel_id=1, source_target_pairs={{0,32},{16,48},{32,64},{48,80},{64,96},{80,112},{96,0},{112,16},{1... | collective-permute-start | bytes 7077896 | tf_op jit(solution)/shard_map/ppermute | solution.py:24
  271.6 55.0 %collective-permute-start.38 = (bf16[768,1536]{1,0:T(8,128)(2,1)S(1)}, bf16[768,1536]{1,0:T(8,128)(2,1)S(1)}, u32[]{:S(2)}, u32[]{:S(2)}) collective-permute-start(bf16[768,1536]{1,0:T(8,128)(2,1)S(1)} %get-tuple-element.63.rest_3_), channel_id=1, source_target_pairs={{0,96},{16,112},{32,0},{48,16},{64,32},{80,48},{96,64},{112,80},{1... | collective-permute-start | bytes 7077896 | tf_op jit(solution)/shard_map/ppermute | solution.py:24
  274.5 17.8 %collective-permute-start.6 = (bf16[256,1536]{1,0:T(8,128)(2,1)S(1)}, bf16[256,1536]{1,0:T(8,128)(2,1)S(1)}, u32[]{:S(2)}, u32[]{:S(2)}) collective-permute-start(bf16[256,1536]{1,0:T(8,128)(2,1)S(1)} %add_convert_fusion), channel_id=1, source_target_pairs={{0,14},{2,0},{4,2},{6,4},{8,6},{10,8},{12,10},{14,12},{1,15},{3,1}... | collective-permute-start | bytes 2359304 | tf_op jit(solution)/shard_map/ppermute | solution.py:24
  277.2 22.2 %collective-permute-start.14 = (bf16[512,1536]{1,0:T(8,128)(2,1)S(1)}, bf16[512,1536]{1,0:T(8,128)(2,1)S(1)}, u32[]{:S(2)}, u32[]{:S(2)}) collective-permute-start(bf16[512,1536]{1,0:T(8,128)(2,1)S(1)} %get-tuple-element.49.down.refs_1_), channel_id=1, source_target_pairs={{0,16},{16,0},{32,48},{48,32},{64,80},{80,64},{96,112},{112,96},{1... | collective-permute-start | bytes 4718600 | tf_op jit(solution)/shard_map/ppermute | solution.py:28
  292.3 68.0 %collective-permute-start.17 = (bf16[512,1536]{1,0:T(8,128)(2,1)S(1)}, bf16[512,1536]{1,0:T(8,128)(2,1)S(1)}, u32[]{:S(2)}, u32[]{:S(2)}) collective-permute-start(bf16[512,1536]{1,0:T(8,128)(2,1)S(1)} %get-tuple-element.50.refs_4_), channel_id=1, source_target_pairs={{0,32},{16,48},{32,64},{48,80},{64,96},{80,112},{96,0},{112,16},{1... | collective-permute-start | bytes 4718600 | tf_op jit(solution)/shard_map/ppermute | solution.py:24
  292.3 84.4 %collective-permute-start.18 = (bf16[512,1536]{1,0:T(8,128)(2,1)S(1)}, bf16[512,1536]{1,0:T(8,128)(2,1)}, u32[]{:S(2)}, u32[]{:S(2)}) collective-permute-start(bf16[512,1536]{1,0:T(8,128)(2,1)S(1)} %get-tuple-element.51.refs_5_), channel_id=1, source_target_pairs={{0,96},{16,112},{32,0},{48,16},{64,32},{80,48},{96,64},{112,80},{1... | collective-permute-start | bytes 4718600 | tf_op jit(solution)/shard_map/ppermute | solution.py:24
  300.7 81.1 %collective-permute-start.7 = (bf16[256,1536]{1,0:T(8,128)(2,1)S(1)}, bf16[256,1536]{1,0:T(8,128)(2,1)}, u32[]{:S(2)}, u32[]{:S(2)}) collective-permute-start(bf16[256,1536]{1,0:T(8,128)(2,1)S(1)} %get-tuple-element.44.up.refs_0_), channel_id=1, source_target_pairs={{0,16},{16,0},{32,48},{48,32},{64,80},{80,64},{96,112},{112,96},{1... | collective-permute-start | bytes 2359304 | tf_op jit(solution)/shard_map/ppermute | solution.py:28
  326.6 55.2 %collective-permute-start.8 = (bf16[256,1536]{1,0:T(8,128)(2,1)}, bf16[256,1536]{1,0:T(8,128)(2,1)}, u32[]{:S(2)}, u32[]{:S(2)}) collective-permute-start(bf16[256,1536]{1,0:T(8,128)(2,1)} %get-tuple-element.45.down.refs_1_), channel_id=1, source_target_pairs={{0,16},{16,0},{32,48},{48,32},{64,80},{80,64},{96,112},{112,96},{1... | collective-permute-start | bytes 2359304 | tf_op jit(solution)/shard_map/ppermute | solution.py:28
  326.6 55.2 %collective-permute-start.11 = (bf16[256,1536]{1,0:T(8,128)(2,1)}, bf16[256,1536]{1,0:T(8,128)(2,1)}, u32[]{:S(2)}, u32[]{:S(2)}) collective-permute-start(bf16[256,1536]{1,0:T(8,128)(2,1)} %get-tuple-element.46.refs_4_), channel_id=1, source_target_pairs={{0,32},{16,48},{32,64},{48,80},{64,96},{80,112},{96,0},{112,16},{1... | collective-permute-start | bytes 2359304 | tf_op jit(solution)/shard_map/ppermute | solution.py:24
  360.3 21.5 %collective-permute-start.12 = (bf16[256,1536]{1,0:T(8,128)(2,1)}, bf16[256,1536]{1,0:T(8,128)(2,1)}, u32[]{:S(2)}, u32[]{:S(2)}) collective-permute-start(bf16[256,1536]{1,0:T(8,128)(2,1)} %get-tuple-element.47.refs_5_), channel_id=1, source_target_pairs={{0,96},{16,112},{32,0},{48,16},{64,32},{80,48},{96,64},{112,80},{1... | collective-permute-start | bytes 2359304 | tf_op jit(solution)/shard_map/ppermute | solution.py:24
  (53 other events, 889.0 us)

commit v2 on v1

--- a/solution.py
+++ b/solution.py
@@ -16,6 +16,8 @@
 LEARN_RATE = 0.2
 MASK_FILL = -1e30
 BLOCK = 256
+EDGE = 128
+TOGETHER = 2
 STRIP = 512
 
 
@@ -138,30 +140,38 @@
     return (expo / jnp.sum(expo, axis=-1, keepdims=True)).astype(jnp.bfloat16)
 
 
+def head_columns():
+    return [slice(head * HEAD, (head + 1) * HEAD) for head in range(TOGETHER)]
+
+
 def onward_kernel(queries, keys, values, rows, tall, wide, out):
-    probs = head_probs(queries[...], keys[...], tall[...], wide[...])
-    mixed = dot(probs, values[...], ROWS_COLS)
-    out[...] = (rows[...].astype(jnp.float32) + mixed).astype(jnp.bfloat16)
+    for cols in head_columns():
+        probs = head_probs(queries[:, cols], keys[...], tall[...], wide[...])
+        mixed = dot(probs, values[:, cols], ROWS_COLS)
+        out[:, cols] = (rows[:, cols].astype(jnp.float32) + mixed).astype(jnp.bfloat16)
 
 
 def back_kernel(queries, keys, values, grads, tall, wide, query_grad, value_grad, key_part, total):
-    head = pl.program_id(0)
-
-    @pl.when(head == 0)
+    group = pl.program_id(0)
+
+    @pl.when(group == 0)
     def _():
         total[...] = jnp.zeros_like(total)
 
-    query, key, grad = queries[...], keys[...], grads[...]
-    probs = head_probs(query, key, tall[...], wide[...])
-    prob_f = probs.astype(jnp.float32)
-    value_grad[...] = dot(probs, grad, FIRST_FIRST)
-    prob_grad = dot(grad, values[...], LAST_LAST)
-    inner = jnp.sum(prob_grad * prob_f, axis=-1, keepdims=True)
-    score_grad = (prob_f * (prob_grad - inner) * HEAD ** (-0.5)).astype(jnp.bfloat16)
-    query_grad[...] = dot(score_grad, key, ROWS_COLS).astype(jnp.bfloat16)
-    total[...] += dot(score_grad, query, FIRST_FIRST)
-
-    @pl.when(head == pl.num_programs(0) - 1)
+    key, terms = keys[...], []
+    for cols in head_columns():
+        query, grad = queries[:, cols], grads[:, cols]
+        probs = head_probs(query, key, tall[...], wide[...])
+        prob_f = probs.astype(jnp.float32)
+        value_grad[:, cols] = dot(probs, grad, FIRST_FIRST)
+        prob_grad = dot(grad, values[:, cols], LAST_LAST)
+        inner = jnp.sum(prob_grad * prob_f, axis=-1, keepdims=True)
+        score_grad = (prob_f * (prob_grad - inner) * HEAD ** (-0.5)).astype(jnp.bfloat16)
+        query_grad[:, cols] = dot(score_grad, key, ROWS_COLS).astype(jnp.bfloat16)
+        terms.append(dot(score_grad, query, FIRST_FIRST))
+    total[...] += sum(terms)
+
+    @pl.when(group == pl.num_programs(0) - 1)
     def _():
         key_part[...] = total[...].astype(jnp.bfloat16)
 
@@ -169,14 +179,14 @@
 def per_head(kernel, caption, queries, keys, extras, outs, products):
     count, width = queries.shape
     heads = width // HEAD
-    by_head = pl.BlockSpec((count, HEAD), lambda h: (0, h))
+    by_head = pl.BlockSpec((count, TOGETHER * HEAD), lambda h: (0, h))
     fixed = pl.BlockSpec((count, HEAD), lambda h: (0, 0))
     specs = [by_head, fixed] + [by_head] * len(extras)
     specs += [pl.BlockSpec((count, 1), lambda h: (0, 0)), pl.BlockSpec((1, count), lambda h: (0, 0))]
     backward = len(outs) > 1
     return pl.pallas_call(
         kernel,
-        grid=(heads,),
+        grid=(heads // TOGETHER,),
         in_specs=specs,
         out_specs=[by_head if shape[1] == width else fixed for shape, kind in outs],
         out_shape=[jax.ShapeDtypeStruct(shape, kind) for shape, kind in outs],
@@ -234,6 +244,49 @@
     return at
 
 
+def cut_kernel(weights, up, down, held, sems):
+    rows, base = up.shape[0], weights.shape[0] // 2
+    pieces = [
+        (half, pl.ds(half * base + start, BLOCK), pl.ds(start, BLOCK))
+        for start in range(0, rows, BLOCK)
+        for half in range(2)
+    ]
+    loads = [
+        pltpu.make_async_copy(weights.at[there], held.at[half, here], sems.at[0, number])
+        for number, (half, there, here) in enumerate(pieces)
+    ]
+    stores = [
+        pltpu.make_async_copy(held.at[half, here], (up, down)[half].at[here], sems.at[1, number])
+        for number, (half, there, here) in enumerate(pieces)
+    ]
+    for load in loads:
+        load.start()
+    for load, store in zip(loads, stores):
+        load.wait()
+        store.start()
+    for store in stores:
+        store.wait()
+
+
+def cut_out(weights, rows):
+    columns = weights.shape[1]
+    anywhere = pl.BlockSpec(memory_space=pl.ANY)
+    return pl.pallas_call(
+        cut_kernel,
+        in_specs=[anywhere],
+        out_specs=[anywhere] * 2,
+        out_shape=[jax.ShapeDtypeStruct((rows, columns), weights.dtype)] * 2,
+        scratch_shapes=[
+            pltpu.VMEM((2, rows, columns), weights.dtype),
+            pltpu.SemaphoreType.DMA((2, 2 * rows // BLOCK)),
+        ],
+        cost_estimate=pl.CostEstimate(
+            flops=0, bytes_accessed=8 * rows * columns, transcendentals=0
+        ),
+        compiler_params=pltpu.CompilerParams(vmem_limit_bytes=56 << 20),
+    )(weights)
+
+
 def renew_kernel(scale, up, down, slope_up, slope_down, grad, out_up, out_down):
     step_up = stepped(slope_up[...].T, grad, scale[0])
     step_down = stepped(slope_down[...].T, grad, scale[0])
@@ -247,9 +300,9 @@
 
 def renewed(scale, weights, slope, grad, begin, end):
     rows, columns = weights.shape
-    depth, base = slope.shape[0], rows // (2 * BLOCK)
-    first, blocks = begin // BLOCK, (end - begin) // BLOCK
-    block = (BLOCK, columns)
+    depth, base = slope.shape[0], rows // (2 * EDGE)
+    first, blocks = begin // EDGE, (end - begin) // EDGE
+    block = (EDGE, columns)
     shape = jax.ShapeDtypeStruct((end - begin, columns), weights.dtype)
     size = (end - begin) * columns
     return pl.pallas_call(
@@ -259,8 +312,8 @@
             pl.BlockSpec(memory_space=pltpu.SMEM),
             pl.BlockSpec(block, lambda i: (first + i, 0)),
             pl.BlockSpec(block, lambda i: (base + first + i, 0)),
-            pl.BlockSpec((depth, BLOCK), lambda i: (0, first + i)),
-            pl.BlockSpec((depth, BLOCK), lambda i: (0, base + first + i)),
+            pl.BlockSpec((depth, EDGE), lambda i: (0, first + i)),
+            pl.BlockSpec((depth, EDGE), lambda i: (0, base + first + i)),
             pl.BlockSpec((depth, columns), lambda i: (0, 0)),
         ],
         out_specs=[pl.BlockSpec(block, lambda i: (i, 0))] * 2,
@@ -268,7 +321,7 @@
         cost_estimate=pl.CostEstimate(
             flops=4 * size * depth, bytes_accessed=8 * size, transcendentals=0
         ),
-        compiler_params=pltpu.CompilerParams(vmem_limit_bytes=24 << 20),
+        compiler_params=pltpu.CompilerParams(vmem_limit_bytes=56 << 20),
     )(scale, weights, weights, slope, slope, grad)
 
 
@@ -493,8 +546,8 @@
     width = query_weight.shape[0]
     in_scale = width ** (-0.5)
     half, early_rows = width // 2, width // 4
-    cuts = ((early_rows, half - BLOCK), (half - BLOCK, half))
-    parts = query_weight[:early_rows], query_weight[half : half + early_rows]
+    cuts = ((early_rows, half - EDGE), (half - EDGE, half))
+    parts = cut_out(query_weight, early_rows)
     sent = gossip.first(*parts)
     near = [flipped(part, "rep", 0) for part in parts]
 
@@ -569,7 +622,7 @@
     grad_key = weight_grad(own_values_b, key_grad)
     local_squares = query_squares + jnp.sum(grad_gain * grad_gain)
     fwd_other = flipped(fwd_rows, "tp", 0)
-    fwd_other, local_squares = lax.optimization_barrier((fwd_other, local_squares))
+    fwd_other, _ = lax.optimization_barrier((fwd_other, local_squares))
     fwd_full = in_order(fwd_rows, fwd_other, low, 1)
     _, _, _, normed = normalize(fwd_full, gain_full)
     own_values = lax.dynamic_slice_in_dim(normed, offset, local_width, 1)

time: 386 us -> 394 us (1.021)
  starting transfers between devices: 65.6 us -> 60.4 us
  matrix products: 17.9 us -> 22.3 us
    pallas_call x2, Pallas kernels: 4.13 us -> 10.9 us  [renewed(): pl.pallas_call(renew_kernel, grid=(blocks,), in_specs=[pl.BlockSpec(memor...]
    ppermute x26, starting transfers between devices: 39.7 us -> 33.5 us  [from_behind(): lax.ppermute(shard, axis, [(i, (i + by) % length) for i in range(length)])]
    dot_general x4, matrix products: 10 us -> 15.7 us  [projected(): product = jnp.dot(normed, weight, preferred_element_type=jnp.float32)]
    slice x1 -> x0, local copies, waits for them, and re-layouts: 5.24 us -> none  [section(): parts = (query_weight[:early_rows], query_weight[half:half + early_rows])]
    unnamed x110 -> x134, local copies, waits for them, and re-layouts: 8.53 us -> 13.3 us
    pallas_call x2 -> x3, Pallas kernels: 22 us -> 18.4 us  [the longest x2 14.4 us: per_head(): pl.pallas_call(kernel, grid=(heads // TOGETHER,), in_specs=specs, out_spe...]
  transfers between devices with their start and end apart: 46 -> 46, of which waited for: 13 -> 12; matrix products, arithmetic and copies ran while one was open for 10% -> 9% of each run, Pallas kernels for 9% -> 11%
where the time goes in v2:
time: 394 us; the launch traced here: 393 us
  waiting for transfers between devices  207 us (53%)
  starting transfers between devices  60.4 us (15%)
  Pallas kernels  55.7 us (14%)
  other arithmetic  25.9 us (7%)
  matrix products  22.3 us (6%)
  local copies, waits for them, and re-layouts  17.1 us (4%)
  between operations  4.51 us (1%)
    ppermute x26, waiting for transfers between devices, from_behind(): lax.ppermute(shard, axis, [(i, (i + by) % length) for i in range(length)])  186 us
    ppermute x26, starting transfers between devices, from_behind(): lax.ppermute(shard, axis, [(i, (i + by) % length) for i in range(length)])  33.5 us
    ppermute x19, waiting for transfers between devices, flipped(): lax.ppermute(block, axis, [(i, i ^ 1 << bit) for i in range(lax.axis_size...  20.8 us
    ppermute x19, starting transfers between devices, flipped(): lax.ppermute(block, axis, [(i, i ^ 1 << bit) for i in range(lax.axis_size...  18.7 us
    dot_general x4, matrix products, projected(): product = jnp.dot(normed, weight, preferred_element_type=jnp.float32)  15.7 us
    pallas_call x2, Pallas kernels, per_head(): pl.pallas_call(kernel, grid=(heads // TOGETHER,), in_specs=specs, out_spe...  14.4 us
    unnamed x134, local copies, waits for them, and re-layouts  13.3 us
    pallas_call x1, Pallas kernels, averaged(): pl.pallas_call(kernel, grid_spec=pltpu.PrefetchScalarGridSpec(num_scalar_...  11.2 us
  transfers between devices with their start and end apart: 46, of which 12 were waited for; matrix products, arithmetic and copies ran while one was open for 9% of the time, Pallas kernels for 11%

profile of v2, /device:TPU:0, one launch (start us, length us, event | category | flops | bytes accessed | tf_op | source)
XLA Modules:
  0.0 393.0 jit_solution(13113846419307406984)
XLA Ops:
  2.6 3.4 collective-permute-start.1
  7.4 4.0 %shard_map.138 = (bf16[768,1536]{1,0:T(8,128)(2,1)}, bf16[768,1536]{1,0:T(8,128)(2,1)}) custom-call(bf16[3072,1536]{1,0:T(8,128)(2,1)} %bitcast.58), custom_call_target="tpu_custom_call" | custom-call | bytes 9437184 | tf_op jit(solution)/shard_map/pallas_call | solution.py:274
  12.2 12.4 %collective-permute-done.1 = bf16[272,1536]{1,0:T(8,128)(2,1)S(1)} collective-permute-done((bf16[272,1536]{1,0:T(8,128)(2,1)S(1)}, bf16[272,1536]{1,0:T(8,128)(2,1)S(1)}, u32[]{:S(2)}, u32[]{:S(2)}) %collective-permute-start.1) | collective-permute-done | bytes 835616 | tf_op jit(solution)/shard_map/ppermute | solution.py:30
  26.7 8.3 %fusion.8.queries = bf16[256,1536]{1,0:T(8,128)(2,1)S(1)} fusion(bf16[256,3072]{1,0:T(8,128)(2,1)S(1)} %get-tuple-element.74.slope.slope_up.slope_down, bf16[1,1,3072,1536]{3,2,1,0:T(8,128)(2,1)} %param.14), kind=kOutput, calls=%fused_computation.17 | convolution fusion | flops 2416705536 | bytes 11796480 | tf_op jit(solution)/shard_map/dot_general | solution.py:124
  37.3 8.4 %shard_map.128 = (bf16[256,1536]{1,0:T(8,128)(2,1)S(1)}, f32[256,1536]{1,0:T(8,128)S(1)}, bf16[256,128]{1,0:T(8,128)(2,1)S(1)}) custom-call(bf16[256,1536]{1,0:T(8,128)(2,1)S(1)} %fusion.8.queries, bf16[256,128]{1,0:T(8,128)(2,1)S(1)} %fusion.14.keys, bf16[256,1536]{1,0:T(8,128)(2,1)S(1)} %constant_dynamic-slice_fusion.3.values, ...), custom_call_target="tpu_custom_call" | custom-call | flops 1006632960 | bytes 4718592 | tf_op jit(solution)/shard_map/pallas_call | solution.py:187
  45.8 2.7 convolution_multiply_fusion
  48.6 3.3 collective-permute-start.2
  51.9 1.9 collective-permute-start.29
  53.9 2.0 collective-permute-start.23
  58.6 9.5 %collective-permute-done.23.above_in = bf16[128,768]{1,0:T(8,128)(2,1)S(1)} collective-permute-done((bf16[128,768]{1,0:T(8,128)(2,1)S(1)}, bf16[128,768]{1,0:T(8,128)(2,1)S(1)}, u32[]{:S(2)}, u32[]{:S(2)}) %collective-permute-start.23) | collective-permute-done | bytes 196640 | tf_op jit(solution)/shard_map/ppermute | solution.py:26
  69.5 2.6 collective-permute-start.25
  72.1 6.4 %shard_map.129 = f32[1,1]{1,0:T(1,128)} custom-call(bf16[256,3072]{1,0:T(8,128)(2,1)S(1)} %get-tuple-element.74.slope.slope_up.slope_down, bf16[256,1536]{1,0:T(8,128)(2,1)S(1)} %get-tuple-element.57.grad, bf16[256,128]{1,0:T(8,128)(2,1)S(1)} %add_convert_fusion.2.key_grad), custom_call_target="tpu_custom_call" | custom-call | flops 2617245696 | bytes 2359296 | tf_op jit(solution)/shard_map/pallas_call | solution.py:489
  79.2 3.3 collective-permute-start
  82.6 3.3 collective-permute-start.31
  87.2 2.5 multiply_reduce_fusion
  92.1 8.2 %all-to-all-start = ((f32[16,1,1]{2,1,0:T(1,128)}), f32[16,1,1]{2,1,0:T(1,128)}, u32[]{:S(2)}, u32[]{:S(2)}) async-start(f32[16,1,1]{2,1,0:T(1,128)} %broadcast_in_dim.35), calls=%async_computation | async-start | bytes 16384 | tf_op jit(solution)/shard_map/all_to_all | solution.py:41
  101.6 3.4 collective-permute-start.5
  105.0 1.9 convert_reduce_fusion
  107.4 2.1 fusion.4
  115.5 2.9 collective-permute-start.41
  119.4 3.4 collective-permute-start.21
  122.8 3.1 shard_map.132
  126.1 3.2 collective-permute-start.36
  129.8 2.3 fusion.6
  132.2 56.9 %collective-permute-done.10.below_in = bf16[128,1536]{1,0:T(8,128)(2,1)S(1)} collective-permute-done((bf16[128,1536]{1,0:T(8,128)(2,1)}, bf16[128,1536]{1,0:T(8,128)(2,1)S(1)}, u32[]{:S(2)}, u32[]{:S(2)}) %collective-permute-start.10) | collective-permute-done | bytes 393248 | tf_op jit(solution)/shard_map/ppermute | solution.py:26
  189.5 6.3 %fusion.9.queries = bf16[256,1536]{1,0:T(8,128)(2,1)S(1)} fusion(bf16[256,3072]{1,0:T(8,128)(2,1)S(1)} %fusion.6, bf16[1,1,3072,1536]{3,2,1,0:T(8,128)(2,1)} %param.14), kind=kOutput, calls=%fused_computation.18 | convolution fusion | flops 2416705536 | bytes 11796480 | tf_op jit(solution)/shard_map/dot_general | solution.py:124
  195.9 6.0 %collective-permute-done.9.above_in = bf16[128,1536]{1,0:T(8,128)(2,1)S(1)} collective-permute-done((bf16[128,1536]{1,0:T(8,128)(2,1)S(1)}, bf16[128,1536]{1,0:T(8,128)(2,1)S(1)}, u32[]{:S(2)}, u32[]{:S(2)}) %collective-permute-start.9) | collective-permute-done | bytes 393248 | tf_op jit(solution)/shard_map/ppermute | solution.py:26
  201.9 1.7 collective-permute-start.42
  204.2 3.5 collective-permute-done.42
  208.3 6.0 %shard_map.130 = bf16[256,1536]{1,0:T(8,128)(2,1)S(1)} custom-call(bf16[256,1536]{1,0:T(8,128)(2,1)S(1)} %fusion.9.queries, bf16[256,128]{1,0:T(8,128)(2,1)S(1)} %fusion.15.keys, bf16[256,1536]{1,0:T(8,128)(2,1)S(1)} %constant_dynamic-slice_fusion.2.values, bf16[256,1536]{1,0:T(8,128)(2,1)S(1)} %bitcast.52, s32[256,1]{1,0:T(8,128)S(1)} %copy-done.26, ...), custom_call_target="tpu_custom_call" | custom-call | flops 402653184 | bytes 3145728 | tf_op jit(solution)/shard_map/pallas_call | solution.py:187
  215.2 7.8 %shard_map.134 = (bf16[640,1536]{1,0:T(8,128)(2,1)}, bf16[640,1536]{1,0:T(8,128)(2,1)}) custom-call(f32[1]{0:T(128)} %bitcast.20.scale, bf16[3072,1536]{1,0:T(8,128)(2,1)} %bitcast.61, bf16[3072,1536]{1,0:T(8,128)(2,1)} %bitcast.62, bf16[256,3072]{1,0:T(8,128)(2,1)} %copy-done, bf16[256,3072]{1,0:T(8,128)(2,1)} %copy-done, bf16[256,1536]{1,0:T(8,128)(2,1)} %copy-done.2), custom_call_target="tpu_custom_call" | custom-call | flops 1006632960 | bytes 7864320 | tf_op jit(solution)/shard_map/pallas_call | solution.py:308
  224.4 2.7 collective-permute-start.16
  231.5 2.3 add_convert_fusion
  233.9 13.6 %collective-permute-done.4.a_ref = bf16[256,1536]{1,0:T(8,128)(2,1)S(1)} collective-permute-done((bf16[256,1536]{1,0:T(8,128)(2,1)S(1)}, bf16[256,1536]{1,0:T(8,128)(2,1)S(1)}, u32[]{:S(2)}, u32[]{:S(2)}) %collective-permute-start.4) | collective-permute-done | bytes 786464 | tf_op jit(solution)/shard_map/ppermute | solution.py:26
  248.0 8.4 %collective-permute-done.44 = bf16[1536,128]{1,0:T(8,128)(2,1)S(1)} collective-permute-done((bf16[1536,128]{1,0:T(8,128)(2,1)S(1)}, bf16[1536,128]{1,0:T(8,128)(2,1)S(1)}, u32[]{:S(2)}, u32[]{:S(2)}) %collective-permute-start.44) | collective-permute-done | bytes 393248 | tf_op jit(solution)/shard_map/ppermute | solution.py:30
  256.4 13.8 %collective-permute-done.15.above_in = bf16[640,1536]{1,0:T(8,128)(2,1)S(1)} collective-permute-done((bf16[640,1536]{1,0:T(8,128)(2,1)}, bf16[640,1536]{1,0:T(8,128)(2,1)S(1)}, u32[]{:S(2)}, u32[]{:S(2)}) %collective-permute-start.15) | collective-permute-done | bytes 1966112 | tf_op jit(solution)/shard_map/ppermute | solution.py:26
  270.3 1.6 collective-permute-start.38
  272.9 2.4 collective-permute-start.18
  281.0 39.9 %collective-permute-done.37.rest_4_ = bf16[768,1536]{1,0:T(8,128)(2,1)S(1)} collective-permute-done((bf16[768,1536]{1,0:T(8,128)(2,1)S(1)}, bf16[768,1536]{1,0:T(8,128)(2,1)S(1)}, u32[]{:S(2)}, u32[]{:S(2)}) %collective-permute-start.37) | collective-permute-done | bytes 2359328 | tf_op jit(solution)/shard_map/ppermute | solution.py:26
  320.8 3.6 collective-permute-done.38.rest_5_
  324.8 38.1 %collective-permute-done.17.refs_6_ = bf16[640,1536]{1,0:T(8,128)(2,1)S(1)} collective-permute-done((bf16[640,1536]{1,0:T(8,128)(2,1)S(1)}, bf16[640,1536]{1,0:T(8,128)(2,1)S(1)}, u32[]{:S(2)}, u32[]{:S(2)}) %collective-permute-start.17) | collective-permute-done | bytes 1966112 | tf_op jit(solution)/shard_map/ppermute | solution.py:26
  364.3 1.6 collective-permute-start.12
  368.3 1.7 shard_map.131
  370.0 11.2 %shard_map.140.refs_8_ = bf16[3072,1536]{1,0:T(8,128)(2,1)} custom-call(s32[1]{0:T(128)} %bitcast.19.case_ref, f32[2]{0:T(128)S(1)} %pad_maximum_fusion.4.scales, bf16[3072,1536]{1,0:T(8,128)(2,1)} %bitcast.63, bf16[256,3072]{1,0:T(8,128)(2,1)S(1)} %copy-done.1, bf16[256,1536]{1,0:T(8,128)(2,1)S(1)} %maximum_select_fusion.2.slope_other, ...), custom_call_target="tpu_custom_call" | custom-call | flops 9437184 | bytes 14155776 | tf_op jit(solution)/shard_map/pallas_call | solution.py:406
  382.7 1.5 copy-done.10
  384.2 1.5 copy-done.12
  385.8 4.7 %shard_map.141.refs_8_ = bf16[3072,1536]{1,0:T(8,128)(2,1)} custom-call(s32[1]{0:T(128)} %bitcast.19.case_ref, bf16[640,1536]{1,0:T(8,128)(2,1)S(1)} %copy-done.5, bf16[640,1536]{1,0:T(8,128)(2,1)S(1)} %copy-done.6, bf16[640,1536]{1,0:T(8,128)(2,1)S(1)} %copy-done.8, bf16[640,1536]{1,0:T(8,128)(2,1)S(1)} %copy-done.10, ...), custom_call_target="tpu_custom_call", output_to_operand_aliasing={{}: (9, {})} | custom-call | flops 3932160 | bytes 11796480 | tf_op jit(solution)/shard_map/pallas_call | solution.py:441
  390.6 2.3 shard_map.142
  (251 shorter events, 45.0 us)
Async XLA Ops:
  2.6 22.0 %collective-permute-start.1 = (bf16[272,1536]{1,0:T(8,128)(2,1)S(1)}, bf16[272,1536]{1,0:T(8,128)(2,1)S(1)}, u32[]{:S(2)}, u32[]{:S(2)}) collective-permute-start(bf16[272,1536]{1,0:T(8,128)(2,1)S(1)} %pad_maximum_fusion), channel_id=1, source_target_pairs={{0,1},{1,0},{2,3},{3,2},{4,5},{5,4},{6,7},{7,6},{8,9},{9,8},{10,11... | collective-permute-start | bytes 2506760 | tf_op jit(solution)/shard_map/ppermute | solution.py:30
  26.7 60.5 %copy-start.29 = (f32[256,3072]{1,0:T(8,128)}, f32[256,3072]{1,0:T(8,128)S(1)}, u32[]{:S(2)}) copy-start(f32[256,3072]{1,0:T(8,128)S(1)} %get-tuple-element.75) | copy-start | bytes 9437188
  26.7 85.4 %copy-start = (bf16[256,3072]{1,0:T(8,128)(2,1)}, bf16[256,3072]{1,0:T(8,128)(2,1)S(1)}, u32[]{:S(2)}) copy-start(bf16[256,3072]{1,0:T(8,128)(2,1)S(1)} %get-tuple-element.74.slope.slope_up.slope_down) | copy-start | bytes 4718596
  48.6 9.1 %collective-permute-start.2 = (bf16[256,128]{1,0:T(8,128)(2,1)S(1)}, bf16[256,128]{1,0:T(8,128)(2,1)S(1)}, u32[]{:S(2)}, u32[]{:S(2)}) collective-permute-start(bf16[256,128]{1,0:T(8,128)(2,1)S(1)} %get-tuple-element.39), channel_id=1, source_target_pairs={{0,1},{1,0},{2,3},{3,2},{4,5},{5,4},{6,7},{7,6},{8,9},{9,8},{10,11... | collective-permute-start | bytes 196616 | tf_op jit(solution)/shard_map/ppermute | solution.py:30
  51.9 20.2 %collective-permute-start.29 = (bf16[128,1536]{1,0:T(8,128)(2,1)S(1)}, bf16[128,1536]{1,0:T(8,128)(2,1)S(1)}, u32[]{:S(2)}, u32[]{:S(2)}) collective-permute-start(bf16[128,1536]{1,0:T(8,128)(2,1)S(1)} %get-tuple-element.58.up), channel_id=1, source_target_pairs={{0,32},{16,48},{32,64},{48,80},{64,96},{80,112},{96,0},{112,16},{1... | collective-permute-start | bytes 1179656 | tf_op jit(solution)/shard_map/ppermute | solution.py:26
  53.9 14.3 %collective-permute-start.23 = (bf16[128,768]{1,0:T(8,128)(2,1)S(1)}, bf16[128,768]{1,0:T(8,128)(2,1)S(1)}, u32[]{:S(2)}, u32[]{:S(2)}) collective-permute-start(bf16[128,768]{1,0:T(8,128)(2,1)S(1)} %get-tuple-element.53.up), channel_id=1, source_target_pairs={{0,32},{16,48},{32,64},{48,80},{64,96},{80,112},{96,0},{112,16},{1... | collective-permute-start | bytes 589832 | tf_op jit(solution)/shard_map/ppermute | solution.py:26
  55.9 30.9 %collective-permute-start.3 = (bf16[256,1536]{1,0:T(8,128)(2,1)S(1)}, bf16[256,1536]{1,0:T(8,128)(2,1)S(1)}, u32[]{:S(2)}, u32[]{:S(2)}) collective-permute-start(bf16[256,1536]{1,0:T(8,128)(2,1)S(1)} %dynamic-slice_convert_fusion), channel_id=1, source_target_pairs={{0,1},{1,0},{2,3},{3,2},{4,5},{5,4},{6,7},{7,6},{8,9},{9,8},{10,11... | collective-permute-start | bytes 2359304 | tf_op jit(solution)/shard_map/ppermute | solution.py:30
  56.3 22.8 %collective-permute-start.30 = (bf16[128,1536]{1,0:T(8,128)(2,1)S(1)}, bf16[128,1536]{1,0:T(8,128)(2,1)}, u32[]{:S(2)}, u32[]{:S(2)}) collective-permute-start(bf16[128,1536]{1,0:T(8,128)(2,1)S(1)} %get-tuple-element.59.down), channel_id=1, source_target_pairs={{0,96},{16,112},{32,0},{48,16},{64,32},{80,48},{96,64},{112,80},{1... | collective-permute-start | bytes 1179656 | tf_op jit(solution)/shard_map/ppermute | solution.py:26
  57.7 11.8 %collective-permute-start.24 = (bf16[128,768]{1,0:T(8,128)(2,1)S(1)}, bf16[128,768]{1,0:T(8,128)(2,1)S(1)}, u32[]{:S(2)}, u32[]{:S(2)}) collective-permute-start(bf16[128,768]{1,0:T(8,128)(2,1)S(1)} %get-tuple-element.54.down), channel_id=1, source_target_pairs={{0,96},{16,112},{32,0},{48,16},{64,32},{80,48},{96,64},{112,80},{1... | collective-permute-start | bytes 589832 | tf_op jit(solution)/shard_map/ppermute | solution.py:26
  68.1 17.7 %collective-permute-start.22 = (bf16[256,768]{1,0:T(8,128)(2,1)S(1)}, bf16[256,768]{1,0:T(8,128)(2,1)S(1)}, u32[]{:S(2)}, u32[]{:S(2)}) collective-permute-start(bf16[256,768]{1,0:T(8,128)(2,1)S(1)} %constant_dynamic-slice_fusion), channel_id=1, source_target_pairs={{0,16},{16,0},{32,48},{48,32},{64,80},{80,64},{96,112},{112,96},{1... | collective-permute-start | bytes 1179656 | tf_op jit(solution)/shard_map/ppermute | solution.py:30
  69.5 13.0 %collective-permute-start.25 = (bf16[128,768]{1,0:T(8,128)(2,1)S(1)}, bf16[128,768]{1,0:T(8,128)(2,1)S(1)}, u32[]{:S(2)}, u32[]{:S(2)}) collective-permute-start(bf16[128,768]{1,0:T(8,128)(2,1)S(1)} %get-tuple-element.55), channel_id=1, source_target_pairs={{0,96},{16,112},{32,0},{48,16},{64,32},{80,48},{96,64},{112,80},{1... | collective-permute-start | bytes 589832 | tf_op jit(solution)/shard_map/ppermute | solution.py:26
  72.1 10.5 %collective-permute-start.26 = (bf16[128,768]{1,0:T(8,128)(2,1)S(1)}, bf16[128,768]{1,0:T(8,128)(2,1)S(1)}, u32[]{:S(2)}, u32[]{:S(2)}) collective-permute-start(bf16[128,768]{1,0:T(8,128)(2,1)S(1)} %get-tuple-element.56), channel_id=1, source_target_pairs={{0,32},{16,48},{32,64},{48,80},{64,96},{80,112},{96,0},{112,16},{1... | collective-permute-start | bytes 589832 | tf_op jit(solution)/shard_map/ppermute | solution.py:26
  79.2 22.5 %collective-permute-start = (bf16[256,1536]{1,0:T(8,128)(2,1)S(1)}, bf16[256,1536]{1,0:T(8,128)(2,1)}, u32[]{:S(2)}, u32[]{:S(2)}) collective-permute-start(bf16[256,1536]{1,0:T(8,128)(2,1)S(1)} %bitcast.48), channel_id=1, source_target_pairs={{0,1},{1,0},{2,3},{3,2},{4,5},{5,4},{6,7},{7,6},{8,9},{9,8},{10,11... | collective-permute-start | bytes 2359304 | tf_op jit(solution)/shard_map/ppermute | solution.py:30
  82.5 36.7 %collective-permute-start.28 = (bf16[256,1536]{1,0:T(8,128)(2,1)S(1)}, bf16[256,1536]{1,0:T(8,128)(2,1)}, u32[]{:S(2)}, u32[]{:S(2)}) collective-permute-start(bf16[256,1536]{1,0:T(8,128)(2,1)S(1)} %get-tuple-element.57.grad), channel_id=1, source_target_pairs={{0,16},{16,0},{32,48},{48,32},{64,80},{80,64},{96,112},{112,96},{1... | collective-permute-start | bytes 2359304 | tf_op jit(solution)/shard_map/ppermute | solution.py:30
  82.6 32.5 %collective-permute-start.31 = (bf16[128,1536]{1,0:T(8,128)(2,1)}, bf16[128,1536]{1,0:T(8,128)(2,1)}, u32[]{:S(2)}, u32[]{:S(2)}) collective-permute-start(bf16[128,1536]{1,0:T(8,128)(2,1)} %get-tuple-element.60), channel_id=1, source_target_pairs={{0,96},{16,112},{32,0},{48,16},{64,32},{80,48},{96,64},{112,80},{1... | collective-permute-start | bytes 1179656 | tf_op jit(solution)/shard_map/ppermute | solution.py:26
  85.9 29.6 %collective-permute-start.32 = (bf16[128,1536]{1,0:T(8,128)(2,1)S(1)}, bf16[128,1536]{1,0:T(8,128)(2,1)}, u32[]{:S(2)}, u32[]{:S(2)}) collective-permute-start(bf16[128,1536]{1,0:T(8,128)(2,1)S(1)} %get-tuple-element.61), channel_id=1, source_target_pairs={{0,32},{16,48},{32,64},{48,80},{64,96},{80,112},{96,0},{112,16},{1... | collective-permute-start | bytes 1179656 | tf_op jit(solution)/shard_map/ppermute | solution.py:26
  86.8 32.4 %collective-permute-start.27 = (bf16[256,768]{1,0:T(8,128)(2,1)}, bf16[256,768]{1,0:T(8,128)(2,1)}, u32[]{:S(2)}, u32[]{:S(2)}) collective-permute-start(bf16[256,768]{1,0:T(8,128)(2,1)} %pad_maximum_fusion.2), channel_id=1, source_target_pairs={{0,1},{1,0},{2,3},{3,2},{4,5},{5,4},{6,7},{7,6},{8,9},{9,8},{10,11... | collective-permute-start | bytes 1179656 | tf_op jit(solution)/shard_map/ppermute | solution.py:30
  92.1 17.9 %all-to-all-start = ((f32[16,1,1]{2,1,0:T(1,128)}), f32[16,1,1]{2,1,0:T(1,128)}, u32[]{:S(2)}, u32[]{:S(2)}) async-start(f32[16,1,1]{2,1,0:T(1,128)} %broadcast_in_dim.35), calls=%async_computation | async-start | bytes 16384 | tf_op jit(solution)/shard_map/all_to_all | solution.py:41
  101.6 17.7 %collective-permute-start.5 = (f32[2,256]{1,0:T(2,128)}, f32[2,256]{1,0:T(2,128)}, u32[]{:S(2)}, u32[]{:S(2)}) collective-permute-start(f32[2,256]{1,0:T(2,128)} %pad_maximum_fusion.3), channel_id=1, source_target_pairs={{0,1},{1,0},{2,3},{3,2},{4,5},{5,4},{6,7},{7,6},{8,9},{9,8},{10,11... | collective-permute-start | bytes 6152 | tf_op jit(solution)/shard_map/ppermute | solution.py:30
  115.1 14.2 %collective-permute-start.40 = (bf16[768,128]{1,0:T(8,128)(2,1)}, bf16[768,128]{1,0:T(8,128)(2,1)}, u32[]{:S(2)}, u32[]{:S(2)}) collective-permute-start(bf16[768,128]{1,0:T(8,128)(2,1)} %get-tuple-element.67.up), channel_id=1, source_target_pairs={{0,32},{16,48},{32,64},{48,80},{64,96},{80,112},{96,0},{112,16},{1... | collective-permute-start | bytes 589832 | tf_op jit(solution)/shard_map/ppermute | solution.py:26
  115.5 14.0 %collective-permute-start.41 = (bf16[768,128]{1,0:T(8,128)(2,1)}, bf16[768,128]{1,0:T(8,128)(2,1)S(1)}, u32[]{:S(2)}, u32[]{:S(2)}) collective-permute-start(bf16[768,128]{1,0:T(8,128)(2,1)} %get-tuple-element.68.down), channel_id=1, source_target_pairs={{0,96},{16,112},{32,0},{48,16},{64,32},{80,48},{96,64},{112,80},{1... | collective-permute-start | bytes 589832 | tf_op jit(solution)/shard_map/ppermute | solution.py:26
  119.1 6.7 %collective-permute-start.19 = (f32[1664]{0:T(1024)S(1)}, f32[1664]{0:T(1024)S(1)}, u32[]{:S(2)}, u32[]{:S(2)}) collective-permute-start(f32[1664]{0:T(1024)S(1)} %concatenate.81), channel_id=1, source_target_pairs={{0,16},{16,0},{32,48},{48,32},{64,80},{80,64},{96,112},{112,96},{1... | collective-permute-start | bytes 19976 | tf_op jit(solution)/shard_map/ppermute | solution.py:30
  119.2 6.7 %collective-permute-start.20 = (f32[1664]{0:T(1024)S(1)}, f32[1664]{0:T(1024)S(1)}, u32[]{:S(2)}, u32[]{:S(2)}) collective-permute-start(f32[1664]{0:T(1024)S(1)} %concatenate.81), channel_id=1, source_target_pairs={{0,32},{16,48},{32,0},{48,16},{64,96},{80,112},{96,64},{112,80},{1... | collective-permute-start | bytes 19976 | tf_op jit(solution)/shard_map/ppermute | solution.py:30
  119.4 6.7 %collective-permute-start.21 = (f32[1664]{0:T(1024)S(1)}, f32[1664]{0:T(1024)S(1)}, u32[]{:S(2)}, u32[]{:S(2)}) collective-permute-start(f32[1664]{0:T(1024)S(1)} %concatenate.81), channel_id=1, source_target_pairs={{0,64},{16,80},{32,96},{48,112},{64,0},{80,16},{96,32},{112,48},{1... | collective-permute-start | bytes 19976 | tf_op jit(solution)/shard_map/ppermute | solution.py:30
  125.9 98.6 %collective-permute-start.35 = (bf16[768,1536]{1,0:T(8,128)(2,1)}, bf16[768,1536]{1,0:T(8,128)(2,1)S(1)}, u32[]{:S(2)}, u32[]{:S(2)}) collective-permute-start(bf16[768,1536]{1,0:T(8,128)(2,1)} %get-tuple-element.62.up), channel_id=1, source_target_pairs={{0,32},{16,48},{32,64},{48,80},{64,96},{80,112},{96,0},{112,16},{1... | collective-permute-start | bytes 7077896 | tf_op jit(solution)/shard_map/ppermute | solution.py:26
  126.0 103.8 %collective-permute-start.33 = (bf16[768,1536]{1,0:T(8,128)(2,1)}, bf16[768,1536]{1,0:T(8,128)(2,1)}, u32[]{:S(2)}, u32[]{:S(2)}) collective-permute-start(bf16[768,1536]{1,0:T(8,128)(2,1)} %get-tuple-element.62.up), channel_id=1, source_target_pairs={{0,16},{16,0},{32,48},{48,32},{64,80},{80,64},{96,112},{112,96},{1... | collective-permute-start | bytes 7077896 | tf_op jit(solution)/shard_map/ppermute | solution.py:30
  126.1 102.1 %collective-permute-start.36 = (bf16[768,1536]{1,0:T(8,128)(2,1)}, bf16[768,1536]{1,0:T(8,128)(2,1)S(1)}, u32[]{:S(2)}, u32[]{:S(2)}) collective-permute-start(bf16[768,1536]{1,0:T(8,128)(2,1)} %get-tuple-element.63.down), channel_id=1, source_target_pairs={{0,96},{16,112},{32,0},{48,16},{64,32},{80,48},{96,64},{112,80},{1... | collective-permute-start | bytes 7077896 | tf_op jit(solution)/shard_map/ppermute | solution.py:26
  129.3 2.8 collective-permute-start.39
  129.4 59.7 %collective-permute-start.10 = (bf16[128,1536]{1,0:T(8,128)(2,1)}, bf16[128,1536]{1,0:T(8,128)(2,1)S(1)}, u32[]{:S(2)}, u32[]{:S(2)}) collective-permute-start(bf16[128,1536]{1,0:T(8,128)(2,1)} %get-tuple-element.45.down.refs_1_), channel_id=1, source_target_pairs={{0,96},{16,112},{32,0},{48,16},{64,32},{80,48},{96,64},{112,80},{1... | collective-permute-start | bytes 1179656 | tf_op jit(solution)/shard_map/ppermute | solution.py:26
  132.1 98.7 %collective-permute-start.34 = (bf16[768,1536]{1,0:T(8,128)(2,1)}, bf16[768,1536]{1,0:T(8,128)(2,1)}, u32[]{:S(2)}, u32[]{:S(2)}) collective-permute-start(bf16[768,1536]{1,0:T(8,128)(2,1)} %get-tuple-element.63.down), channel_id=1, source_target_pairs={{0,16},{16,0},{32,48},{48,32},{64,80},{80,64},{96,112},{112,96},{1... | collective-permute-start | bytes 7077896 | tf_op jit(solution)/shard_map/ppermute | solution.py:30
  189.1 12.7 %collective-permute-start.9 = (bf16[128,1536]{1,0:T(8,128)(2,1)S(1)}, bf16[128,1536]{1,0:T(8,128)(2,1)S(1)}, u32[]{:S(2)}, u32[]{:S(2)}) collective-permute-start(bf16[128,1536]{1,0:T(8,128)(2,1)S(1)} %copy-done.13), channel_id=1, source_target_pairs={{0,32},{16,48},{32,64},{48,80},{64,96},{80,112},{96,0},{112,16},{1... | collective-permute-start | bytes 1179656 | tf_op jit(solution)/shard_map/ppermute | solution.py:26
  201.9 5.8 %collective-permute-start.42 = (bf16[768,128]{1,0:T(8,128)(2,1)S(1)}, bf16[768,128]{1,0:T(8,128)(2,1)S(1)}, u32[]{:S(2)}, u32[]{:S(2)}) collective-permute-start(bf16[768,128]{1,0:T(8,128)(2,1)S(1)} %get-tuple-element.69), channel_id=1, source_target_pairs={{0,96},{16,112},{32,0},{48,16},{64,32},{80,48},{96,64},{112,80},{1... | collective-permute-start | bytes 589832 | tf_op jit(solution)/shard_map/ppermute | solution.py:26
  207.7 15.4 %collective-permute-start.43 = (bf16[768,128]{1,0:T(8,128)(2,1)}, bf16[768,128]{1,0:T(8,128)(2,1)}, u32[]{:S(2)}, u32[]{:S(2)}) collective-permute-start(bf16[768,128]{1,0:T(8,128)(2,1)} %get-tuple-element.70), channel_id=1, source_target_pairs={{0,32},{16,48},{32,64},{48,80},{64,96},{80,112},{96,0},{112,16},{1... | collective-permute-start | bytes 589832 | tf_op jit(solution)/shard_map/ppermute | solution.py:26
  223.1 47.2 %collective-permute-start.15 = (bf16[640,1536]{1,0:T(8,128)(2,1)}, bf16[640,1536]{1,0:T(8,128)(2,1)S(1)}, u32[]{:S(2)}, u32[]{:S(2)}) collective-permute-start(bf16[640,1536]{1,0:T(8,128)(2,1)} %get-tuple-element.48.up.refs_0_), channel_id=1, source_target_pairs={{0,32},{16,48},{32,64},{48,80},{64,96},{80,112},{96,0},{112,16},{1... | collective-permute-start | bytes 5898248 | tf_op jit(solution)/shard_map/ppermute | solution.py:26
  224.4 47.4 %collective-permute-start.16 = (bf16[640,1536]{1,0:T(8,128)(2,1)}, bf16[640,1536]{1,0:T(8,128)(2,1)S(1)}, u32[]{:S(2)}, u32[]{:S(2)}) collective-permute-start(bf16[640,1536]{1,0:T(8,128)(2,1)} %get-tuple-element.49.down.refs_1_), channel_id=1, source_target_pairs={{0,96},{16,112},{32,0},{48,16},{64,32},{80,48},{96,64},{112,80},{1... | collective-permute-start | bytes 5898248 | tf_op jit(solution)/shard_map/ppermute | solution.py:26
  228.2 19.3 %collective-permute-start.4 = (bf16[256,1536]{1,0:T(8,128)(2,1)S(1)}, bf16[256,1536]{1,0:T(8,128)(2,1)S(1)}, u32[]{:S(2)}, u32[]{:S(2)}) collective-permute-start(bf16[256,1536]{1,0:T(8,128)(2,1)S(1)} %copy-done.24), channel_id=1, source_target_pairs={{0,2},{2,4},{4,6},{6,8},{8,10},{10,12},{12,14},{14,0},{1,3},{3,5},... | collective-permute-start | bytes 2359304 | tf_op jit(solution)/shard_map/ppermute | solution.py:26
  229.7 43.2 %collective-permute-start.13 = (bf16[640,1536]{1,0:T(8,128)(2,1)}, bf16[640,1536]{1,0:T(8,128)(2,1)S(1)}, u32[]{:S(2)}, u32[]{:S(2)}) collective-permute-start(bf16[640,1536]{1,0:T(8,128)(2,1)} %get-tuple-element.48.up.refs_0_), channel_id=1, source_target_pairs={{0,16},{16,0},{32,48},{48,32},{64,80},{80,64},{96,112},{112,96},{1... | collective-permute-start | bytes 5898248 | tf_op jit(solution)/shard_map/ppermute | solution.py:30
  230.9 25.6 %collective-permute-start.44 = (bf16[1536,128]{1,0:T(8,128)(2,1)S(1)}, bf16[1536,128]{1,0:T(8,128)(2,1)S(1)}, u32[]{:S(2)}, u32[]{:S(2)}) collective-permute-start(bf16[1536,128]{1,0:T(8,128)(2,1)S(1)} %multiply_convert_fusion.1), channel_id=1, source_target_pairs={{0,1},{1,0},{2,3},{3,2},{4,5},{5,4},{6,7},{7,6},{8,9},{9,8},{10,11... | collective-permute-start | bytes 1179656 | tf_op jit(solution)/shard_map/ppermute | solution.py:30
  247.5 24.4 %collective-permute-start.6 = (bf16[256,1536]{1,0:T(8,128)(2,1)S(1)}, bf16[256,1536]{1,0:T(8,128)(2,1)S(1)}, u32[]{:S(2)}, u32[]{:S(2)}) collective-permute-start(bf16[256,1536]{1,0:T(8,128)(2,1)S(1)} %add_convert_fusion), channel_id=1, source_target_pairs={{0,14},{2,0},{4,2},{6,4},{8,6},{10,8},{12,10},{14,12},{1,15},{3,1}... | collective-permute-start | bytes 2359304 | tf_op jit(solution)/shard_map/ppermute | solution.py:26
  256.4 64.4 %collective-permute-start.37 = (bf16[768,1536]{1,0:T(8,128)(2,1)S(1)}, bf16[768,1536]{1,0:T(8,128)(2,1)S(1)}, u32[]{:S(2)}, u32[]{:S(2)}) collective-permute-start(bf16[768,1536]{1,0:T(8,128)(2,1)S(1)} %get-tuple-element.64.rest_2_), channel_id=1, source_target_pairs={{0,32},{16,48},{32,64},{48,80},{64,96},{80,112},{96,0},{112,16},{1... | collective-permute-start | bytes 7077896 | tf_op jit(solution)/shard_map/ppermute | solution.py:26
  270.3 54.1 %collective-permute-start.38 = (bf16[768,1536]{1,0:T(8,128)(2,1)S(1)}, bf16[768,1536]{1,0:T(8,128)(2,1)S(1)}, u32[]{:S(2)}, u32[]{:S(2)}) collective-permute-start(bf16[768,1536]{1,0:T(8,128)(2,1)S(1)} %get-tuple-element.65.rest_3_), channel_id=1, source_target_pairs={{0,96},{16,112},{32,0},{48,16},{64,32},{80,48},{96,64},{112,80},{1... | collective-permute-start | bytes 7077896 | tf_op jit(solution)/shard_map/ppermute | solution.py:26
  271.9 7.8 %collective-permute-start.14 = (bf16[640,1536]{1,0:T(8,128)(2,1)S(1)}, bf16[640,1536]{1,0:T(8,128)(2,1)S(1)}, u32[]{:S(2)}, u32[]{:S(2)}) collective-permute-start(bf16[640,1536]{1,0:T(8,128)(2,1)S(1)} %copy-done.6), channel_id=1, source_target_pairs={{0,16},{16,0},{32,48},{48,32},{64,80},{80,64},{96,112},{112,96},{1... | collective-permute-start | bytes 5898248 | tf_op jit(solution)/shard_map/ppermute | solution.py:30
  272.0 91.0 %collective-permute-start.17 = (bf16[640,1536]{1,0:T(8,128)(2,1)S(1)}, bf16[640,1536]{1,0:T(8,128)(2,1)S(1)}, u32[]{:S(2)}, u32[]{:S(2)}) collective-permute-start(bf16[640,1536]{1,0:T(8,128)(2,1)S(1)} %get-tuple-element.50.refs_4_), channel_id=1, source_target_pairs={{0,32},{16,48},{32,64},{48,80},{64,96},{80,112},{96,0},{112,16},{1... | collective-permute-start | bytes 5898248 | tf_op jit(solution)/shard_map/ppermute | solution.py:26
  272.9 108.2 %collective-permute-start.18 = (bf16[640,1536]{1,0:T(8,128)(2,1)S(1)}, bf16[640,1536]{1,0:T(8,128)(2,1)}, u32[]{:S(2)}, u32[]{:S(2)}) collective-permute-start(bf16[640,1536]{1,0:T(8,128)(2,1)S(1)} %get-tuple-element.51.refs_5_), channel_id=1, source_target_pairs={{0,96},{16,112},{32,0},{48,16},{64,32},{80,48},{96,64},{112,80},{1... | collective-permute-start | bytes 5898248 | tf_op jit(solution)/shard_map/ppermute | solution.py:26
  281.0 109.5 %collective-permute-start.7 = (bf16[128,1536]{1,0:T(8,128)(2,1)S(1)}, bf16[128,1536]{1,0:T(8,128)(2,1)S(1)}, u32[]{:S(2)}, u32[]{:S(2)}) collective-permute-start(bf16[128,1536]{1,0:T(8,128)(2,1)S(1)} %copy-done.13), channel_id=1, source_target_pairs={{0,16},{16,0},{32,48},{48,32},{64,80},{80,64},{96,112},{112,96},{1... | collective-permute-start | bytes 1179656 | tf_op jit(solution)/shard_map/ppermute | solution.py:30
  320.8 69.7 %collective-permute-start.8 = (bf16[128,1536]{1,0:T(8,128)(2,1)S(1)}, bf16[128,1536]{1,0:T(8,128)(2,1)}, u32[]{:S(2)}, u32[]{:S(2)}) collective-permute-start(bf16[128,1536]{1,0:T(8,128)(2,1)S(1)} %copy-done.14), channel_id=1, source_target_pairs={{0,16},{16,0},{32,48},{48,32},{64,80},{80,64},{96,112},{112,96},{1... | collective-permute-start | bytes 1179656 | tf_op jit(solution)/shard_map/ppermute | solution.py:30
  324.4 66.1 %collective-permute-start.11 = (bf16[128,1536]{1,0:T(8,128)(2,1)S(1)}, bf16[128,1536]{1,0:T(8,128)(2,1)}, u32[]{:S(2)}, u32[]{:S(2)}) collective-permute-start(bf16[128,1536]{1,0:T(8,128)(2,1)S(1)} %get-tuple-element.46.refs_4_), channel_id=1, source_target_pairs={{0,32},{16,48},{32,64},{48,80},{64,96},{80,112},{96,0},{112,16},{1... | collective-permute-start | bytes 1179656 | tf_op jit(solution)/shard_map/ppermute | solution.py:26
  364.3 26.3 %collective-permute-start.12 = (bf16[128,1536]{1,0:T(8,128)(2,1)S(1)}, bf16[128,1536]{1,0:T(8,128)(2,1)}, u32[]{:S(2)}, u32[]{:S(2)}) collective-permute-start(bf16[128,1536]{1,0:T(8,128)(2,1)S(1)} %get-tuple-element.47.refs_5_), channel_id=1, source_target_pairs={{0,96},{16,112},{32,0},{48,16},{64,32},{80,48},{96,64},{112,80},{1... | collective-permute-start | bytes 1179656 | tf_op jit(solution)/shard_map/ppermute | solution.py:26
  (65 other events, 681.2 us)

commit v3 on v2

--- a/solution.py
+++ b/solution.py
@@ -17,8 +17,7 @@
 MASK_FILL = -1e30
 BLOCK = 256
 EDGE = 128
-TOGETHER = 2
-STRIP = 512
+STRIP = 256
 
 
 def from_behind(shard, axis, by):
@@ -140,12 +139,12 @@
     return (expo / jnp.sum(expo, axis=-1, keepdims=True)).astype(jnp.bfloat16)
 
 
-def head_columns():
-    return [slice(head * HEAD, (head + 1) * HEAD) for head in range(TOGETHER)]
+def head_columns(ref):
+    return [slice(begin, begin + HEAD) for begin in range(0, ref.shape[1], HEAD)]
 
 
 def onward_kernel(queries, keys, values, rows, tall, wide, out):
-    for cols in head_columns():
+    for cols in head_columns(queries):
         probs = head_probs(queries[:, cols], keys[...], tall[...], wide[...])
         mixed = dot(probs, values[:, cols], ROWS_COLS)
         out[:, cols] = (rows[:, cols].astype(jnp.float32) + mixed).astype(jnp.bfloat16)
@@ -159,7 +158,7 @@
         total[...] = jnp.zeros_like(total)
 
     key, terms = keys[...], []
-    for cols in head_columns():
+    for cols in head_columns(queries):
         query, grad = queries[:, cols], grads[:, cols]
         probs = head_probs(query, key, tall[...], wide[...])
         prob_f = probs.astype(jnp.float32)
@@ -179,14 +178,15 @@
 def per_head(kernel, caption, queries, keys, extras, outs, products):
     count, width = queries.shape
     heads = width // HEAD
-    by_head = pl.BlockSpec((count, TOGETHER * HEAD), lambda h: (0, h))
+    backward = len(outs) > 1
+    together = 2 if backward else 1
+    by_head = pl.BlockSpec((count, together * HEAD), lambda h: (0, h))
     fixed = pl.BlockSpec((count, HEAD), lambda h: (0, 0))
     specs = [by_head, fixed] + [by_head] * len(extras)
     specs += [pl.BlockSpec((count, 1), lambda h: (0, 0)), pl.BlockSpec((1, count), lambda h: (0, 0))]
-    backward = len(outs) > 1
     return pl.pallas_call(
         kernel,
-        grid=(heads // TOGETHER,),
+        grid=(heads // together,),
         in_specs=specs,
         out_specs=[by_head if shape[1] == width else fixed for shape, kind in outs],
         out_shape=[jax.ShapeDtypeStruct(shape, kind) for shape, kind in outs],
@@ -244,10 +244,10 @@
     return at
 
 
-def cut_kernel(weights, up, down, held, sems):
+def cut_kernel(begin, weights, up, down, held, sems):
     rows, base = up.shape[0], weights.shape[0] // 2
     pieces = [
-        (half, pl.ds(half * base + start, BLOCK), pl.ds(start, BLOCK))
+        (half, pl.ds(half * base + begin + start, BLOCK), pl.ds(start, BLOCK))
         for start in range(0, rows, BLOCK)
         for half in range(2)
     ]
@@ -268,11 +268,11 @@
         store.wait()
 
 
-def cut_out(weights, rows):
-    columns = weights.shape[1]
+def cut_out(weights, begin, end):
+    rows, columns = end - begin, weights.shape[1]
     anywhere = pl.BlockSpec(memory_space=pl.ANY)
     return pl.pallas_call(
-        cut_kernel,
+        partial(cut_kernel, begin),
         in_specs=[anywhere],
         out_specs=[anywhere] * 2,
         out_shape=[jax.ShapeDtypeStruct((rows, columns), weights.dtype)] * 2,
@@ -384,7 +384,7 @@
     def near_map(wanted):
         def index(half, i, case_ref):
             used = (half == wanted) & (case_ref[0] == 0)
-            return (jnp.where(used, i, 0), 0)
+            return (jnp.where(used, wanted * base + first + i, 0), 0)
 
         return index
 
@@ -418,20 +418,21 @@
     )(*operands)
 
 
-def averaged_weights(case, scales, weights, slopes, grads, sources, end, out):
+def averaged_weights(case, scales, weights, slopes, grads, sources, begin, end, out):
     rows, columns = weights.shape
-    depth, base, short = slopes[0].shape[0], rows // (2 * BLOCK), end // BLOCK
+    depth, base, short = slopes[0].shape[0], rows // (2 * BLOCK), slopes[1].shape[1] // (2 * BLOCK)
+    first = begin // BLOCK
     fixed = pl.BlockSpec((depth, columns), lambda half, i, case_ref: (0, 0))
     own_specs = [
         pl.BlockSpec(memory_space=pltpu.SMEM),
-        pl.BlockSpec((BLOCK, columns), lambda half, i, case_ref: (half * base + i, 0)),
-        pl.BlockSpec((depth, BLOCK), lambda half, i, case_ref: (0, half * base + i)),
-        pl.BlockSpec((depth, BLOCK), lambda half, i, case_ref: (0, half * short + i)),
+        pl.BlockSpec((BLOCK, columns), lambda half, i, case_ref: (half * base + first + i, 0)),
+        pl.BlockSpec((depth, BLOCK), lambda half, i, case_ref: (0, half * base + first + i)),
+        pl.BlockSpec((depth, BLOCK), lambda half, i, case_ref: (0, half * short + first + i)),
         fixed,
         fixed,
     ]
     own = (scales, weights, *slopes, *grads)
-    return averaged(average_kernel, case, own, own_specs, sources, 0, end, weights.shape, out)
+    return averaged(average_kernel, case, own, own_specs, sources, begin, end, weights.shape, out)
 
 
 def averaged_updates(case, own, sources, begin, end, shape, out):
@@ -547,9 +548,11 @@
     in_scale = width ** (-0.5)
     half, early_rows = width // 2, width // 4
     cuts = ((early_rows, half - EDGE), (half - EDGE, half))
-    parts = cut_out(query_weight, early_rows)
-    sent = gossip.first(*parts)
-    near = [flipped(part, "rep", 0) for part in parts]
+    pieces, sent = ((0, BLOCK), (BLOCK, early_rows)), []
+    for begin, end in pieces:
+        parts = cut_out(query_weight, begin, end)
+        sent.append(gossip.first(*parts))
+    near = flipped(query_weight, "rep", 0)
 
     beside = jnp.broadcast_to(gain_local[None], (16, local_width))
     other = flipped(jnp.concatenate([bwd_rows, beside], axis=0), "tp", 0)
@@ -666,18 +669,23 @@
         later = gossip.second(state)
         news.append((new, (*new_near, *later)))
 
-    sources = (*near, *gossip.second(sent))
+    passed = []
+    for state in sent:
+        passed.append((near, near, *gossip.second(state)))
     next_rows, prev_rows = settled(next_rows, prev_rows)
-    query_out = averaged_weights(
-        gossip.case,
-        jnp.stack([inverse, inverse_partner]),
-        query_weight,
-        (normed_b, normed_partner),
-        (query_grad, query_grad_partner),
-        sources,
-        early_rows,
-        None,
-    )
+    query_out = None
+    for number, (begin, end) in enumerate(pieces):
+        query_out = averaged_weights(
+            gossip.case,
+            jnp.stack([inverse, inverse_partner]),
+            query_weight,
+            (normed_b, normed_partner),
+            (query_grad, query_grad_partner),
+            passed[number],
+            begin,
+            end,
+            query_out,
+        )
     for number, (begin, end) in enumerate(cuts):
         query_out = averaged_updates(
             gossip.case, *news[number], begin, end, query_weight.shape, query_out

time: 394 us -> 352 us (0.89)
  waiting for transfers between devices: 207 us -> 149 us
  Pallas kernels: 55.7 us -> 67.5 us
  starting transfers between devices: 60.4 us -> 67.3 us
    ppermute x26 -> x30, waiting for transfers between devices: 186 us -> 133 us  [from_behind(): lax.ppermute(shard, axis, [(i, (i + by) % length) for i in range(length)])]
    ppermute x26 -> x30, starting transfers between devices: 33.5 us -> 48.2 us  [from_behind(): lax.ppermute(shard, axis, [(i, (i + by) % length) for i in range(length)])]
    pallas_call x1 -> x2, Pallas kernels: 11.2 us -> 16.4 us  [averaged(): pl.pallas_call(kernel, grid_spec=pltpu.PrefetchScalarGridSpec(num_scalar_...]
    ppermute x19 -> x18, waiting for transfers between devices: 20.8 us -> 15.7 us  [flipped(): lax.ppermute(block, axis, [(i, i ^ 1 << bit) for i in range(lax.axis_size...]
    ppermute x19 -> x18, starting transfers between devices: 18.7 us -> 13.8 us  [flipped(): lax.ppermute(block, axis, [(i, i ^ 1 << bit) for i in range(lax.axis_size...]
    unnamed x134 -> x108, local copies, waits for them, and re-layouts: 13.3 us -> 8.69 us
    pallas_call x3 -> x4, Pallas kernels: 18.4 us -> 21 us  [the longest x2 15.8 us: per_head(): pl.pallas_call(kernel, grid=(heads // together,), in_specs=specs, out_spe...]
  transfers between devices with their start and end apart: 46 -> 49, of which waited for: 12 -> 16; matrix products, arithmetic and copies ran while one was open for 9% -> 15% of each run, Pallas kernels for 11% -> 19%
where the time goes in v3:
time: 352 us; the launch traced here: 351 us
  waiting for transfers between devices  149 us (42%)
  Pallas kernels  67.5 us (19%)
  starting transfers between devices  67.3 us (19%)
  matrix products  25.3 us (7%)
  other arithmetic  22.6 us (6%)
  local copies, waits for them, and re-layouts  14.7 us (4%)
  between operations  4.49 us (1%)
    ppermute x30, waiting for transfers between devices, from_behind(): lax.ppermute(shard, axis, [(i, (i + by) % length) for i in range(length)])  133 us
    ppermute x30, starting transfers between devices, from_behind(): lax.ppermute(shard, axis, [(i, (i + by) % length) for i in range(length)])  48.2 us
    pallas_call x2, Pallas kernels, averaged(): pl.pallas_call(kernel, grid_spec=pltpu.PrefetchScalarGridSpec(num_scalar_...  16.4 us
    pallas_call x2, Pallas kernels, per_head(): pl.pallas_call(kernel, grid=(heads // together,), in_specs=specs, out_spe...  15.8 us
    ppermute x18, waiting for transfers between devices, flipped(): lax.ppermute(block, axis, [(i, i ^ 1 << bit) for i in range(lax.axis_size...  15.7 us
    dot_general x4, matrix products, projected(): product = jnp.dot(normed, weight, preferred_element_type=jnp.float32)  15.4 us
    ppermute x18, starting transfers between devices, flipped(): lax.ppermute(block, axis, [(i, i ^ 1 << bit) for i in range(lax.axis_size...  13.8 us
    pallas_call x2, Pallas kernels, renewed(): pl.pallas_call(renew_kernel, grid=(blocks,), in_specs=[pl.BlockSpec(memor...  12.8 us
  transfers between devices with their start and end apart: 49, of which 16 were waited for; matrix products, arithmetic and copies ran while one was open for 15% of the time, Pallas kernels for 19%

profile of v3, /device:TPU:0, one launch (start us, length us, event | category | flops | bytes accessed | tf_op | source)
XLA Modules:
  0.0 350.7 jit_solution(1830079879037258806)
XLA Ops:
  1.4 2.1 pad_maximum_fusion
  3.5 3.3 collective-permute-start.1
  6.8 2.3 shard_map.140
  9.1 2.0 collective-permute-start.38
  11.1 2.2 collective-permute-start.39
  13.3 3.0 shard_map.138
  16.4 3.2 collective-permute-start.35
  21.8 10.1 %collective-permute-done.38.above_in = bf16[256,1536]{1,0:T(8,128)(2,1)} collective-permute-done((bf16[256,1536]{1,0:T(8,128)(2,1)}, bf16[256,1536]{1,0:T(8,128)(2,1)}, u32[]{:S(2)}, u32[]{:S(2)}) %collective-permute-start.38) | collective-permute-done | bytes 786464 | tf_op jit(solution)/shard_map/ppermute | solution.py:25
  36.1 8.0 %fusion.8.queries = bf16[256,1536]{1,0:T(8,128)(2,1)S(1)} fusion(bf16[256,3072]{1,0:T(8,128)(2,1)S(1)} %get-tuple-element.82.slope.slope_up.slope_down, bf16[1,1,3072,1536]{3,2,1,0:T(8,128)(2,1)} %param.14), kind=kOutput, calls=%fused_computation.17 | convolution fusion | flops 2416705536 | bytes 11796480 | tf_op jit(solution)/shard_map/dot_general | solution.py:123
  45.8 8.4 %shard_map.128 = (bf16[256,1536]{1,0:T(8,128)(2,1)S(1)}, f32[256,1536]{1,0:T(8,128)S(1)}, bf16[256,128]{1,0:T(8,128)(2,1)S(1)}) custom-call(bf16[256,1536]{1,0:T(8,128)(2,1)S(1)} %fusion.8.queries, bf16[256,128]{1,0:T(8,128)(2,1)S(1)} %fusion.14.keys, bf16[256,1536]{1,0:T(8,128)(2,1)S(1)} %constant_dynamic-slice_fusion.3.values, ...), custom_call_target="tpu_custom_call" | custom-call | flops 1006632960 | bytes 4718592 | tf_op jit(solution)/shard_map/pallas_call | solution.py:187
  58.2 10.3 %collective-permute-done.23.above_in = bf16[128,768]{1,0:T(8,128)(2,1)S(1)} collective-permute-done((bf16[128,768]{1,0:T(8,128)(2,1)S(1)}, bf16[128,768]{1,0:T(8,128)(2,1)S(1)}, u32[]{:S(2)}, u32[]{:S(2)}) %collective-permute-start.23) | collective-permute-done | bytes 196640 | tf_op jit(solution)/shard_map/ppermute | solution.py:25
  68.6 3.2 collective-permute-start.30
  71.8 5.2 %convolution_multiply_fusion = f32[256,3072]{1,0:T(8,128)S(1)} fusion(bf16[256,1536]{1,0:T(8,128)(2,1)S(1)} %get-tuple-element.61.grad, bf16[1,1,3072,1536]{3,2,1,0:T(8,128)(2,1)} %param.14), kind=kOutput, calls=%fused_computation | convolution fusion | flops 2416705536 | bytes 13369344 | tf_op jit(solution)/shard_map/dot_general | solution.py:591
  77.2 2.6 collective-permute-done.29.above_in
  81.9 3.5 %collective-permute-done.25 = bf16[128,768]{1,0:T(8,128)(2,1)S(1)} collective-permute-done((bf16[128,768]{1,0:T(8,128)(2,1)S(1)}, bf16[128,768]{1,0:T(8,128)(2,1)S(1)}, u32[]{:S(2)}, u32[]{:S(2)}) %collective-permute-start.25) | collective-permute-done | bytes 196640 | tf_op jit(solution)/shard_map/ppermute | solution.py:25
  87.2 9.0 %shard_map.129 = f32[1,1]{1,0:T(1,128)} custom-call(bf16[256,3072]{1,0:T(8,128)(2,1)S(1)} %get-tuple-element.82.slope.slope_up.slope_down, bf16[256,1536]{1,0:T(8,128)(2,1)S(1)} %get-tuple-element.61.grad, bf16[256,128]{1,0:T(8,128)(2,1)S(1)} %add_convert_fusion.2.key_grad), custom_call_target="tpu_custom_call" | custom-call | flops 2617245696 | bytes 2359296 | tf_op jit(solution)/shard_map/pallas_call | solution.py:490
  100.2 3.2 collective-permute-start.41
  104.9 2.5 multiply_reduce_fusion
  109.8 5.2 %all-to-all-start = ((f32[16,1,1]{2,1,0:T(1,128)}), f32[16,1,1]{2,1,0:T(1,128)}, u32[]{:S(2)}, u32[]{:S(2)}) async-start(f32[16,1,1]{2,1,0:T(1,128)} %broadcast_in_dim.35), calls=%async_computation | async-start | bytes 16384 | tf_op jit(solution)/shard_map/all_to_all | solution.py:40
  115.0 5.3 %collective-permute-done = bf16[256,1536]{1,0:T(8,128)(2,1)} collective-permute-done((bf16[256,1536]{1,0:T(8,128)(2,1)S(1)}, bf16[256,1536]{1,0:T(8,128)(2,1)}, u32[]{:S(2)}, u32[]{:S(2)}) %collective-permute-start) | collective-permute-done | bytes 786464 | tf_op jit(solution)/shard_map/ppermute | solution.py:29
  120.4 2.2 collective-permute-start.31
  124.5 2.1 fusion.4
  126.7 3.5 fusion.6
  133.4 2.2 fusion.13
  136.7 3.3 collective-permute-start.5
  140.0 3.4 collective-permute-done.32
  145.3 9.2 %shard_map.134 = (bf16[640,1536]{1,0:T(8,128)(2,1)}, bf16[640,1536]{1,0:T(8,128)(2,1)}) custom-call(f32[1]{0:T(128)} %bitcast.20.scale, bf16[3072,1536]{1,0:T(8,128)(2,1)} %bitcast.2.up.down.weights, bf16[3072,1536]{1,0:T(8,128)(2,1)} %bitcast.2.up.down.weights, bf16[256,3072]{1,0:T(8,128)(2,1)} %copy-done, bf16[256,3072]{1,0:T(8,128)(2,1)} %copy-done, ...), custom_call_target="tpu_custom_call" | custom-call | flops 1006632960 | bytes 7864320 | tf_op jit(solution)/shard_map/pallas_call | solution.py:308
  154.5 2.4 collective-permute-start.43
  159.0 6.3 %fusion.9.queries = bf16[256,1536]{1,0:T(8,128)(2,1)S(1)} fusion(bf16[256,3072]{1,0:T(8,128)(2,1)S(1)} %copy-done.30, bf16[1,1,3072,1536]{3,2,1,0:T(8,128)(2,1)} %param.14), kind=kOutput, calls=%fused_computation.18 | convolution fusion | flops 2416705536 | bytes 11796480 | tf_op jit(solution)/shard_map/dot_general | solution.py:123
  165.3 3.6 %shard_map.132 = (bf16[128,1536]{1,0:T(8,128)(2,1)}, bf16[128,1536]{1,0:T(8,128)(2,1)}) custom-call(f32[1]{0:T(128)} %bitcast.20.scale, bf16[3072,1536]{1,0:T(8,128)(2,1)} %bitcast.2.up.down.weights, bf16[3072,1536]{1,0:T(8,128)(2,1)} %bitcast.2.up.down.weights, bf16[256,3072]{1,0:T(8,128)(2,1)} %copy-done, bf16[256,3072]{1,0:T(8,128)(2,1)} %copy-done, ...), custom_call_target="tpu_custom_call" | custom-call | flops 201326592 | bytes 1572864 | tf_op jit(solution)/shard_map/pallas_call | solution.py:308
  169.0 2.3 collective-permute-start.10
  171.9 3.3 collective-permute-start.16
  175.3 7.3 %shard_map.130 = bf16[256,1536]{1,0:T(8,128)(2,1)S(1)} custom-call(bf16[256,1536]{1,0:T(8,128)(2,1)S(1)} %fusion.9.queries, bf16[256,128]{1,0:T(8,128)(2,1)S(1)} %fusion.15.keys, bf16[256,1536]{1,0:T(8,128)(2,1)S(1)} %constant_dynamic-slice_fusion.2.values, bf16[256,1536]{1,0:T(8,128)(2,1)S(1)} %bitcast.52, s32[256,1]{1,0:T(8,128)S(1)} %copy-done.24, ...), custom_call_target="tpu_custom_call" | custom-call | flops 402653184 | bytes 3145728 | tf_op jit(solution)/shard_map/pallas_call | solution.py:187
  184.3 28.7 %collective-permute-done.9.above_in = bf16[128,1536]{1,0:T(8,128)(2,1)} collective-permute-done((bf16[128,1536]{1,0:T(8,128)(2,1)}, bf16[128,1536]{1,0:T(8,128)(2,1)}, u32[]{:S(2)}, u32[]{:S(2)}) %collective-permute-start.9) | collective-permute-done | bytes 393248 | tf_op jit(solution)/shard_map/ppermute | solution.py:25
  214.7 12.2 %collective-permute-done.45 = bf16[768,128]{1,0:T(8,128)(2,1)S(1)} collective-permute-done((bf16[768,128]{1,0:T(8,128)(2,1)S(1)}, bf16[768,128]{1,0:T(8,128)(2,1)S(1)}, u32[]{:S(2)}, u32[]{:S(2)}) %collective-permute-start.45) | collective-permute-done | bytes 196640 | tf_op jit(solution)/shard_map/ppermute | solution.py:25
  227.2 7.4 %collective-permute-done.46 = bf16[768,128]{1,0:T(8,128)(2,1)S(1)} collective-permute-done((bf16[768,128]{1,0:T(8,128)(2,1)S(1)}, bf16[768,128]{1,0:T(8,128)(2,1)S(1)}, u32[]{:S(2)}, u32[]{:S(2)}) %collective-permute-start.46) | collective-permute-done | bytes 196640 | tf_op jit(solution)/shard_map/ppermute | solution.py:25
  235.2 3.3 collective-permute-start.37
  239.6 2.9 collective-permute-start.6
  243.7 2.1 collective-permute-start.47
  245.8 8.4 %collective-permute-done.47 = bf16[1536,128]{1,0:T(8,128)(2,1)S(1)} collective-permute-done((bf16[1536,128]{1,0:T(8,128)(2,1)S(1)}, bf16[1536,128]{1,0:T(8,128)(2,1)S(1)}, u32[]{:S(2)}, u32[]{:S(2)}) %collective-permute-start.47) | collective-permute-done | bytes 393248 | tf_op jit(solution)/shard_map/ppermute | solution.py:29
  254.2 3.5 %collective-permute-done.6.b_ref = bf16[256,1536]{1,0:T(8,128)(2,1)S(1)} collective-permute-done((bf16[256,1536]{1,0:T(8,128)(2,1)S(1)}, bf16[256,1536]{1,0:T(8,128)(2,1)S(1)}, u32[]{:S(2)}, u32[]{:S(2)}) %collective-permute-start.6) | collective-permute-done | bytes 786464 | tf_op jit(solution)/shard_map/ppermute | solution.py:25
  257.7 13.3 %collective-permute-done.36.rest_4_ = bf16[512,1536]{1,0:T(8,128)(2,1)S(1)} collective-permute-done((bf16[512,1536]{1,0:T(8,128)(2,1)}, bf16[512,1536]{1,0:T(8,128)(2,1)S(1)}, u32[]{:S(2)}, u32[]{:S(2)}) %collective-permute-start.36) | collective-permute-done | bytes 1572896 | tf_op jit(solution)/shard_map/ppermute | solution.py:25
  272.2 3.2 collective-permute-start.18
  279.4 36.6 %collective-permute-done.17.refs_6_ = bf16[640,1536]{1,0:T(8,128)(2,1)S(1)} collective-permute-done((bf16[640,1536]{1,0:T(8,128)(2,1)S(1)}, bf16[640,1536]{1,0:T(8,128)(2,1)S(1)}, u32[]{:S(2)}, u32[]{:S(2)}) %collective-permute-start.17) | collective-permute-done | bytes 1966112 | tf_op jit(solution)/shard_map/ppermute | solution.py:25
  317.3 3.2 collective-permute-start.12
  324.6 6.8 %shard_map.142.rest_6_ = bf16[3072,1536]{1,0:T(8,128)(2,1)} custom-call(s32[1]{0:T(128)} %bitcast.19.case_ref, f32[2]{0:T(128)S(1)} %pad_maximum_fusion.4.scales, bf16[3072,1536]{1,0:T(8,128)(2,1)} %bitcast.2.up.down.weights, bf16[256,3072]{1,0:T(8,128)(2,1)S(1)} %copy-done.1, bf16[256,1536]{1,0:T(8,128)(2,1)S(1)} %maximum_select_fusion.2.slope_other, ...), custom_call_target="tpu_custom_call" | custom-call | flops 3145728 | bytes 4718592 | tf_op jit(solution)/shard_map/pallas_call | solution.py:406
  332.8 9.6 %shard_map.143.refs_8_ = bf16[3072,1536]{1,0:T(8,128)(2,1)} custom-call(s32[1]{0:T(128)} %bitcast.19.case_ref, f32[2]{0:T(128)S(1)} %pad_maximum_fusion.4.scales, bf16[3072,1536]{1,0:T(8,128)(2,1)} %bitcast.2.up.down.weights, bf16[256,3072]{1,0:T(8,128)(2,1)S(1)} %copy-done.1, ...), custom_call_target="tpu_custom_call", output_to_operand_aliasing={{}: (13, {})} | custom-call | flops 6291456 | bytes 9437184 | tf_op jit(solution)/shard_map/pallas_call | solution.py:406
  343.9 4.7 %shard_map.144.refs_8_ = bf16[3072,1536]{1,0:T(8,128)(2,1)} custom-call(s32[1]{0:T(128)} %bitcast.19.case_ref, bf16[640,1536]{1,0:T(8,128)(2,1)S(1)} %copy-done.5, bf16[640,1536]{1,0:T(8,128)(2,1)S(1)} %copy-done.6, bf16[640,1536]{1,0:T(8,128)(2,1)S(1)} %collective-permute-done.13.refs_2_, ...), custom_call_target="tpu_custom_call", output_to_operand_aliasing={{}: (9, {})} | custom-call | flops 3932160 | bytes 11796480 | tf_op jit(solution)/shard_map/pallas_call | solution.py:442
  (233 shorter events, 54.2 us)
Async XLA Ops:
  3.5 28.5 %collective-permute-start.1 = (bf16[272,1536]{1,0:T(8,128)(2,1)}, bf16[272,1536]{1,0:T(8,128)(2,1)}, u32[]{:S(2)}, u32[]{:S(2)}) collective-permute-start(bf16[272,1536]{1,0:T(8,128)(2,1)} %pad_maximum_fusion), channel_id=1, source_target_pairs={{0,1},{1,0},{2,3},{3,2},{4,5},{5,4},{6,7},{7,6},{8,9},{9,8},{10,11... | collective-permute-start | bytes 2506760 | tf_op jit(solution)/shard_map/ppermute | solution.py:29
  9.1 22.8 %collective-permute-start.38 = (bf16[256,1536]{1,0:T(8,128)(2,1)}, bf16[256,1536]{1,0:T(8,128)(2,1)}, u32[]{:S(2)}, u32[]{:S(2)}) collective-permute-start(bf16[256,1536]{1,0:T(8,128)(2,1)} %get-tuple-element.70.up), channel_id=1, source_target_pairs={{0,32},{16,48},{32,64},{48,80},{64,96},{80,112},{96,0},{112,16},{1... | collective-permute-start | bytes 2359304 | tf_op jit(solution)/shard_map/ppermute | solution.py:25
  11.1 20.8 %collective-permute-start.39 = (bf16[256,1536]{1,0:T(8,128)(2,1)}, bf16[256,1536]{1,0:T(8,128)(2,1)}, u32[]{:S(2)}, u32[]{:S(2)}) collective-permute-start(bf16[256,1536]{1,0:T(8,128)(2,1)} %get-tuple-element.71.down), channel_id=1, source_target_pairs={{0,96},{16,112},{32,0},{48,16},{64,32},{80,48},{96,64},{112,80},{1... | collective-permute-start | bytes 2359304 | tf_op jit(solution)/shard_map/ppermute | solution.py:25
  16.3 83.9 %collective-permute-start.34 = (bf16[512,1536]{1,0:T(8,128)(2,1)}, bf16[512,1536]{1,0:T(8,128)(2,1)}, u32[]{:S(2)}, u32[]{:S(2)}) collective-permute-start(bf16[512,1536]{1,0:T(8,128)(2,1)} %get-tuple-element.66.up), channel_id=1, source_target_pairs={{0,32},{16,48},{32,64},{48,80},{64,96},{80,112},{96,0},{112,16},{1... | collective-permute-start | bytes 4718600 | tf_op jit(solution)/shard_map/ppermute | solution.py:25
  16.4 83.8 %collective-permute-start.35 = (bf16[512,1536]{1,0:T(8,128)(2,1)}, bf16[512,1536]{1,0:T(8,128)(2,1)}, u32[]{:S(2)}, u32[]{:S(2)}) collective-permute-start(bf16[512,1536]{1,0:T(8,128)(2,1)} %get-tuple-element.67.down), channel_id=1, source_target_pairs={{0,96},{16,112},{32,0},{48,16},{64,32},{80,48},{96,64},{112,80},{1... | collective-permute-start | bytes 4718600 | tf_op jit(solution)/shard_map/ppermute | solution.py:25
  54.2 22.8 %collective-permute-start.2 = (bf16[256,128]{1,0:T(8,128)(2,1)S(1)}, bf16[256,128]{1,0:T(8,128)(2,1)S(1)}, u32[]{:S(2)}, u32[]{:S(2)}) collective-permute-start(bf16[256,128]{1,0:T(8,128)(2,1)S(1)} %get-tuple-element.43), channel_id=1, source_target_pairs={{0,1},{1,0},{2,3},{3,2},{4,5},{5,4},{6,7},{7,6},{8,9},{9,8},{10,11... | collective-permute-start | bytes 196616 | tf_op jit(solution)/shard_map/ppermute | solution.py:29
  54.7 13.9 %collective-permute-start.23 = (bf16[128,768]{1,0:T(8,128)(2,1)S(1)}, bf16[128,768]{1,0:T(8,128)(2,1)S(1)}, u32[]{:S(2)}, u32[]{:S(2)}) collective-permute-start(bf16[128,768]{1,0:T(8,128)(2,1)S(1)} %get-tuple-element.57.up), channel_id=1, source_target_pairs={{0,32},{16,48},{32,64},{48,80},{64,96},{80,112},{96,0},{112,16},{1... | collective-permute-start | bytes 589832 | tf_op jit(solution)/shard_map/ppermute | solution.py:25
  56.6 11.9 %collective-permute-start.24 = (bf16[128,768]{1,0:T(8,128)(2,1)S(1)}, bf16[128,768]{1,0:T(8,128)(2,1)S(1)}, u32[]{:S(2)}, u32[]{:S(2)}) collective-permute-start(bf16[128,768]{1,0:T(8,128)(2,1)S(1)} %get-tuple-element.58.down), channel_id=1, source_target_pairs={{0,96},{16,112},{32,0},{48,16},{64,32},{80,48},{96,64},{112,80},{1... | collective-permute-start | bytes 589832 | tf_op jit(solution)/shard_map/ppermute | solution.py:25
  68.6 11.2 %collective-permute-start.29 = (bf16[128,1536]{1,0:T(8,128)(2,1)S(1)}, bf16[128,1536]{1,0:T(8,128)(2,1)S(1)}, u32[]{:S(2)}, u32[]{:S(2)}) collective-permute-start(bf16[128,1536]{1,0:T(8,128)(2,1)S(1)} %get-tuple-element.62.up), channel_id=1, source_target_pairs={{0,32},{16,48},{32,64},{48,80},{64,96},{80,112},{96,0},{112,16},{1... | collective-permute-start | bytes 1179656 | tf_op jit(solution)/shard_map/ppermute | solution.py:25
  68.6 11.5 %collective-permute-start.30 = (bf16[128,1536]{1,0:T(8,128)(2,1)S(1)}, bf16[128,1536]{1,0:T(8,128)(2,1)S(1)}, u32[]{:S(2)}, u32[]{:S(2)}) collective-permute-start(bf16[128,1536]{1,0:T(8,128)(2,1)S(1)} %get-tuple-element.63.down), channel_id=1, source_target_pairs={{0,96},{16,112},{32,0},{48,16},{64,32},{80,48},{96,64},{112,80},{1... | collective-permute-start | bytes 1179656 | tf_op jit(solution)/shard_map/ppermute | solution.py:25
  77.1 240.2 %collective-permute-start.33 = (bf16[3072,1536]{1,0:T(8,128)(2,1)}, bf16[3072,1536]{1,0:T(8,128)(2,1)}, u32[]{:S(2)}, u32[]{:S(2)}) collective-permute-start(bf16[3072,1536]{1,0:T(8,128)(2,1)} %bitcast.2.up.down.weights), channel_id=1, source_target_pairs={{0,16},{16,0},{32,48},{48,32},{64,80},{80,64},{96,112},{112,96},{1... | collective-permute-start | bytes 28311560 | tf_op jit(solution)/shard_map/ppermute | solution.py:29
  80.1 7.0 %collective-permute-start.26 = (bf16[128,768]{1,0:T(8,128)(2,1)S(1)}, bf16[128,768]{1,0:T(8,128)(2,1)S(1)}, u32[]{:S(2)}, u32[]{:S(2)}) collective-permute-start(bf16[128,768]{1,0:T(8,128)(2,1)S(1)} %get-tuple-element.60), channel_id=1, source_target_pairs={{0,32},{16,48},{32,64},{48,80},{64,96},{80,112},{96,0},{112,16},{1... | collective-permute-start | bytes 589832 | tf_op jit(solution)/shard_map/ppermute | solution.py:25
  85.5 19.4 %collective-permute-start.3 = (bf16[256,1536]{1,0:T(8,128)(2,1)S(1)}, bf16[256,1536]{1,0:T(8,128)(2,1)S(1)}, u32[]{:S(2)}, u32[]{:S(2)}) collective-permute-start(bf16[256,1536]{1,0:T(8,128)(2,1)S(1)} %dynamic-slice_convert_fusion), channel_id=1, source_target_pairs={{0,1},{1,0},{2,3},{3,2},{4,5},{5,4},{6,7},{7,6},{8,9},{9,8},{10,11... | collective-permute-start | bytes 2359304 | tf_op jit(solution)/shard_map/ppermute | solution.py:29
  87.1 9.8 %collective-permute-start.22 = (bf16[256,768]{1,0:T(8,128)(2,1)S(1)}, bf16[256,768]{1,0:T(8,128)(2,1)S(1)}, u32[]{:S(2)}, u32[]{:S(2)}) collective-permute-start(bf16[256,768]{1,0:T(8,128)(2,1)S(1)} %constant_dynamic-slice_fusion), channel_id=1, source_target_pairs={{0,16},{16,0},{32,48},{48,32},{64,80},{80,64},{96,112},{112,96},{1... | collective-permute-start | bytes 1179656 | tf_op jit(solution)/shard_map/ppermute | solution.py:29
  97.3 23.0 %collective-permute-start = (bf16[256,1536]{1,0:T(8,128)(2,1)S(1)}, bf16[256,1536]{1,0:T(8,128)(2,1)}, u32[]{:S(2)}, u32[]{:S(2)}) collective-permute-start(bf16[256,1536]{1,0:T(8,128)(2,1)S(1)} %bitcast.48), channel_id=1, source_target_pairs={{0,1},{1,0},{2,3},{3,2},{4,5},{5,4},{6,7},{7,6},{8,9},{9,8},{10,11... | collective-permute-start | bytes 2359304 | tf_op jit(solution)/shard_map/ppermute | solution.py:29
  100.1 32.8 %collective-permute-start.40 = (bf16[256,1536]{1,0:T(8,128)(2,1)}, bf16[256,1536]{1,0:T(8,128)(2,1)}, u32[]{:S(2)}, u32[]{:S(2)}) collective-permute-start(bf16[256,1536]{1,0:T(8,128)(2,1)} %get-tuple-element.72.rest_2_), channel_id=1, source_target_pairs={{0,32},{16,48},{32,64},{48,80},{64,96},{80,112},{96,0},{112,16},{1... | collective-permute-start | bytes 2359304 | tf_op jit(solution)/shard_map/ppermute | solution.py:25
  100.2 32.8 %collective-permute-start.41 = (bf16[256,1536]{1,0:T(8,128)(2,1)}, bf16[256,1536]{1,0:T(8,128)(2,1)}, u32[]{:S(2)}, u32[]{:S(2)}) collective-permute-start(bf16[256,1536]{1,0:T(8,128)(2,1)} %get-tuple-element.73.rest_3_), channel_id=1, source_target_pairs={{0,96},{16,112},{32,0},{48,16},{64,32},{80,48},{96,64},{112,80},{1... | collective-permute-start | bytes 2359304 | tf_op jit(solution)/shard_map/ppermute | solution.py:25
  104.8 38.5 %collective-permute-start.28 = (bf16[256,1536]{1,0:T(8,128)(2,1)S(1)}, bf16[256,1536]{1,0:T(8,128)(2,1)}, u32[]{:S(2)}, u32[]{:S(2)}) collective-permute-start(bf16[256,1536]{1,0:T(8,128)(2,1)S(1)} %get-tuple-element.61.grad), channel_id=1, source_target_pairs={{0,16},{16,0},{32,48},{48,32},{64,80},{80,64},{96,112},{112,96},{1... | collective-permute-start | bytes 2359304 | tf_op jit(solution)/shard_map/ppermute | solution.py:29
  109.8 20.4 %all-to-all-start = ((f32[16,1,1]{2,1,0:T(1,128)}), f32[16,1,1]{2,1,0:T(1,128)}, u32[]{:S(2)}, u32[]{:S(2)}) async-start(f32[16,1,1]{2,1,0:T(1,128)} %broadcast_in_dim.35), calls=%async_computation | async-start | bytes 16384 | tf_op jit(solution)/shard_map/all_to_all | solution.py:40
  120.4 16.3 %collective-permute-start.31 = (bf16[128,1536]{1,0:T(8,128)(2,1)}, bf16[128,1536]{1,0:T(8,128)(2,1)}, u32[]{:S(2)}, u32[]{:S(2)}) collective-permute-start(bf16[128,1536]{1,0:T(8,128)(2,1)} %copy-done.9), channel_id=1, source_target_pairs={{0,96},{16,112},{32,0},{48,16},{64,32},{80,48},{96,64},{112,80},{1... | collective-permute-start | bytes 1179656 | tf_op jit(solution)/shard_map/ppermute | solution.py:25
  132.9 10.4 %collective-permute-start.32 = (bf16[128,1536]{1,0:T(8,128)(2,1)S(1)}, bf16[128,1536]{1,0:T(8,128)(2,1)S(1)}, u32[]{:S(2)}, u32[]{:S(2)}) collective-permute-start(bf16[128,1536]{1,0:T(8,128)(2,1)S(1)} %get-tuple-element.65), channel_id=1, source_target_pairs={{0,32},{16,48},{32,64},{48,80},{64,96},{80,112},{96,0},{112,16},{1... | collective-permute-start | bytes 1179656 | tf_op jit(solution)/shard_map/ppermute | solution.py:25
  133.0 11.0 %collective-permute-start.27 = (bf16[256,768]{1,0:T(8,128)(2,1)}, bf16[256,768]{1,0:T(8,128)(2,1)S(1)}, u32[]{:S(2)}, u32[]{:S(2)}) collective-permute-start(bf16[256,768]{1,0:T(8,128)(2,1)} %pad_maximum_fusion.2), channel_id=1, source_target_pairs={{0,1},{1,0},{2,3},{3,2},{4,5},{5,4},{6,7},{7,6},{8,9},{9,8},{10,11... | collective-permute-start | bytes 1179656 | tf_op jit(solution)/shard_map/ppermute | solution.py:29
  136.7 17.8 %collective-permute-start.5 = (f32[2,256]{1,0:T(2,128)S(1)}, f32[2,256]{1,0:T(2,128)S(1)}, u32[]{:S(2)}, u32[]{:S(2)}) collective-permute-start(f32[2,256]{1,0:T(2,128)S(1)} %pad_maximum_fusion.3), channel_id=1, source_target_pairs={{0,1},{1,0},{2,3},{3,2},{4,5},{5,4},{6,7},{7,6},{8,9},{9,8},{10,11... | collective-permute-start | bytes 6152 | tf_op jit(solution)/shard_map/ppermute | solution.py:29
  143.3 13.6 %collective-permute-start.19 = (f32[1664]{0:T(1024)S(1)}, f32[1664]{0:T(1024)S(1)}, u32[]{:S(2)}, u32[]{:S(2)}) collective-permute-start(f32[1664]{0:T(1024)S(1)} %concatenate.81), channel_id=1, source_target_pairs={{0,16},{16,0},{32,48},{48,32},{64,80},{80,64},{96,112},{112,96},{1... | collective-permute-start | bytes 19976 | tf_op jit(solution)/shard_map/ppermute | solution.py:29
  143.3 14.5 %collective-permute-start.20 = (f32[1664]{0:T(1024)S(1)}, f32[1664]{0:T(1024)S(1)}, u32[]{:S(2)}, u32[]{:S(2)}) collective-permute-start(f32[1664]{0:T(1024)S(1)} %concatenate.81), channel_id=1, source_target_pairs={{0,32},{16,48},{32,0},{48,16},{64,96},{80,112},{96,64},{112,80},{1... | collective-permute-start | bytes 19976 | tf_op jit(solution)/shard_map/ppermute | solution.py:29
  144.0 13.9 %collective-permute-start.21 = (f32[1664]{0:T(1024)S(1)}, f32[1664]{0:T(1024)S(1)}, u32[]{:S(2)}, u32[]{:S(2)}) collective-permute-start(f32[1664]{0:T(1024)S(1)} %concatenate.81), channel_id=1, source_target_pairs={{0,64},{16,80},{32,96},{48,112},{64,0},{80,16},{96,32},{112,48},{1... | collective-permute-start | bytes 19976 | tf_op jit(solution)/shard_map/ppermute | solution.py:29
  154.5 14.5 %collective-permute-start.43 = (bf16[768,128]{1,0:T(8,128)(2,1)S(1)}, bf16[768,128]{1,0:T(8,128)(2,1)S(1)}, u32[]{:S(2)}, u32[]{:S(2)}) collective-permute-start(bf16[768,128]{1,0:T(8,128)(2,1)S(1)} %get-tuple-element.75.up), channel_id=1, source_target_pairs={{0,32},{16,48},{32,64},{48,80},{64,96},{80,112},{96,0},{112,16},{1... | collective-permute-start | bytes 589832 | tf_op jit(solution)/shard_map/ppermute | solution.py:25
  156.9 14.4 %collective-permute-start.44 = (bf16[768,128]{1,0:T(8,128)(2,1)S(1)}, bf16[768,128]{1,0:T(8,128)(2,1)S(1)}, u32[]{:S(2)}, u32[]{:S(2)}) collective-permute-start(bf16[768,128]{1,0:T(8,128)(2,1)S(1)} %get-tuple-element.76.down), channel_id=1, source_target_pairs={{0,96},{16,112},{32,0},{48,16},{64,32},{80,48},{96,64},{112,80},{1... | collective-permute-start | bytes 589832 | tf_op jit(solution)/shard_map/ppermute | solution.py:25
  157.8 14.1 %collective-permute-start.42 = (bf16[1536,128]{1,0:T(8,128)(2,1)}, bf16[1536,128]{1,0:T(8,128)(2,1)}, u32[]{:S(2)}, u32[]{:S(2)}) collective-permute-start(bf16[1536,128]{1,0:T(8,128)(2,1)} %fusion.13), channel_id=1, source_target_pairs={{0,16},{16,0},{32,48},{48,32},{64,80},{80,64},{96,112},{112,96},{1... | collective-permute-start | bytes 1179656 | tf_op jit(solution)/shard_map/ppermute | solution.py:29
  157.8 81.8 %collective-permute-start.15 = (bf16[640,1536]{1,0:T(8,128)(2,1)}, bf16[640,1536]{1,0:T(8,128)(2,1)S(1)}, u32[]{:S(2)}, u32[]{:S(2)}) collective-permute-start(bf16[640,1536]{1,0:T(8,128)(2,1)} %get-tuple-element.52.up.refs_0_), channel_id=1, source_target_pairs={{0,32},{16,48},{32,64},{48,80},{64,96},{80,112},{96,0},{112,16},{1... | collective-permute-start | bytes 5898248 | tf_op jit(solution)/shard_map/ppermute | solution.py:25
  169.0 13.7 %collective-permute-start.10 = (bf16[128,1536]{1,0:T(8,128)(2,1)}, bf16[128,1536]{1,0:T(8,128)(2,1)S(1)}, u32[]{:S(2)}, u32[]{:S(2)}) collective-permute-start(bf16[128,1536]{1,0:T(8,128)(2,1)} %get-tuple-element.49.down.refs_1_), channel_id=1, source_target_pairs={{0,96},{16,112},{32,0},{48,16},{64,32},{80,48},{96,64},{112,80},{1... | collective-permute-start | bytes 1179656 | tf_op jit(solution)/shard_map/ppermute | solution.py:25
  171.3 41.7 %collective-permute-start.9 = (bf16[128,1536]{1,0:T(8,128)(2,1)}, bf16[128,1536]{1,0:T(8,128)(2,1)}, u32[]{:S(2)}, u32[]{:S(2)}) collective-permute-start(bf16[128,1536]{1,0:T(8,128)(2,1)} %get-tuple-element.48.up.refs_0_), channel_id=1, source_target_pairs={{0,32},{16,48},{32,64},{48,80},{64,96},{80,112},{96,0},{112,16},{1... | collective-permute-start | bytes 1179656 | tf_op jit(solution)/shard_map/ppermute | solution.py:25
  171.9 71.8 %collective-permute-start.16 = (bf16[640,1536]{1,0:T(8,128)(2,1)S(1)}, bf16[640,1536]{1,0:T(8,128)(2,1)S(1)}, u32[]{:S(2)}, u32[]{:S(2)}) collective-permute-start(bf16[640,1536]{1,0:T(8,128)(2,1)S(1)} %copy-done.6), channel_id=1, source_target_pairs={{0,96},{16,112},{32,0},{48,16},{64,32},{80,48},{96,64},{112,80},{1... | collective-permute-start | bytes 5898248 | tf_op jit(solution)/shard_map/ppermute | solution.py:25
  182.7 52.5 %collective-permute-start.4 = (bf16[256,1536]{1,0:T(8,128)(2,1)S(1)}, bf16[256,1536]{1,0:T(8,128)(2,1)S(1)}, u32[]{:S(2)}, u32[]{:S(2)}) collective-permute-start(bf16[256,1536]{1,0:T(8,128)(2,1)S(1)} %shard_map.130), channel_id=1, source_target_pairs={{0,2},{2,4},{4,6},{6,8},{8,10},{10,12},{12,14},{14,0},{1,3},{3,5},... | collective-permute-start | bytes 2359304 | tf_op jit(solution)/shard_map/ppermute | solution.py:25
  213.0 13.9 %collective-permute-start.45 = (bf16[768,128]{1,0:T(8,128)(2,1)S(1)}, bf16[768,128]{1,0:T(8,128)(2,1)S(1)}, u32[]{:S(2)}, u32[]{:S(2)}) collective-permute-start(bf16[768,128]{1,0:T(8,128)(2,1)S(1)} %get-tuple-element.77), channel_id=1, source_target_pairs={{0,96},{16,112},{32,0},{48,16},{64,32},{80,48},{96,64},{112,80},{1... | collective-permute-start | bytes 589832 | tf_op jit(solution)/shard_map/ppermute | solution.py:25
  227.0 7.7 %collective-permute-start.46 = (bf16[768,128]{1,0:T(8,128)(2,1)S(1)}, bf16[768,128]{1,0:T(8,128)(2,1)S(1)}, u32[]{:S(2)}, u32[]{:S(2)}) collective-permute-start(bf16[768,128]{1,0:T(8,128)(2,1)S(1)} %get-tuple-element.78), channel_id=1, source_target_pairs={{0,32},{16,48},{32,64},{48,80},{64,96},{80,112},{96,0},{112,16},{1... | collective-permute-start | bytes 589832 | tf_op jit(solution)/shard_map/ppermute | solution.py:25
  234.6 36.4 %collective-permute-start.36 = (bf16[512,1536]{1,0:T(8,128)(2,1)}, bf16[512,1536]{1,0:T(8,128)(2,1)S(1)}, u32[]{:S(2)}, u32[]{:S(2)}) collective-permute-start(bf16[512,1536]{1,0:T(8,128)(2,1)} %get-tuple-element.68.rest_2_), channel_id=1, source_target_pairs={{0,32},{16,48},{32,64},{48,80},{64,96},{80,112},{96,0},{112,16},{1... | collective-permute-start | bytes 4718600 | tf_op jit(solution)/shard_map/ppermute | solution.py:25
  235.2 37.0 %collective-permute-start.37 = (bf16[512,1536]{1,0:T(8,128)(2,1)}, bf16[512,1536]{1,0:T(8,128)(2,1)S(1)}, u32[]{:S(2)}, u32[]{:S(2)}) collective-permute-start(bf16[512,1536]{1,0:T(8,128)(2,1)} %get-tuple-element.69.rest_3_), channel_id=1, source_target_pairs={{0,96},{16,112},{32,0},{48,16},{64,32},{80,48},{96,64},{112,80},{1... | collective-permute-start | bytes 4718600 | tf_op jit(solution)/shard_map/ppermute | solution.py:25
  239.6 18.1 %collective-permute-start.6 = (bf16[256,1536]{1,0:T(8,128)(2,1)S(1)}, bf16[256,1536]{1,0:T(8,128)(2,1)S(1)}, u32[]{:S(2)}, u32[]{:S(2)}) collective-permute-start(bf16[256,1536]{1,0:T(8,128)(2,1)S(1)} %add_convert_fusion), channel_id=1, source_target_pairs={{0,14},{2,0},{4,2},{6,4},{8,6},{10,8},{12,10},{14,12},{1,15},{3,1}... | collective-permute-start | bytes 2359304 | tf_op jit(solution)/shard_map/ppermute | solution.py:25
  243.7 10.5 %collective-permute-start.47 = (bf16[1536,128]{1,0:T(8,128)(2,1)S(1)}, bf16[1536,128]{1,0:T(8,128)(2,1)S(1)}, u32[]{:S(2)}, u32[]{:S(2)}) collective-permute-start(bf16[1536,128]{1,0:T(8,128)(2,1)S(1)} %multiply_convert_fusion.1), channel_id=1, source_target_pairs={{0,1},{1,0},{2,3},{3,2},{4,5},{5,4},{6,7},{7,6},{8,9},{9,8},{10,11... | collective-permute-start | bytes 1179656 | tf_op jit(solution)/shard_map/ppermute | solution.py:29
  254.2 24.6 %collective-permute-start.13 = (bf16[640,1536]{1,0:T(8,128)(2,1)S(1)}, bf16[640,1536]{1,0:T(8,128)(2,1)S(1)}, u32[]{:S(2)}, u32[]{:S(2)}) collective-permute-start(bf16[640,1536]{1,0:T(8,128)(2,1)S(1)} %copy-done.5), channel_id=1, source_target_pairs={{0,16},{16,0},{32,48},{48,32},{64,80},{80,64},{96,112},{112,96},{1... | collective-permute-start | bytes 5898248 | tf_op jit(solution)/shard_map/ppermute | solution.py:29
  257.7 21.2 %collective-permute-start.14 = (bf16[640,1536]{1,0:T(8,128)(2,1)S(1)}, bf16[640,1536]{1,0:T(8,128)(2,1)S(1)}, u32[]{:S(2)}, u32[]{:S(2)}) collective-permute-start(bf16[640,1536]{1,0:T(8,128)(2,1)S(1)} %copy-done.6), channel_id=1, source_target_pairs={{0,16},{16,0},{32,48},{48,32},{64,80},{80,64},{96,112},{112,96},{1... | collective-permute-start | bytes 5898248 | tf_op jit(solution)/shard_map/ppermute | solution.py:29
  272.2 43.8 %collective-permute-start.17 = (bf16[640,1536]{1,0:T(8,128)(2,1)S(1)}, bf16[640,1536]{1,0:T(8,128)(2,1)S(1)}, u32[]{:S(2)}, u32[]{:S(2)}) collective-permute-start(bf16[640,1536]{1,0:T(8,128)(2,1)S(1)} %get-tuple-element.54.refs_4_), channel_id=1, source_target_pairs={{0,32},{16,48},{32,64},{48,80},{64,96},{80,112},{96,0},{112,16},{1... | collective-permute-start | bytes 5898248 | tf_op jit(solution)/shard_map/ppermute | solution.py:25
  272.2 70.2 %collective-permute-start.18 = (bf16[640,1536]{1,0:T(8,128)(2,1)S(1)}, bf16[640,1536]{1,0:T(8,128)(2,1)}, u32[]{:S(2)}, u32[]{:S(2)}) collective-permute-start(bf16[640,1536]{1,0:T(8,128)(2,1)S(1)} %get-tuple-element.55.refs_5_), channel_id=1, source_target_pairs={{0,96},{16,112},{32,0},{48,16},{64,32},{80,48},{96,64},{112,80},{1... | collective-permute-start | bytes 5898248 | tf_op jit(solution)/shard_map/ppermute | solution.py:25
  278.8 69.9 %collective-permute-start.7 = (bf16[128,1536]{1,0:T(8,128)(2,1)S(1)}, bf16[128,1536]{1,0:T(8,128)(2,1)S(1)}, u32[]{:S(2)}, u32[]{:S(2)}) collective-permute-start(bf16[128,1536]{1,0:T(8,128)(2,1)S(1)} %copy-done.13), channel_id=1, source_target_pairs={{0,16},{16,0},{32,48},{48,32},{64,80},{80,64},{96,112},{112,96},{1... | collective-permute-start | bytes 1179656 | tf_op jit(solution)/shard_map/ppermute | solution.py:29
  278.9 69.8 %collective-permute-start.8 = (bf16[128,1536]{1,0:T(8,128)(2,1)S(1)}, bf16[128,1536]{1,0:T(8,128)(2,1)S(1)}, u32[]{:S(2)}, u32[]{:S(2)}) collective-permute-start(bf16[128,1536]{1,0:T(8,128)(2,1)S(1)} %copy-done.14), channel_id=1, source_target_pairs={{0,16},{16,0},{32,48},{48,32},{64,80},{80,64},{96,112},{112,96},{1... | collective-permute-start | bytes 1179656 | tf_op jit(solution)/shard_map/ppermute | solution.py:29
  317.3 31.4 %collective-permute-start.11 = (bf16[128,1536]{1,0:T(8,128)(2,1)}, bf16[128,1536]{1,0:T(8,128)(2,1)S(1)}, u32[]{:S(2)}, u32[]{:S(2)}) collective-permute-start(bf16[128,1536]{1,0:T(8,128)(2,1)} %get-tuple-element.50.refs_4_), channel_id=1, source_target_pairs={{0,32},{16,48},{32,64},{48,80},{64,96},{80,112},{96,0},{112,16},{1... | collective-permute-start | bytes 1179656 | tf_op jit(solution)/shard_map/ppermute | solution.py:25
  317.3 31.4 %collective-permute-start.12 = (bf16[128,1536]{1,0:T(8,128)(2,1)S(1)}, bf16[128,1536]{1,0:T(8,128)(2,1)S(1)}, u32[]{:S(2)}, u32[]{:S(2)}) collective-permute-start(bf16[128,1536]{1,0:T(8,128)(2,1)S(1)} %get-tuple-element.51.refs_5_), channel_id=1, source_target_pairs={{0,96},{16,112},{32,0},{48,16},{64,32},{80,48},{96,64},{112,80},{1... | collective-permute-start | bytes 1179656 | tf_op jit(solution)/shard_map/ppermute | solution.py:25
  (55 other events, 900.8 us)
